TPU v7x, 32 devices: a whole 2x2x4 slice. The times are simulated.
32 devices in a mesh: lat: 2 (over y), lon: 16 (over z, x, core).
Axes of the slice: x: 2, y: 2, z: 4, core: 2. Of those that a mesh axis runs over, the one named last changes fastest.
Arguments:
- sea_level: float32 [2048, 256], P('lon', 'lat'), may hold values from -1 to 5
- east_velocity: float32 [2048, 256], P('lon', 'lat'), may hold values from -6 to 6
- north_velocity: float32 [2048, 256], P('lon', 'lat'), may hold values from -6 to 6
- depth: float32 [2048, 256], P('lon', 'lat'), may hold values from 0.25 to 1
- land_mask: int32 [2048, 256], P('lon', 'lat'), may hold values from 0 to 1, as said below
- wet_counts: int32 [2, 16], replicated, may hold values from 1 to 16384, as said below
- loading_prev: float32 [2048, 256], P('lon', 'lat'), may hold values from -4 to 4
- tide_amp: float32 [8], replicated, may hold values from 0.3 to 1
- tide_phase: float32 [8], replicated, may hold values from -3.140625 to 3.140625
- legendre: bfloat16 [512, 1024, 256], P('lon', None, 'lat'), may hold values from -0.375 to 0.375
- love_factor: float32 [1024], replicated, may hold values from 0.05 to 1
Outputs:
- height_new: float32 [2048, 256], P('lon', 'lat')
- east_new: float32 [2048, 256], P('lon', 'lat')
- north_new: float32 [2048, 256], P('lon', 'lat')
- self_attraction: float32 [2048, 256], P('lon', 'lat')
Inputs may be any that keep to these rules, and one draw needn't show every extreme that they name: `land_mask`: every tile of 128 columns by 128 rows holds at least one wet column, and one tile is wholly wet. wet_counts[p, q] is the number of wet columns of land_mask in latitude band p and longitude band q.
All inputs are finite; a program needn't handle non-finite values.
Results may differ from a plain program's by a relative error of at most 0.0038.
Values may be sent and summed in bfloat16 or wider, within the bound.
No kernel may reach another device: no remote copies, remote signals or barrier semaphores. Data moves between devices by JAX's collectives and lax.ppermute only.
A program may use at most 64 MiB of HBM per device.

v0:
```python
import functools
import math

import jax
import jax.numpy as jnp
from jax import lax
from jax.experimental import pallas as pl
from jax.experimental.pallas import tpu as pltpu
from jax.sharding import PartitionSpec as P


SUBSTEPS = 4
MARGIN = 2 * SUBSTEPS

lat_edge = 1.3089969
courant = 0.4
friction = 0.02
rotation = 0.2
frequencies = (0.1405, 0.1454, 0.1379, 0.1458, 0.0729, 0.0676, 0.0725, 0.0649)
diurnal_from = 4

f32 = jnp.float32
bf16 = jnp.bfloat16
LANES = 128


def split_bf16(x):
    high = x.astype(bf16)
    return high, (x - high.astype(f32)).astype(bf16)


def call(kernel, out_shape, in_specs=None, scratch=(), vmem=None):
    params = pltpu.CompilerParams(vmem_limit_bytes=(vmem or 16) << 20)
    kwargs = {} if in_specs is None else {"in_specs": in_specs}
    return pl.pallas_call(
        kernel, out_shape=out_shape, scratch_shapes=scratch, compiler_params=params, **kwargs
    )


def shaped(*dims, dtype=f32):
    return jax.ShapeDtypeStruct(dims, dtype)


def fetch(source, first, target, sems):
    pieces = sems.shape[0]
    span = target.shape[0] // pieces
    copies = []
    for piece in range(pieces):
        taken = source.at[pl.ds(first + piece * span, span)]
        placed = target.at[pl.ds(piece * span, span)]
        copies.append(pltpu.make_async_copy(taken, placed, sems.at[piece]))
    return copies


def pack_kernel(sea, east, north, depth, mask, loading, own, near, away, *rest):
    strips = rest[:-3]
    wet, sems, wet_sem = rest[-3:]
    copies = [pltpu.make_async_copy(mask, wet, wet_sem)]
    for index, ref in ((0, sea), (1, east), (2, north), (3, depth), (5, loading)):
        copies.append(pltpu.make_async_copy(ref, own.at[index], sems.at[index]))
    for copy in copies:
        copy.start()
    odd = (lax.axis_index("lon") & 1) > 0
    lat_index = lax.axis_index("lat")
    rows, lat_dev = sea.shape
    for copy in copies:
        copy.wait()
    own[4] = wet[...].astype(f32)
    for index in range(6):
        cells = own[index]
        first = cells[:MARGIN]
        last = cells[rows - MARGIN :]
        near[index] = jnp.where(odd, first, last)
        away[index] = jnp.where(odd, last, first)
        turned = cells.T
        top = turned[lat_dev - MARGIN :]
        bottom = turned[:MARGIN]
        if len(strips) == 1:
            strips[0][index] = jnp.where(lat_index == 0, top, bottom)
        else:
            strips[0][index] = top
            strips[1][index] = bottom


def table_kernel(
    sizes,
    amp_in,
    phase_in,
    love_in,
    counts_in,
    legendre,
    own,
    forward,
    inverse,
    keep,
    send,
    forcing,
    latitude_out,
    love_out,
    counts_out,
    table,
    amp,
    phase,
    outer,
    sems,
    table_sems,
):
    lon_dev, lat_dev, total_cols, total_rows, wave_dev, gens = sizes
    pairs = ((amp_in, amp), (phase_in, phase), (love_in, love_out), (counts_in, counts_out))
    copies = [
        pltpu.make_async_copy(source, target, sems.at[place])
        for place, (source, target) in enumerate(pairs)
    ]
    large = fetch(legendre, 0, table, table_sems)
    for copy in copies + large:
        copy.start()
    lon_index = lax.axis_index("lon")
    lat_index = lax.axis_index("lat")
    chunk = 2 * wave_dev
    chunks = 1 << len(gens)
    scale = 1.0 / math.sqrt(total_cols)
    turn = 2.0 * math.pi / total_cols

    def trig(turns):
        angle = turn * (turns % total_cols).astype(f32)
        return jnp.cos(angle), jnp.sin(angle)

    columns = lon_index * lon_dev + lax.broadcasted_iota(jnp.int32, (wave_dev, lon_dev), 1)
    wave = lax.broadcasted_iota(jnp.int32, (wave_dev, lon_dev), 0)
    cos_in, sin_in = trig(wave * columns)
    cos_in = cos_in * scale
    sin_in = sin_in * scale
    columns = lon_index * lon_dev + lax.broadcasted_iota(jnp.int32, (chunks, lon_dev), 1)
    piece = lax.broadcasted_iota(jnp.int32, (chunks, lon_dev), 0)
    owner = jnp.zeros((chunks, lon_dev), jnp.int32) + lon_index
    for place, gen in enumerate(gens):
        owner = owner ^ (((piece >> (len(gens) - 1 - place)) & 1) * gen)
    cos_out, sin_out = trig(owner * wave_dev * columns)
    outer[0] = cos_out
    outer[1] = sin_out
    block = LANES // chunk

    def fill(index, _):
        rows = []
        for inner in range(block):
            at = pl.ds(index * block + inner, 1)
            cos_at, sin_at = outer[0, at], outer[1, at]
            rows.append(cos_at * cos_in - sin_at * sin_in)
            rows.append(-(sin_at * cos_in + cos_at * sin_in))
        rows = jnp.concatenate(rows, axis=0)
        high, low = split_bf16(rows)
        span = pl.ds(pl.multiple_of(index * LANES, LANES), LANES)
        forward[span, :lon_dev] = high
        forward[span, lon_dev:] = low
        high_t, low_t = split_bf16(rows.T)
        inverse[:lon_dev, span] = high_t
        inverse[lon_dev:, span] = low_t
        return 0

    lax.fori_loop(0, chunks // block, fill, 0)
    half = chunks * chunk // 2
    wet = own[4].astype(bf16)
    twice = jnp.concatenate([wet, wet], axis=0)
    send[...] = jnp.dot(forward[half:], twice, preferred_element_type=f32)
    keep[...] = jnp.dot(forward[:half], twice, preferred_element_type=f32)

    wide = lon_dev + 2 * MARGIN
    lane = lax.broadcasted_iota(jnp.int32, (8, 2 * lat_dev), 1)
    row = jnp.where(lane < lat_dev + lat_dev // 2, lane, lane - 2 * lat_dev) + lat_index * lat_dev
    latitude = -lat_edge + 2.0 * lat_edge * (row.astype(f32) + 0.5) / total_rows
    inside = jnp.clip(latitude, -1.5, 1.5)
    cosine = jnp.cos(inside)
    latitude_out[0] = cosine
    latitude_out[1] = 1.0 / cosine
    latitude_out[2] = rotation * jnp.sin(inside)
    semi = jnp.cos(latitude) ** 2
    diurnal = jnp.sin(2.0 * latitude)

    spot = lax.broadcasted_iota(jnp.int32, (8, wide), 1)
    order = 1 + (lax.broadcasted_iota(jnp.int32, (8, wide), 0) & 1)
    spot = jnp.where(spot < lon_dev + MARGIN, spot, spot - wide) + lon_index * lon_dev
    cos_lon, sin_lon = trig(spot * order + total_cols * 2)
    both = jnp.concatenate([cos_lon, sin_lon], axis=0).T
    cos_one, cos_two = both[:, 0:1], both[:, 1:2]
    sin_one, sin_two = both[:, 8:9], both[:, 9:10]

    count = len(frequencies)
    place = lax.broadcasted_iota(jnp.int32, (8, count), 1)
    moment = lax.broadcasted_iota(jnp.int32, (8, count), 0).astype(f32)
    omega = jnp.zeros((8, count), f32)
    for index in range(count):
        omega = jnp.where(place == index, frequencies[index], omega)
    for copy in copies:
        copy.wait()
    argument = omega * moment + phase[...]
    strength = amp[...] * (total_cols / 64.0)
    real = strength * jnp.cos(argument)
    imag = strength * jnp.sin(argument)
    is_semi = place < diurnal_from

    def total(values, chosen):
        return jnp.sum(jnp.where(chosen, values, 0.0), axis=1, keepdims=True)

    semi_real = total(real, is_semi)
    semi_imag = total(imag, is_semi)
    diurnal_real = total(real, jnp.logical_not(is_semi))
    diurnal_imag = total(imag, jnp.logical_not(is_semi))
    for k in range(SUBSTEPS):
        at = slice(k, k + 1)
        along = cos_two * semi_real[at] - sin_two * semi_imag[at]
        across = cos_one * diurnal_real[at] - sin_one * diurnal_imag[at]
        forcing[k] = along * semi[0:1] + across * diurnal[0:1]
    for copy in large:
        copy.wait()


def step_kernel(count, own, near, away, *rest):
    strips = rest[: 3 if count == 2 else 6]
    (
        forcing,
        latitude,
        legendre,
        height_out,
        east_out,
        north_out,
        wet_height,
        wet_sum,
        table,
        state,
        static,
        table_sems,
    ) = rest[len(strips) :]
    copies = fetch(legendre, table.shape[0], table, table_sems)
    for copy in copies:
        copy.start()
    above = strips[:3]
    below = strips[-3:]
    lon_dev, lat_dev = own.shape[1:]
    wide = lon_dev + 2 * MARGIN
    lanes = 2 * lat_dev
    lat_index = lax.axis_index("lat")
    odd = (lax.axis_index("lon") & 1) > 0
    has_top = lat_index < count - 1
    has_bottom = lat_index > 0
    middle = jnp.zeros((lat_dev - 2 * MARGIN, lon_dev), f32)
    lane = lax.broadcasted_iota(jnp.int32, (MARGIN, lon_dev), 1)
    use_near = (lane < MARGIN) != odd

    fields = []
    for index in range(6):
        cells = own[index]
        north_rows = jnp.where(has_top, above[0][index], 0.0)
        south_rows = jnp.where(has_bottom, below[0][index], 0.0)
        side = jnp.concatenate([north_rows, middle, south_rows], axis=0).T
        north_rows = jnp.where(use_near, above[1][index], above[2][index])
        south_rows = jnp.where(use_near, below[1][index], below[2][index])
        north_rows = jnp.where(has_top, north_rows, 0.0)
        south_rows = jnp.where(has_bottom, south_rows, 0.0)
        corner = jnp.concatenate([north_rows, middle, south_rows], axis=0).T
        from_east = jnp.where(odd, away[index], near[index])
        from_west = jnp.where(odd, near[index], away[index])
        left = jnp.concatenate([cells, from_east, from_west], axis=0)
        right = jnp.concatenate([side, corner[:MARGIN], corner[lon_dev - MARGIN :]], axis=0)
        fields.append(jnp.concatenate([left, right], axis=1))
    for index in range(3):
        state[index] = fields[index]
        static[index] = fields[3 + index]

    def along(f):
        return pltpu.roll(f, wide - 1, axis=0) - pltpu.roll(f, 1, axis=0)

    def across(f):
        return pltpu.roll(f, lanes - 1, axis=1) - pltpu.roll(f, 1, axis=1)

    cosine = latitude[0][0:1]
    secant = latitude[1][0:1]
    coriolis = latitude[2][0:1]

    def substep(k, _):
        east = state[1]
        north = state[2]
        depth = static[0]
        wet = static[1]
        divergence = (along(depth * east) + across(depth * north * cosine)) * 0.5 * secant
        height = state[0] - courant * divergence * wet
        state[0] = height
        pressure = height - forcing[k] - static[2]
        slope_east = along(pressure) * 0.5 * secant
        slope_north = across(pressure) * 0.5
        state[1] = wet * ((1.0 - friction) * east + courant * (coriolis * north - slope_east))
        state[2] = wet * ((1.0 - friction) * north - courant * (coriolis * east + slope_north))
        return 0

    lax.fori_loop(0, SUBSTEPS, substep, 0)
    core = state[0, :lon_dev, :lat_dev]
    height_out[...] = core
    east_out[...] = state[1, :lon_dev, :lat_dev]
    north_out[...] = state[2, :lon_dev, :lat_dev]
    product = core * own[4]
    wet_height[...] = product
    level = jnp.sum(jnp.sum(product, axis=0, keepdims=True), axis=1, keepdims=True)
    wet_sum[...] = jnp.broadcast_to(level, wet_sum.shape)
    for copy in copies:
        copy.wait()


def fourier_kernel(wet_height, wet_sum, forward, keep, send):
    high, low = split_bf16(wet_height[...])
    top = jnp.concatenate([high, low], axis=1)
    under = jnp.concatenate([high, jnp.zeros_like(low)], axis=1)
    weights = jnp.concatenate([top, under], axis=0)
    half = keep.shape[0]
    cols = wet_height.shape[1]

    def transform(span):
        both = jnp.dot(forward[span], weights, preferred_element_type=f32)
        return both[:, :cols] + both[:, cols:]

    send[:half] = transform(slice(half, 2 * half))
    send[half:] = wet_sum[...]
    keep[...] = transform(slice(0, half))


GROUP = 8


def pair(legendre, wave):
    return jnp.concatenate([legendre[wave], legendre[wave + 1]], axis=1)


def analysis_kernel(sizes, keep, recv, wet_sum, wet_counts, wet_keep, wet_recv, legendre, out):
    first, waves, wave_dev = sizes
    lat_dev = keep.shape[1]
    counts = wet_counts[...].astype(f32)
    total = jnp.sum(jnp.sum(counts, axis=1, keepdims=True), axis=0, keepdims=True)
    mean = wet_sum[0:1, 0:1] / total
    lines = 2 * GROUP
    line = lax.broadcasted_iota(jnp.int32, (lines, lat_dev), 0) & (GROUP - 1)
    for group in range(waves // GROUP):
        values = []
        for part in range(2):
            begin = part * wave_dev + first + group * GROUP
            span = slice(begin, begin + GROUP)
            values.append(
                (keep[span] + recv[span]) - mean * (wet_keep[span] + wet_recv[span])
            )
        value = jnp.concatenate(values, axis=0)
        result = None
        for step in range(0, GROUP, 2):
            wave = group * GROUP + step
            left = jnp.concatenate(
                [
                    jnp.where(line == step, value, 0.0).astype(bf16),
                    jnp.where(line == step + 1, value, 0.0).astype(bf16),
                ],
                axis=1,
            )
            term = lax.dot_general(
                left,
                pair(legendre, wave),
                (((1,), (1,)), ((), ())),
                preferred_element_type=f32,
            )
            result = term if result is None else result + term
        out[group * lines : (group + 1) * lines] = result.astype(out.dtype)


def synthesis_kernel(sizes, own, recv, love, legendre, *rest):
    first, waves, wave_dev = sizes
    out = rest[-1]
    lat_dev = out.shape[1]
    lines = 2 * GROUP
    line = lax.broadcasted_iota(jnp.int32, (lines, lat_dev), 0) & (GROUP - 1)
    base = lax.axis_index("lon") * wave_dev + first
    real, imag = [], []
    for group in range(waves // GROUP):
        span = slice(group * lines, (group + 1) * lines)
        total = own[span].astype(f32) + recv[span].astype(f32)
        scaled = (love[...] * total).astype(bf16)
        result = None
        for step in range(0, GROUP, 2):
            both = jnp.dot(
                scaled,
                pair(legendre, group * GROUP + step),
                preferred_element_type=f32,
            )
            left, right = both[:, :lat_dev], both[:, lat_dev:]
            result = left if result is None else jnp.where(line == step, left, result)
            result = jnp.where(line == step + 1, right, result)
        result = jnp.where(base + group * GROUP + line == 0, 1.0, 2.0) * result
        real.append(result[:GROUP])
        imag.append(result[GROUP:])
    if len(rest) == 2:
        half = rest[0].shape[0] // 2
        real.insert(0, rest[0][:half])
        imag.insert(0, rest[0][half:])
    out[...] = jnp.concatenate(real + imag, axis=0).astype(out.dtype)


def inverse_kernel(inverse, near, far, out):
    lon_dev = out.shape[0]
    half = near.shape[0]
    both = jnp.dot(inverse[:, :half], near[...], preferred_element_type=f32)
    both += jnp.dot(inverse[:, half:], far[...], preferred_element_type=f32)
    out[...] = both[:lon_dev] + both[lon_dev:]


def shards(
    sea_level,
    east_velocity,
    north_velocity,
    depth,
    land_mask,
    wet_counts,
    loading_prev,
    tide_amp,
    tide_phase,
    legendre,
    love_factor,
):
    lon_dev, lat_dev = sea_level.shape
    wave_dev, degrees = legendre.shape[:2]
    lon_count = lax.axis_size("lon")
    lat_count = lax.axis_size("lat")
    total_cols = lon_dev * lon_count
    total_rows = lat_dev * lat_count
    bits = lon_count.bit_length() - 1
    lat_bits = lat_count.bit_length() - 1
    assert lon_count == 1 << bits and lat_count == 1 << lat_bits
    gens = [1] + [(1 << b) ^ 1 for b in (1, *range(bits - 1, 1, -1))][: bits - 1]
    vmem = pl.BlockSpec(memory_space=pltpu.VMEM)
    hbm = pl.BlockSpec(memory_space=pltpu.HBM)

    strip = shaped(6, MARGIN, LANES)

    def stay_put(cells):
        return pltpu.with_memory_space_constraint(cells, pltpu.HBM)

    own, near, away, *strips = call(
        pack_kernel,
        [shaped(6, lon_dev, lat_dev), strip, strip] + [strip] * (1 if lat_count == 2 else 2),
        in_specs=[hbm] * 6,
        scratch=[
            pltpu.VMEM((lon_dev, lat_dev), jnp.int32),
            pltpu.SemaphoreType.DMA((6,)),
            pltpu.SemaphoreType.DMA,
        ],
    )(*map(stay_put, (sea_level, east_velocity, north_velocity, depth, land_mask, loading_prev)))

    def stay(b):
        return b

    def nearby(b):
        return b ^ 1

    def beyond(b):
        return (b + 1 if b & 1 else b - 1) % lon_count

    def shift(cells, lat_step, move):
        pairs = []
        for a in range(lat_count):
            target = a ^ 1 if lat_step is None else a + lat_step
            if 0 <= target < lat_count:
                for b in range(lon_count):
                    pairs.append((a * lon_count + b, target * lon_count + move(b)))
        return lax.ppermute(cells, ("lat", "lon"), pairs)

    moves = (stay, nearby, beyond)
    away = shift(away, 0, beyond)
    sources = [(None, strips[0])] if lat_count == 2 else [(-1, strips[1]), (1, strips[0])]
    strips = []
    for lat_step, source in sources:
        for move in moves:
            strips.append(shift(source, lat_step, move))
    near = shift(near, 0, nearby)

    chunk = 2 * wave_dev
    lines = chunk * lon_count
    half = lines // 2
    wide = lon_dev + 2 * MARGIN
    table_shape = pltpu.VMEM((wave_dev // 2, *legendre.shape[1:]), bf16)
    forward, inverse, wet_keep, wet_send, forcing, latitude, love, counts, table_0 = call(
        functools.partial(
            table_kernel, (lon_dev, lat_dev, total_cols, total_rows, wave_dev, tuple(gens))
        ),
        [
            shaped(lines, 2 * lon_dev, dtype=bf16),
            shaped(2 * lon_dev, lines, dtype=bf16),
            shaped(half, lat_dev),
            shaped(half, lat_dev),
            shaped(SUBSTEPS, wide, 2 * lat_dev),
            shaped(3, 8, 2 * lat_dev),
            shaped(1, degrees),
            shaped(*wet_counts.shape, dtype=jnp.int32),
            table_shape,
        ],
        in_specs=[hbm] * 5 + [vmem],
        scratch=[
            pltpu.VMEM((1, len(frequencies)), f32),
            pltpu.VMEM((1, len(frequencies)), f32),
            pltpu.VMEM((2, lon_count, lon_dev), f32),
            pltpu.SemaphoreType.DMA((4,)),
            pltpu.SemaphoreType.DMA((4,)),
        ],
    )(
        stay_put(tide_amp[None]),
        stay_put(tide_phase[None]),
        stay_put(love_factor[None]),
        stay_put(wet_counts),
        stay_put(legendre),
        own,
    )

    def swap(cells, gen):
        return lax.ppermute(cells, "lon", [(i, i ^ gen) for i in range(lon_count)])

    wet_recv = swap(wet_send, gens[0])
    for gen in gens[1:]:
        part = wet_keep.shape[0] // 2
        wet_send = wet_keep[part:] + wet_recv[part:]
        wet_keep = wet_keep[:part] + wet_recv[:part]
        wet_recv = swap(wet_send, gen)

    height, east_new, north_new, wet_height, wet_sum, table_1 = call(
        functools.partial(step_kernel, lat_count),
        [shaped(lon_dev, lat_dev)] * 4 + [shaped(8, lat_dev), table_shape],
        in_specs=[vmem] * (5 + len(strips)) + [hbm],
        scratch=[
            pltpu.VMEM((3, wide, 2 * lat_dev), f32),
            pltpu.VMEM((3, wide, 2 * lat_dev), f32),
            pltpu.SemaphoreType.DMA((4,)),
        ],
    )(own, near, away, *strips, forcing, latitude, stay_put(legendre))

    keep, send = call(
        fourier_kernel, [shaped(half, lat_dev), shaped(half + 8, lat_dev)]
    )(wet_height, wet_sum, forward)
    recv = swap(send, gens[0])
    level = wet_sum + recv[half:]
    joined = lat_count == 2 and bits > 1
    for place, gen in enumerate(gens[1:]):
        part = keep.shape[0] // 2
        send = jnp.concatenate([keep[part:] + recv[part : 2 * part], level], axis=0)
        keep = keep[:part] + recv[:part]
        recv = swap(send, gen)
        arrived = recv[part:]
        if place == 0 and joined:
            arrived = arrived + shift(level, None, stay)
            arrived = arrived + shift(level, None, lambda b: b ^ gen)
        level = level + arrived
    if not joined:
        for b in range(lat_bits):
            level = level + lax.ppermute(
                level, "lat", [(i, i ^ (1 << b)) for i in range(lat_count)]
            )

    tables = (table_0, table_1)
    parts = len(tables)
    waves = wave_dev // parts
    sums = []
    for piece in range(parts):
        mine = call(
            functools.partial(analysis_kernel, (piece * waves, waves, wave_dev)),
            shaped(2 * waves, degrees),
            in_specs=[vmem] * 7,
        )(keep, recv, level, counts, wet_keep, wet_recv, tables[piece])
        for b in range(lat_bits):
            other = lax.ppermute(mine, "lat", [(i, i ^ (1 << b)) for i in range(lat_count)])
            if b < lat_bits - 1:
                mine = mine + other
        sums.append((mine, other))
    spectra = ()
    for piece in range(parts):
        last = piece == parts - 1
        spectra = (
            call(
                functools.partial(synthesis_kernel, (piece * waves, waves, wave_dev)),
                shaped(2 * waves * (piece + 1), lat_dev, dtype=bf16 if last else f32),
                in_specs=[vmem] * (4 + len(spectra)),
            )(*sums[piece], love, tables[piece], *spectra),
        )
    near = spectra[0]
    for gen in gens[:0:-1]:
        near = jnp.concatenate([near, swap(near, gen)], axis=0)
    far = swap(near, gens[0])
    loading_new = call(inverse_kernel, shaped(lon_dev, lat_dev))(inverse, near, far)
    return (height, east_new, north_new, loading_new)


def solution(mesh):
    tile = P("lon", "lat")
    return jax.shard_map(
        shards,
        mesh=mesh,
        in_specs=(tile,) * 5 + (P(), tile, P(), P(), P("lon", None, "lat"), P()),
        out_specs=(tile,) * 4,
        check_vma=False,
    )
```

profile of v0, /device:TPU:0, one launch (start us, length us, event | category | flops | bytes accessed | tf_op | source)
XLA Modules:
  0.0 65.5 jit_solution(8105088498734079817)
XLA Ops:
  0.6 1.2 %shard_map.138 = (f32[6,128,128]{2,1,0:T(8,128)S(1)}, f32[6,8,128]{2,1,0:T(8,128)S(1)}, f32[6,8,128]{2,1,0:T(8,128)S(1)}, f32[6,8,128]{2,1,0:T(8,128)S(1)}) custom-call(f32[128,128]{1,0:T(8,128)} %sea.1, f32[128,128]{1,0:T(8,128)} %east.1, f32[128,128]{1,0:T(8,128)} %north.1, f32[128,128]{1,0:T(8,128)} %depth.1, s32[128,128]{1,0:T(8,128)} %mask.1, ...), custom_call_target="tpu_custom_call" | custom-call | tf_op jit(solution)/shard_map/pallas_call | solution.py:439
  1.9 0.6 collective-permute-start
  2.4 5.6 %collective-permute-start.1 = (f32[6,8,128]{2,1,0:T(8,128)S(1)}, f32[6,8,128]{2,1,0:T(8,128)S(1)}, u32[]{:S(2)}, u32[]{:S(2)}) collective-permute-start(f32[6,8,128]{2,1,0:T(8,128)S(1)} %get-tuple-element.27), channel_id=1, source_target_pairs={{0,15},{1,2},{2,1},{3,4},{4,3},{5,6},{6,5},{7,8},{8,7},{9,10},{10,... | collective-permute-start | bytes 73736 | tf_op jit(solution)/shard_map/ppermute | solution.py:466
  8.1 1.0 %collective-permute-start.4 = (f32[6,8,128]{2,1,0:T(8,128)S(1)}, f32[6,8,128]{2,1,0:T(8,128)S(1)}, u32[]{:S(2)}, u32[]{:S(2)}) collective-permute-start(f32[6,8,128]{2,1,0:T(8,128)S(1)} %get-tuple-element.28), channel_id=1, source_target_pairs={{0,31},{1,18},{2,17},{3,20},{4,19},{5,22},{6,21},{7,24},{8,23},{9,... | collective-permute-start | bytes 73736 | tf_op jit(solution)/shard_map/ppermute | solution.py:466
  9.0 0.0 collective-permute-start.3
  9.0 0.6 collective-permute-start.2
  9.6 2.4 %shard_map.139 = (bf16[1024,256]{1,0:T(8,128)(2,1)S(1)}, bf16[256,1024]{1,0:T(8,128)(2,1)S(1)}, f32[512,128]{1,0:T(8,128)S(1)}, f32[512,128]{1,0:T(8,128)S(1)}, ...) custom-call(f32[1,8]{1,0:T(1,128)} %bitcast.4, ...), custom_call_target="tpu_custom_call" | custom-call | tf_op jit(solution)/shard_map/pallas_call | solution.py:482
  12.0 0.0 collective-permute-done.near
  12.0 0.0 collective-permute-done.1.away
  12.0 2.9 %collective-permute-done.4.rest_2_ = f32[6,8,128]{2,1,0:T(8,128)S(1)} collective-permute-done((f32[6,8,128]{2,1,0:T(8,128)S(1)}, f32[6,8,128]{2,1,0:T(8,128)S(1)}, u32[]{:S(2)}, u32[]{:S(2)}) %collective-permute-start.4) | collective-permute-done | bytes 24608 | tf_op jit(solution)/shard_map/ppermute | solution.py:466
  14.9 0.0 collective-permute-done.3.rest_1_
  14.9 0.0 collective-permute-done.2.rest_0_
  14.9 2.9 %shard_map.140 = (f32[128,128]{1,0:T(8,128)}, f32[128,128]{1,0:T(8,128)}, f32[128,128]{1,0:T(8,128)}, f32[128,128]{1,0:T(8,128)S(1)}, f32[8,128]{1,0:T(8,128)S(1)}, /*index=5*/bf16[16,1024,128]{2,1,0:T(8,128)(2,1)S(1)}) custom-call(f32[6,128,128]{2,1,0:T(8,128)S(1)} %get-tuple-element.25.own, f32[6,8,128]{2,1,0:T(8,128)S(1)} %collective-permute-done.near, ...), custom_call_target="tpu_custom_call" | custom-call | tf_op jit(solution)/shard_map/pallas_call | solution.py:524
  17.8 0.3 shard_map.141
  18.1 0.1 collective-permute-start.5
  18.2 0.5 collective-permute-start.11
  18.7 1.0 %collective-permute-done.5 = f32[520,128]{1,0:T(8,128)S(1)} collective-permute-done((f32[520,128]{1,0:T(8,128)S(1)}, f32[520,128]{1,0:T(8,128)S(1)}, u32[]{:S(2)}, u32[]{:S(2)}) %collective-permute-start.5) | collective-permute-done | bytes 266272 | tf_op jit(solution)/shard_map/ppermute | solution.py:515
  19.8 0.1 collective-permute-start.6
  19.9 0.2 collective-permute-done.11
  20.1 1.6 %collective-permute-start.12 = (f32[256,128]{1,0:T(8,128)S(1)}, f32[256,128]{1,0:T(8,128)S(1)}, u32[]{:S(2)}, u32[]{:S(2)}) collective-permute-start(f32[256,128]{1,0:T(8,128)S(1)} %get-tuple-element.49), channel_id=1, source_target_pairs={{0,3},{1,2},{2,1},{3,0},{4,7},{5,6},{6,5},{7,4},{8,11},{9,10},{10,... | collective-permute-start | bytes 393224 | tf_op jit(solution)/shard_map/ppermute | solution.py:515
  21.7 1.2 %collective-permute-start.8 = (f32[8,128]{1,0:T(8,128)S(1)}, f32[8,128]{1,0:T(8,128)S(1)}, u32[]{:S(2)}, u32[]{:S(2)}) collective-permute-start(f32[8,128]{1,0:T(8,128)S(1)} %slice_add_fusion.15), channel_id=1, source_target_pairs={{0,19},{1,18},{2,17},{3,16},{4,23},{5,22},{6,21},{7,20},{8,27},{9,... | collective-permute-start | bytes 12296 | tf_op jit(solution)/shard_map/ppermute | solution.py:466
  22.9 0.5 collective-permute-start.7
  23.4 2.0 %collective-permute-done.6 = f32[264,128]{1,0:T(8,128)S(1)} collective-permute-done((f32[264,128]{1,0:T(8,128)S(1)}, f32[264,128]{1,0:T(8,128)S(1)}, u32[]{:S(2)}, u32[]{:S(2)}) %collective-permute-start.6) | collective-permute-done | bytes 135200 | tf_op jit(solution)/shard_map/ppermute | solution.py:515
  25.4 3.8 %collective-permute-done.8 = f32[8,128]{1,0:T(8,128)S(1)} collective-permute-done((f32[8,128]{1,0:T(8,128)S(1)}, f32[8,128]{1,0:T(8,128)S(1)}, u32[]{:S(2)}, u32[]{:S(2)}) %collective-permute-start.8) | collective-permute-done | bytes 4128 | tf_op jit(solution)/shard_map/ppermute | solution.py:466
  29.3 0.0 collective-permute-done.7
  29.3 0.1 collective-permute-start.9
  29.4 0.0 collective-permute-done.12
  29.4 2.7 %collective-permute-start.13 = (f32[128,128]{1,0:T(8,128)S(1)}, f32[128,128]{1,0:T(8,128)S(1)}, u32[]{:S(2)}, u32[]{:S(2)}) collective-permute-start(f32[128,128]{1,0:T(8,128)S(1)} %get-tuple-element.53), channel_id=1, source_target_pairs={{0,9},{1,8},{2,11},{3,10},{4,13},{5,12},{6,15},{7,14},{8,1},{9,0},... | collective-permute-start | bytes 196616 | tf_op jit(solution)/shard_map/ppermute | solution.py:515
  32.1 2.4 %collective-permute-done.9 = f32[136,128]{1,0:T(8,128)S(1)} collective-permute-done((f32[136,128]{1,0:T(8,128)S(1)}, f32[136,128]{1,0:T(8,128)S(1)}, u32[]{:S(2)}, u32[]{:S(2)}) %collective-permute-start.9) | collective-permute-done | bytes 69664 | tf_op jit(solution)/shard_map/ppermute | solution.py:515
  34.5 0.1 collective-permute-start.10
  34.6 2.7 %collective-permute-done.13 = f32[128,128]{1,0:T(8,128)S(1)} collective-permute-done((f32[128,128]{1,0:T(8,128)S(1)}, f32[128,128]{1,0:T(8,128)S(1)}, u32[]{:S(2)}, u32[]{:S(2)}) %collective-permute-start.13) | collective-permute-done | bytes 65568 | tf_op jit(solution)/shard_map/ppermute | solution.py:515
  37.3 0.1 collective-permute-start.14
  37.4 0.6 collective-permute-done.10.recv
  38.0 2.8 %collective-permute-done.14.wet_recv = f32[64,128]{1,0:T(8,128)S(1)} collective-permute-done((f32[64,128]{1,0:T(8,128)S(1)}, f32[64,128]{1,0:T(8,128)S(1)}, u32[]{:S(2)}, u32[]{:S(2)}) %collective-permute-start.14) | collective-permute-done | bytes 32800 | tf_op jit(solution)/shard_map/ppermute | solution.py:515
  40.8 1.2 %shard_map.143.own = f32[32,1024]{1,0:T(8,128)S(1)} custom-call(f32[64,128]{1,0:T(8,128)S(1)} %get-tuple-element.55.keep, f32[72,128]{1,0:T(8,128)S(1)} %collective-permute-done.10.recv, f32[8,128]{1,0:T(8,128)S(1)} %slice_add_fusion.12.wet_sum, s32[2,16]{1,0:T(2,128)S(1)} %get-tuple-element.40.wet_counts, f32[64,128]{1,0:T(8,128)S(1)} %get-tuple-element.57.wet_keep, ...), custom_call_target="tpu_custom_call" | custom-call | tf_op jit(solution)/shard_map/pallas_call | solution.py:562
  42.0 0.8 %collective-permute-start.16 = (f32[32,1024]{1,0:T(8,128)S(1)}, f32[32,1024]{1,0:T(8,128)S(1)}, u32[]{:S(2)}, u32[]{:S(2)}) collective-permute-start(f32[32,1024]{1,0:T(8,128)S(1)} %shard_map.143.own), channel_id=1, source_target_pairs={{0,16},{16,0},{1,17},{17,1},{2,18},{18,2},{3,19},{19,3},{4,20},{20... | collective-permute-start | bytes 393224 | tf_op jit(solution)/shard_map/ppermute | solution.py:568
  42.8 1.2 %shard_map.142.own = f32[32,1024]{1,0:T(8,128)S(1)} custom-call(f32[64,128]{1,0:T(8,128)S(1)} %get-tuple-element.55.keep, f32[72,128]{1,0:T(8,128)S(1)} %collective-permute-done.10.recv, f32[8,128]{1,0:T(8,128)S(1)} %slice_add_fusion.12.wet_sum, s32[2,16]{1,0:T(2,128)S(1)} %get-tuple-element.40.wet_counts, f32[64,128]{1,0:T(8,128)S(1)} %get-tuple-element.57.wet_keep, ...), custom_call_target="tpu_custom_call" | custom-call | tf_op jit(solution)/shard_map/pallas_call | solution.py:562
  44.0 1.3 %collective-permute-start.15 = (f32[32,1024]{1,0:T(8,128)S(1)}, f32[32,1024]{1,0:T(8,128)S(1)}, u32[]{:S(2)}, u32[]{:S(2)}) collective-permute-start(f32[32,1024]{1,0:T(8,128)S(1)} %shard_map.142.own), channel_id=1, source_target_pairs={{0,16},{16,0},{1,17},{17,1},{2,18},{18,2},{3,19},{19,3},{4,20},{20... | collective-permute-start | bytes 393224 | tf_op jit(solution)/shard_map/ppermute | solution.py:568
  45.3 3.1 %collective-permute-done.16.recv = f32[32,1024]{1,0:T(8,128)S(1)} collective-permute-done((f32[32,1024]{1,0:T(8,128)S(1)}, f32[32,1024]{1,0:T(8,128)S(1)}, u32[]{:S(2)}, u32[]{:S(2)}) %collective-permute-start.16) | collective-permute-done | bytes 131104 | tf_op jit(solution)/shard_map/ppermute | solution.py:568
  48.4 0.7 %shard_map.144.rest_0_ = f32[32,128]{1,0:T(8,128)S(1)} custom-call(f32[32,1024]{1,0:T(8,128)S(1)} %shard_map.143.own, f32[32,1024]{1,0:T(8,128)S(1)} %collective-permute-done.16.recv, f32[1,1024]{1,0:T(1,128)S(1)} %get-tuple-element.44.love, bf16[16,1024,128]{2,1,0:T(8,128)(2,1)S(1)} %get-tuple-element.45.legendre), custom_call_target="tpu_custom_call" | custom-call | tf_op jit(solution)/shard_map/pallas_call | solution.py:576
  49.1 1.3 %collective-permute-done.15.recv = f32[32,1024]{1,0:T(8,128)S(1)} collective-permute-done((f32[32,1024]{1,0:T(8,128)S(1)}, f32[32,1024]{1,0:T(8,128)S(1)}, u32[]{:S(2)}, u32[]{:S(2)}) %collective-permute-start.15) | collective-permute-done | bytes 131104 | tf_op jit(solution)/shard_map/ppermute | solution.py:568
  50.4 0.7 %shard_map.145 = bf16[64,128]{1,0:T(8,128)(2,1)S(1)} custom-call(f32[32,1024]{1,0:T(8,128)S(1)} %shard_map.142.own, f32[32,1024]{1,0:T(8,128)S(1)} %collective-permute-done.15.recv, f32[1,1024]{1,0:T(1,128)S(1)} %get-tuple-element.44.love, bf16[16,1024,128]{2,1,0:T(8,128)(2,1)S(1)} %get-tuple-element.43.legendre, f32[32,128]{1,0:T(8,128)S(1)} %shard_map.144.rest_0_), custom_call_target="tpu_custom_call" | custom-call | tf_op jit(solution)/shard_map/pallas_call | solution.py:576
  51.0 0.0 collective-permute-start.17
  51.0 3.2 %collective-permute-done.17 = bf16[64,128]{1,0:T(8,128)(2,1)S(1)} collective-permute-done((bf16[64,128]{1,0:T(8,128)(2,1)S(1)}, bf16[64,128]{1,0:T(8,128)(2,1)S(1)}, u32[]{:S(2)}, u32[]{:S(2)}) %collective-permute-start.17) | collective-permute-done | bytes 16416 | tf_op jit(solution)/shard_map/ppermute | solution.py:515
  54.2 1.5 %collective-permute-start.18 = (bf16[128,128]{1,0:T(8,128)(2,1)S(1)}, bf16[128,128]{1,0:T(8,128)(2,1)S(1)}, u32[]{:S(2)}, u32[]{:S(2)}) collective-permute-start(bf16[128,128]{1,0:T(8,128)(2,1)S(1)} %pad_maximum_fusion.5), channel_id=1, source_target_pairs={{0,9},{1,8},{2,11},{3,10},{4,13},{5,12},{6,15},{7,14},{8,1},{9,0},... | collective-permute-start | bytes 98312 | tf_op jit(solution)/shard_map/ppermute | solution.py:515
  55.7 3.3 %collective-permute-done.18 = bf16[128,128]{1,0:T(8,128)(2,1)S(1)} collective-permute-done((bf16[128,128]{1,0:T(8,128)(2,1)S(1)}, bf16[128,128]{1,0:T(8,128)(2,1)S(1)}, u32[]{:S(2)}, u32[]{:S(2)}) %collective-permute-start.18) | collective-permute-done | bytes 32800 | tf_op jit(solution)/shard_map/ppermute | solution.py:515
  59.0 0.7 %collective-permute-start.19 = (bf16[256,128]{1,0:T(8,128)(2,1)S(1)}, bf16[256,128]{1,0:T(8,128)(2,1)S(1)}, u32[]{:S(2)}, u32[]{:S(2)}) collective-permute-start(bf16[256,128]{1,0:T(8,128)(2,1)S(1)} %pad_maximum_fusion.3), channel_id=1, source_target_pairs={{0,3},{1,2},{2,1},{3,0},{4,7},{5,6},{6,5},{7,4},{8,11},{9,10},{10,... | collective-permute-start | bytes 196616 | tf_op jit(solution)/shard_map/ppermute | solution.py:515
  59.8 3.4 %collective-permute-done.19 = bf16[256,128]{1,0:T(8,128)(2,1)S(1)} collective-permute-done((bf16[256,128]{1,0:T(8,128)(2,1)S(1)}, bf16[256,128]{1,0:T(8,128)(2,1)S(1)}, u32[]{:S(2)}, u32[]{:S(2)}) %collective-permute-start.19) | collective-permute-done | bytes 65568 | tf_op jit(solution)/shard_map/ppermute | solution.py:515
  63.2 0.1 collective-permute-start.20
  63.2 1.3 %collective-permute-done.20.far = bf16[512,128]{1,0:T(8,128)(2,1)S(1)} collective-permute-done((bf16[512,128]{1,0:T(8,128)(2,1)S(1)}, bf16[512,128]{1,0:T(8,128)(2,1)S(1)}, u32[]{:S(2)}, u32[]{:S(2)}) %collective-permute-start.20) | collective-permute-done | bytes 131104 | tf_op jit(solution)/shard_map/ppermute | solution.py:515
  64.6 0.9 %shard_map.146 = f32[128,128]{1,0:T(8,128)} custom-call(bf16[256,1024]{1,0:T(8,128)(2,1)S(1)} %get-tuple-element.34.inverse, bf16[512,128]{1,0:T(8,128)(2,1)S(1)} %pad_maximum_fusion.1.near, bf16[512,128]{1,0:T(8,128)(2,1)S(1)} %collective-permute-done.20.far), custom_call_target="tpu_custom_call" | custom-call | tf_op jit(solution)/shard_map/pallas_call | solution.py:586
  (16 shorter events, 0.2 us)
Async XLA Ops:
  1.9 10.1 %collective-permute-start = (f32[6,8,128]{2,1,0:T(8,128)S(1)}, f32[6,8,128]{2,1,0:T(8,128)S(1)}, u32[]{:S(2)}, u32[]{:S(2)}) collective-permute-start(f32[6,8,128]{2,1,0:T(8,128)S(1)} %get-tuple-element.26), channel_id=1, source_target_pairs={{0,1},{1,0},{2,3},{3,2},{4,5},{5,4},{6,7},{7,6},{8,9},{9,8},{10,11... | collective-permute-start | bytes 73736 | tf_op jit(solution)/shard_map/ppermute | solution.py:466
  2.4 9.5 %collective-permute-start.1 = (f32[6,8,128]{2,1,0:T(8,128)S(1)}, f32[6,8,128]{2,1,0:T(8,128)S(1)}, u32[]{:S(2)}, u32[]{:S(2)}) collective-permute-start(f32[6,8,128]{2,1,0:T(8,128)S(1)} %get-tuple-element.27), channel_id=1, source_target_pairs={{0,15},{1,2},{2,1},{3,4},{4,3},{5,6},{6,5},{7,8},{8,7},{9,10},{10,... | collective-permute-start | bytes 73736 | tf_op jit(solution)/shard_map/ppermute | solution.py:466
  8.1 6.8 %collective-permute-start.4 = (f32[6,8,128]{2,1,0:T(8,128)S(1)}, f32[6,8,128]{2,1,0:T(8,128)S(1)}, u32[]{:S(2)}, u32[]{:S(2)}) collective-permute-start(f32[6,8,128]{2,1,0:T(8,128)S(1)} %get-tuple-element.28), channel_id=1, source_target_pairs={{0,31},{1,18},{2,17},{3,20},{4,19},{5,22},{6,21},{7,24},{8,23},{9,... | collective-permute-start | bytes 73736 | tf_op jit(solution)/shard_map/ppermute | solution.py:466
  9.0 5.9 %collective-permute-start.3 = (f32[6,8,128]{2,1,0:T(8,128)S(1)}, f32[6,8,128]{2,1,0:T(8,128)S(1)}, u32[]{:S(2)}, u32[]{:S(2)}) collective-permute-start(f32[6,8,128]{2,1,0:T(8,128)S(1)} %get-tuple-element.28), channel_id=1, source_target_pairs={{0,17},{1,16},{2,19},{3,18},{4,21},{5,20},{6,23},{7,22},{8,25},{9,... | collective-permute-start | bytes 73736 | tf_op jit(solution)/shard_map/ppermute | solution.py:466
  9.0 5.9 %collective-permute-start.2 = (f32[6,8,128]{2,1,0:T(8,128)S(1)}, f32[6,8,128]{2,1,0:T(8,128)S(1)}, u32[]{:S(2)}, u32[]{:S(2)}) collective-permute-start(f32[6,8,128]{2,1,0:T(8,128)S(1)} %get-tuple-element.28), channel_id=1, source_target_pairs={{0,16},{1,17},{2,18},{3,19},{4,20},{5,21},{6,22},{7,23},{8,24},{9,... | collective-permute-start | bytes 73736 | tf_op jit(solution)/shard_map/ppermute | solution.py:466
  18.1 1.6 %collective-permute-start.5 = (f32[520,128]{1,0:T(8,128)S(1)}, f32[520,128]{1,0:T(8,128)S(1)}, u32[]{:S(2)}, u32[]{:S(2)}) collective-permute-start(f32[520,128]{1,0:T(8,128)S(1)} %get-tuple-element.39), channel_id=1, source_target_pairs={{0,1},{1,0},{2,3},{3,2},{4,5},{5,4},{6,7},{7,6},{8,9},{9,8},{10,11... | collective-permute-start | bytes 798728 | tf_op jit(solution)/shard_map/ppermute | solution.py:515
  18.2 1.9 %collective-permute-start.11 = (f32[512,128]{1,0:T(8,128)S(1)}, f32[512,128]{1,0:T(8,128)S(1)}, u32[]{:S(2)}, u32[]{:S(2)}) collective-permute-start(f32[512,128]{1,0:T(8,128)S(1)} %get-tuple-element.42), channel_id=1, source_target_pairs={{0,1},{1,0},{2,3},{3,2},{4,5},{5,4},{6,7},{7,6},{8,9},{9,8},{10,11... | collective-permute-start | bytes 786440 | tf_op jit(solution)/shard_map/ppermute | solution.py:515
  19.8 5.6 %collective-permute-start.6 = (f32[264,128]{1,0:T(8,128)S(1)}, f32[264,128]{1,0:T(8,128)S(1)}, u32[]{:S(2)}, u32[]{:S(2)}) collective-permute-start(f32[264,128]{1,0:T(8,128)S(1)} %pad_maximum_fusion), channel_id=1, source_target_pairs={{0,3},{1,2},{2,1},{3,0},{4,7},{5,6},{6,5},{7,4},{8,11},{9,10},{10,... | collective-permute-start | bytes 405512 | tf_op jit(solution)/shard_map/ppermute | solution.py:515
  20.1 9.2 %collective-permute-start.12 = (f32[256,128]{1,0:T(8,128)S(1)}, f32[256,128]{1,0:T(8,128)S(1)}, u32[]{:S(2)}, u32[]{:S(2)}) collective-permute-start(f32[256,128]{1,0:T(8,128)S(1)} %get-tuple-element.49), channel_id=1, source_target_pairs={{0,3},{1,2},{2,1},{3,0},{4,7},{5,6},{6,5},{7,4},{8,11},{9,10},{10,... | collective-permute-start | bytes 393224 | tf_op jit(solution)/shard_map/ppermute | solution.py:515
  21.7 7.6 %collective-permute-start.8 = (f32[8,128]{1,0:T(8,128)S(1)}, f32[8,128]{1,0:T(8,128)S(1)}, u32[]{:S(2)}, u32[]{:S(2)}) collective-permute-start(f32[8,128]{1,0:T(8,128)S(1)} %slice_add_fusion.15), channel_id=1, source_target_pairs={{0,19},{1,18},{2,17},{3,16},{4,23},{5,22},{6,21},{7,20},{8,27},{9,... | collective-permute-start | bytes 12296 | tf_op jit(solution)/shard_map/ppermute | solution.py:466
  22.9 6.4 %collective-permute-start.7 = (f32[8,128]{1,0:T(8,128)S(1)}, f32[8,128]{1,0:T(8,128)S(1)}, u32[]{:S(2)}, u32[]{:S(2)}) collective-permute-start(f32[8,128]{1,0:T(8,128)S(1)} %slice_add_fusion.15), channel_id=1, source_target_pairs={{0,16},{1,17},{2,18},{3,19},{4,20},{5,21},{6,22},{7,23},{8,24},{9,... | collective-permute-start | bytes 12296 | tf_op jit(solution)/shard_map/ppermute | solution.py:466
  29.3 5.2 %collective-permute-start.9 = (f32[136,128]{1,0:T(8,128)S(1)}, f32[136,128]{1,0:T(8,128)S(1)}, u32[]{:S(2)}, u32[]{:S(2)}) collective-permute-start(f32[136,128]{1,0:T(8,128)S(1)} %pad_maximum_fusion.2), channel_id=1, source_target_pairs={{0,9},{1,8},{2,11},{3,10},{4,13},{5,12},{6,15},{7,14},{8,1},{9,0},... | collective-permute-start | bytes 208904 | tf_op jit(solution)/shard_map/ppermute | solution.py:515
  29.4 7.9 %collective-permute-start.13 = (f32[128,128]{1,0:T(8,128)S(1)}, f32[128,128]{1,0:T(8,128)S(1)}, u32[]{:S(2)}, u32[]{:S(2)}) collective-permute-start(f32[128,128]{1,0:T(8,128)S(1)} %get-tuple-element.53), channel_id=1, source_target_pairs={{0,9},{1,8},{2,11},{3,10},{4,13},{5,12},{6,15},{7,14},{8,1},{9,0},... | collective-permute-start | bytes 196616 | tf_op jit(solution)/shard_map/ppermute | solution.py:515
  34.5 3.4 %collective-permute-start.10 = (f32[72,128]{1,0:T(8,128)S(1)}, f32[72,128]{1,0:T(8,128)S(1)}, u32[]{:S(2)}, u32[]{:S(2)}) collective-permute-start(f32[72,128]{1,0:T(8,128)S(1)} %pad_maximum_fusion.4), channel_id=1, source_target_pairs={{0,5},{1,4},{2,7},{3,6},{4,1},{5,0},{6,3},{7,2},{8,13},{9,12},{10,... | collective-permute-start | bytes 110600 | tf_op jit(solution)/shard_map/ppermute | solution.py:515
  37.3 3.5 %collective-permute-start.14 = (f32[64,128]{1,0:T(8,128)S(1)}, f32[64,128]{1,0:T(8,128)S(1)}, u32[]{:S(2)}, u32[]{:S(2)}) collective-permute-start(f32[64,128]{1,0:T(8,128)S(1)} %get-tuple-element.56), channel_id=1, source_target_pairs={{0,5},{1,4},{2,7},{3,6},{4,1},{5,0},{6,3},{7,2},{8,13},{9,12},{10,... | collective-permute-start | bytes 98312 | tf_op jit(solution)/shard_map/ppermute | solution.py:515
  42.0 6.4 %collective-permute-start.16 = (f32[32,1024]{1,0:T(8,128)S(1)}, f32[32,1024]{1,0:T(8,128)S(1)}, u32[]{:S(2)}, u32[]{:S(2)}) collective-permute-start(f32[32,1024]{1,0:T(8,128)S(1)} %shard_map.143.own), channel_id=1, source_target_pairs={{0,16},{16,0},{1,17},{17,1},{2,18},{18,2},{3,19},{19,3},{4,20},{20... | collective-permute-start | bytes 393224 | tf_op jit(solution)/shard_map/ppermute | solution.py:568
  44.0 6.3 %collective-permute-start.15 = (f32[32,1024]{1,0:T(8,128)S(1)}, f32[32,1024]{1,0:T(8,128)S(1)}, u32[]{:S(2)}, u32[]{:S(2)}) collective-permute-start(f32[32,1024]{1,0:T(8,128)S(1)} %shard_map.142.own), channel_id=1, source_target_pairs={{0,16},{16,0},{1,17},{17,1},{2,18},{18,2},{3,19},{19,3},{4,20},{20... | collective-permute-start | bytes 393224 | tf_op jit(solution)/shard_map/ppermute | solution.py:568
  51.0 3.2 %collective-permute-start.17 = (bf16[64,128]{1,0:T(8,128)(2,1)S(1)}, bf16[64,128]{1,0:T(8,128)(2,1)S(1)}, u32[]{:S(2)}, u32[]{:S(2)}) collective-permute-start(bf16[64,128]{1,0:T(8,128)(2,1)S(1)} %shard_map.145), channel_id=1, source_target_pairs={{0,5},{1,4},{2,7},{3,6},{4,1},{5,0},{6,3},{7,2},{8,13},{9,12},{10,... | collective-permute-start | bytes 49160 | tf_op jit(solution)/shard_map/ppermute | solution.py:515
  54.2 4.8 %collective-permute-start.18 = (bf16[128,128]{1,0:T(8,128)(2,1)S(1)}, bf16[128,128]{1,0:T(8,128)(2,1)S(1)}, u32[]{:S(2)}, u32[]{:S(2)}) collective-permute-start(bf16[128,128]{1,0:T(8,128)(2,1)S(1)} %pad_maximum_fusion.5), channel_id=1, source_target_pairs={{0,9},{1,8},{2,11},{3,10},{4,13},{5,12},{6,15},{7,14},{8,1},{9,0},... | collective-permute-start | bytes 98312 | tf_op jit(solution)/shard_map/ppermute | solution.py:515
  59.0 4.1 %collective-permute-start.19 = (bf16[256,128]{1,0:T(8,128)(2,1)S(1)}, bf16[256,128]{1,0:T(8,128)(2,1)S(1)}, u32[]{:S(2)}, u32[]{:S(2)}) collective-permute-start(bf16[256,128]{1,0:T(8,128)(2,1)S(1)} %pad_maximum_fusion.3), channel_id=1, source_target_pairs={{0,3},{1,2},{2,1},{3,0},{4,7},{5,6},{6,5},{7,4},{8,11},{9,10},{10,... | collective-permute-start | bytes 196616 | tf_op jit(solution)/shard_map/ppermute | solution.py:515
  63.2 1.4 %collective-permute-start.20 = (bf16[512,128]{1,0:T(8,128)(2,1)S(1)}, bf16[512,128]{1,0:T(8,128)(2,1)S(1)}, u32[]{:S(2)}, u32[]{:S(2)}) collective-permute-start(bf16[512,128]{1,0:T(8,128)(2,1)S(1)} %pad_maximum_fusion.1.near), channel_id=1, source_target_pairs={{0,1},{1,0},{2,3},{3,2},{4,5},{5,4},{6,7},{7,6},{8,9},{9,8},{10,11... | collective-permute-start | bytes 393224 | tf_op jit(solution)/shard_map/ppermute | solution.py:515
where the time goes:
time: 65.7 us; the launch traced here: 65.5 us
  waiting for transfers between devices  34.1 us (52%)
  starting transfers between devices  18.9 us (29%)
  Pallas kernels  11.5 us (18%)
  between operations  0.81 us (1%)
    ppermute x12, waiting for transfers between devices, swap(): return lax.ppermute(cells, 'lon', [(i, i ^ gen) for i in range(lon_count)])  23 us
    ppermute x7, starting transfers between devices, shift(): return lax.ppermute(cells, ('lat', 'lon'), pairs)  9.41 us
    ppermute x12, starting transfers between devices, swap(): return lax.ppermute(cells, 'lon', [(i, i ^ gen) for i in range(lon_count)])  7.43 us
    ppermute x7, waiting for transfers between devices, shift(): return lax.ppermute(cells, ('lat', 'lon'), pairs)  6.77 us
    ppermute x2, waiting for transfers between devices, shards(): lax.ppermute(mine, 'lat', [(i, i ^ 1 << b) for i in range(lat_count)])  4.39 us
    pallas_call x1, Pallas kernels, shards(): call(functools.partial(step_kernel, lat_count), [shaped(lon_dev, lat_dev)...  2.89 us
    pallas_call x2, Pallas kernels, shards(): call(functools.partial(analysis_kernel, (piece * waves, waves, wave_dev))...  2.47 us
    pallas_call x1, Pallas kernels, shards(): call(functools.partial(table_kernel, (lon_dev, lat_dev, total_cols, total...  2.37 us
  transfers between devices with their start and end apart: 21, of which 15 were waited for; matrix products, arithmetic and copies ran while one was open for 0% of the time, Pallas kernels for 7%

commit v1 on v0

--- a/solution.py
+++ b/solution.py
@@ -65,7 +65,10 @@
     rows, lat_dev = sea.shape
     for copy in copies:
         copy.wait()
-    own[4] = wet[...].astype(f32)
+    filled = wet[...].astype(f32)
+    own[4] = filled
+    for index in range(rows // MARGIN):
+        near[6 + index] = filled[index * MARGIN : (index + 1) * MARGIN]
     for index in range(6):
         cells = own[index]
         first = cells[:MARGIN]
@@ -82,6 +85,18 @@
             strips[1][index] = bottom
 
 
+def turns_trig(turns, total_cols):
+    angle = (2.0 * math.pi / total_cols) * (turns % total_cols).astype(f32)
+    return jnp.cos(angle), jnp.sin(angle)
+
+
+def owners(piece, lon_index, gens):
+    owner = jnp.zeros(piece.shape, jnp.int32) + lon_index
+    for place, gen in enumerate(gens):
+        owner = owner ^ (((piece >> (len(gens) - 1 - place)) & 1) * gen)
+    return owner
+
+
 def table_kernel(
     sizes,
     amp_in,
@@ -90,10 +105,10 @@
     counts_in,
     legendre,
     own,
+    near,
     forward,
     inverse,
-    keep,
-    send,
+    wet_pair,
     forcing,
     latitude_out,
     love_out,
@@ -119,11 +134,9 @@
     chunk = 2 * wave_dev
     chunks = 1 << len(gens)
     scale = 1.0 / math.sqrt(total_cols)
-    turn = 2.0 * math.pi / total_cols
 
     def trig(turns):
-        angle = turn * (turns % total_cols).astype(f32)
-        return jnp.cos(angle), jnp.sin(angle)
+        return turns_trig(turns, total_cols)
 
     columns = lon_index * lon_dev + lax.broadcasted_iota(jnp.int32, (wave_dev, lon_dev), 1)
     wave = lax.broadcasted_iota(jnp.int32, (wave_dev, lon_dev), 0)
@@ -132,9 +145,7 @@
     sin_in = sin_in * scale
     columns = lon_index * lon_dev + lax.broadcasted_iota(jnp.int32, (chunks, lon_dev), 1)
     piece = lax.broadcasted_iota(jnp.int32, (chunks, lon_dev), 0)
-    owner = jnp.zeros((chunks, lon_dev), jnp.int32) + lon_index
-    for place, gen in enumerate(gens):
-        owner = owner ^ (((piece >> (len(gens) - 1 - place)) & 1) * gen)
+    owner = owners(piece, lon_index, gens)
     cos_out, sin_out = trig(owner * wave_dev * columns)
     outer[0] = cos_out
     outer[1] = sin_out
@@ -158,11 +169,11 @@
         return 0
 
     lax.fori_loop(0, chunks // block, fill, 0)
-    half = chunks * chunk // 2
-    wet = own[4].astype(bf16)
-    twice = jnp.concatenate([wet, wet], axis=0)
-    send[...] = jnp.dot(forward[half:], twice, preferred_element_type=f32)
-    keep[...] = jnp.dot(forward[:half], twice, preferred_element_type=f32)
+    wet_pair[:lon_dev] = own[4].astype(bf16)
+    for index in range(0, lon_dev // MARGIN, 2):
+        both = jnp.concatenate([near[6 + index], near[7 + index]], axis=0)
+        at = lon_dev + index * MARGIN
+        wet_pair[at : at + 2 * MARGIN] = both.astype(bf16)
 
     wide = lon_dev + 2 * MARGIN
     lane = lax.broadcasted_iota(jnp.int32, (8, 2 * lat_dev), 1)
@@ -212,6 +223,42 @@
         forcing[k] = along * semi[0:1] + across * diurnal[0:1]
     for copy in large:
         copy.wait()
+
+
+def mask_kernel(sizes, pair, far, keep, send):
+    lon_dev, total_cols, wave_dev, gens = sizes
+    lon_index = lax.axis_index("lon")
+    chunks = 1 << (len(gens) - 2)
+    scale = 1.0 / math.sqrt(total_cols)
+    column = lax.broadcasted_iota(jnp.int32, (wave_dev, lon_dev), 1)
+    wave = lax.broadcasted_iota(jnp.int32, (wave_dev, lon_dev), 0)
+    spot = lax.broadcasted_iota(jnp.int32, (chunks, lon_dev), 1)
+    piece = lax.broadcasted_iota(jnp.int32, (chunks, lon_dev), 0)
+    owner = owners(piece, lon_index, gens[2:])
+    result = None
+    for source, other in ((pair, 0), (far, gens[1])):
+        for at, offset in ((0, other), (1, other ^ gens[0])):
+            start = (lon_index ^ offset) * lon_dev
+            cos_in, sin_in = turns_trig(wave * (column + start), total_cols)
+            cos_in = cos_in * scale
+            sin_in = sin_in * scale
+            cos_out, sin_out = turns_trig(owner * wave_dev * (spot + start), total_cols)
+            rows = []
+            for index in range(chunks):
+                cos_at, sin_at = cos_out[index : index + 1], sin_out[index : index + 1]
+                rows.append(cos_at * cos_in - sin_at * sin_in)
+                rows.append(-(sin_at * cos_in + cos_at * sin_in))
+            high, low = split_bf16(jnp.concatenate(rows, axis=0))
+            wet = source[at * lon_dev : (at + 1) * lon_dev]
+            term = jnp.dot(
+                jnp.concatenate([high, low], axis=1),
+                jnp.concatenate([wet, wet], axis=0),
+                preferred_element_type=f32,
+            )
+            result = term if result is None else result + term
+    half = keep.shape[0]
+    keep[...] = result[:half]
+    send[...] = result[half:]
 
 
 def step_kernel(count, own, near, away, *rest):
@@ -328,26 +375,23 @@
     return jnp.concatenate([legendre[wave], legendre[wave + 1]], axis=1)
 
 
-def analysis_kernel(sizes, keep, recv, wet_sum, wet_counts, wet_keep, wet_recv, legendre, out):
-    first, waves, wave_dev = sizes
+def analysis_kernel(first, keep, recv, wet_keep, wet_sum, wet_counts, table, out, *sent):
     lat_dev = keep.shape[1]
+    rows = keep.shape[0]
     counts = wet_counts[...].astype(f32)
     total = jnp.sum(jnp.sum(counts, axis=1, keepdims=True), axis=0, keepdims=True)
     mean = wet_sum[0:1, 0:1] / total
     lines = 2 * GROUP
     line = lax.broadcasted_iota(jnp.int32, (lines, lat_dev), 0) & (GROUP - 1)
-    for group in range(waves // GROUP):
+    for group in range(table.shape[0] // GROUP):
         values = []
-        for part in range(2):
-            begin = part * wave_dev + first + group * GROUP
+        for begin in (first + group * GROUP, rows // 2 + first + group * GROUP):
             span = slice(begin, begin + GROUP)
-            values.append(
-                (keep[span] + recv[span]) - mean * (wet_keep[span] + wet_recv[span])
-            )
+            wet_span = slice(rows + begin, rows + begin + GROUP)
+            values.append((keep[span] + recv[span]) - mean * (wet_keep[span] + recv[wet_span]))
         value = jnp.concatenate(values, axis=0)
         result = None
         for step in range(0, GROUP, 2):
-            wave = group * GROUP + step
             left = jnp.concatenate(
                 [
                     jnp.where(line == step, value, 0.0).astype(bf16),
@@ -357,43 +401,41 @@
             )
             term = lax.dot_general(
                 left,
-                pair(legendre, wave),
+                pair(table, group * GROUP + step),
                 (((1,), (1,)), ((), ())),
                 preferred_element_type=f32,
             )
             result = term if result is None else result + term
-        out[group * lines : (group + 1) * lines] = result.astype(out.dtype)
-
-
-def synthesis_kernel(sizes, own, recv, love, legendre, *rest):
-    first, waves, wave_dev = sizes
+        for target in (out, *sent):
+            target[group * lines : (group + 1) * lines] = result.astype(target.dtype)
+
+
+def synthesis_kernel(sizes, own, recv, love, table, *rest):
+    first, wave_dev = sizes
     out = rest[-1]
+    lead = rest[:-1]
     lat_dev = out.shape[1]
     lines = 2 * GROUP
     line = lax.broadcasted_iota(jnp.int32, (lines, lat_dev), 0) & (GROUP - 1)
     base = lax.axis_index("lon") * wave_dev + first
     real, imag = [], []
-    for group in range(waves // GROUP):
+    for group in range(table.shape[0] // GROUP):
         span = slice(group * lines, (group + 1) * lines)
         total = own[span].astype(f32) + recv[span].astype(f32)
         scaled = (love[...] * total).astype(bf16)
         result = None
         for step in range(0, GROUP, 2):
-            both = jnp.dot(
-                scaled,
-                pair(legendre, group * GROUP + step),
-                preferred_element_type=f32,
-            )
+            both = jnp.dot(scaled, pair(table, group * GROUP + step), preferred_element_type=f32)
             left, right = both[:, :lat_dev], both[:, lat_dev:]
             result = left if result is None else jnp.where(line == step, left, result)
             result = jnp.where(line == step + 1, right, result)
         result = jnp.where(base + group * GROUP + line == 0, 1.0, 2.0) * result
         real.append(result[:GROUP])
         imag.append(result[GROUP:])
-    if len(rest) == 2:
-        half = rest[0].shape[0] // 2
-        real.insert(0, rest[0][:half])
-        imag.insert(0, rest[0][half:])
+    if lead:
+        half = lead[0].shape[0] // 2
+        real.insert(0, lead[0][:half])
+        imag.insert(0, lead[0][half:])
     out[...] = jnp.concatenate(real + imag, axis=0).astype(out.dtype)
 
 
@@ -438,7 +480,7 @@
 
     own, near, away, *strips = call(
         pack_kernel,
-        [shaped(6, lon_dev, lat_dev), strip, strip] + [strip] * (1 if lat_count == 2 else 2),
+        [shaped(6, lon_dev, lat_dev), shaped(6 + lon_dev // MARGIN, MARGIN, LANES), strip] + [strip] * (1 if lat_count == 2 else 2),
         in_specs=[hbm] * 6,
         scratch=[
             pltpu.VMEM((lon_dev, lat_dev), jnp.int32),
@@ -478,23 +520,23 @@
     lines = chunk * lon_count
     half = lines // 2
     wide = lon_dev + 2 * MARGIN
+    table = stay_put(legendre)
     table_shape = pltpu.VMEM((wave_dev // 2, *legendre.shape[1:]), bf16)
-    forward, inverse, wet_keep, wet_send, forcing, latitude, love, counts, table_0 = call(
+    forward, inverse, wet_pair, forcing, latitude, love, counts, table_0 = call(
         functools.partial(
             table_kernel, (lon_dev, lat_dev, total_cols, total_rows, wave_dev, tuple(gens))
         ),
         [
             shaped(lines, 2 * lon_dev, dtype=bf16),
             shaped(2 * lon_dev, lines, dtype=bf16),
-            shaped(half, lat_dev),
-            shaped(half, lat_dev),
+            shaped(2 * lon_dev, lat_dev, dtype=bf16),
             shaped(SUBSTEPS, wide, 2 * lat_dev),
             shaped(3, 8, 2 * lat_dev),
             shaped(1, degrees),
             shaped(*wet_counts.shape, dtype=jnp.int32),
             table_shape,
         ],
-        in_specs=[hbm] * 5 + [vmem],
+        in_specs=[hbm] * 5 + [vmem] * 2,
         scratch=[
             pltpu.VMEM((1, len(frequencies)), f32),
             pltpu.VMEM((1, len(frequencies)), f32),
@@ -507,19 +549,15 @@
         stay_put(tide_phase[None]),
         stay_put(love_factor[None]),
         stay_put(wet_counts),
-        stay_put(legendre),
+        table,
         own,
+        near,
     )
 
     def swap(cells, gen):
         return lax.ppermute(cells, "lon", [(i, i ^ gen) for i in range(lon_count)])
 
-    wet_recv = swap(wet_send, gens[0])
-    for gen in gens[1:]:
-        part = wet_keep.shape[0] // 2
-        wet_send = wet_keep[part:] + wet_recv[part:]
-        wet_keep = wet_keep[:part] + wet_recv[:part]
-        wet_recv = swap(wet_send, gen)
+    wet_far = swap(wet_pair, gens[1])
 
     height, east_new, north_new, wet_height, wet_sum, table_1 = call(
         functools.partial(step_kernel, lat_count),
@@ -530,24 +568,41 @@
             pltpu.VMEM((3, wide, 2 * lat_dev), f32),
             pltpu.SemaphoreType.DMA((4,)),
         ],
-    )(own, near, away, *strips, forcing, latitude, stay_put(legendre))
+    )(own, near, away, *strips, forcing, latitude, table)
 
     keep, send = call(
         fourier_kernel, [shaped(half, lat_dev), shaped(half + 8, lat_dev)]
     )(wet_height, wet_sum, forward)
     recv = swap(send, gens[0])
+    wet_keep, wet_send = call(
+        functools.partial(mask_kernel, (lon_dev, total_cols, wave_dev, tuple(gens))),
+        [shaped(half // 4, lat_dev)] * 2,
+    )(wet_pair, wet_far)
+    wet_recv = swap(wet_send, gens[2])
     level = wet_sum + recv[half:]
-    joined = lat_count == 2 and bits > 1
-    for place, gen in enumerate(gens[1:]):
+    joined = lat_count == 2
+    part = half // 2
+    send = jnp.concatenate([keep[part:] + recv[part:half], level], axis=0)
+    keep = keep[:part] + recv[:part]
+    recv = swap(send, gens[1])
+    arrived = recv[part:]
+    if joined:
+        arrived = arrived + shift(level, None, stay)
+        arrived = arrived + shift(level, None, lambda b: b ^ gens[1])
+    level = level + arrived
+    for place, gen in enumerate(gens[2:]):
         part = keep.shape[0] // 2
-        send = jnp.concatenate([keep[part:] + recv[part : 2 * part], level], axis=0)
+        sends = [keep[part:] + recv[part : 2 * part]]
         keep = keep[:part] + recv[:part]
-        recv = swap(send, gen)
-        arrived = recv[part:]
-        if place == 0 and joined:
-            arrived = arrived + shift(level, None, stay)
-            arrived = arrived + shift(level, None, lambda b: b ^ gen)
-        level = level + arrived
+        if place > 0:
+            sends.append(wet_keep[part:] + wet_recv[part : 2 * part])
+            wet_keep = wet_keep[:part] + wet_recv[:part]
+        recv = swap(jnp.concatenate([*sends, level], axis=0), gen)
+        if place > 0:
+            wet_recv = recv[part : 2 * part]
+            level = level + recv[2 * part :]
+        else:
+            level = level + recv[part:]
     if not joined:
         for b in range(lat_bits):
             level = level + lax.ppermute(
@@ -559,22 +614,23 @@
     waves = wave_dev // parts
     sums = []
     for piece in range(parts):
-        mine = call(
-            functools.partial(analysis_kernel, (piece * waves, waves, wave_dev)),
-            shaped(2 * waves, degrees),
-            in_specs=[vmem] * 7,
-        )(keep, recv, level, counts, wet_keep, wet_recv, tables[piece])
+        mine, moving = call(
+            functools.partial(analysis_kernel, piece * waves),
+            [shaped(2 * waves, degrees), shaped(2 * waves, degrees, dtype=bf16)],
+            in_specs=[vmem] * 6,
+        )(keep, recv, wet_keep, level, counts, tables[piece])
         for b in range(lat_bits):
-            other = lax.ppermute(mine, "lat", [(i, i ^ (1 << b)) for i in range(lat_count)])
+            other = lax.ppermute(moving, "lat", [(i, i ^ (1 << b)) for i in range(lat_count)])
             if b < lat_bits - 1:
-                mine = mine + other
+                mine = mine + other.astype(f32)
+                moving = mine.astype(bf16)
         sums.append((mine, other))
     spectra = ()
     for piece in range(parts):
         last = piece == parts - 1
         spectra = (
             call(
-                functools.partial(synthesis_kernel, (piece * waves, waves, wave_dev)),
+                functools.partial(synthesis_kernel, (piece * waves, wave_dev)),
                 shaped(2 * waves * (piece + 1), lat_dev, dtype=bf16 if last else f32),
                 in_specs=[vmem] * (4 + len(spectra)),
             )(*sums[piece], love, tables[piece], *spectra),

time: 65.7 us -> 64.6 us (0.983)
  waiting for transfers between devices: 34.1 us -> 28.3 us
  starting transfers between devices: 18.9 us -> 23.1 us
    ppermute x12 -> x10, starting transfers between devices: 7.43 us -> 11.4 us  [swap(): return lax.ppermute(cells, 'lon', [(i, i ^ gen) for i in range(lon_count)])]
    ppermute x12 -> x10, waiting for transfers between devices: 23 us -> 20.1 us  [swap(): return lax.ppermute(cells, 'lon', [(i, i ^ gen) for i in range(lon_count)])]
    ppermute x2, waiting for transfers between devices: 4.39 us -> 2.3 us  [shards(): lax.ppermute(moving, 'lat', [(i, i ^ 1 << b) for i in range(lat_count)])]
    ppermute x7, waiting for transfers between devices: 6.77 us -> 5.89 us  [shift(): return lax.ppermute(cells, ('lat', 'lon'), pairs)]
    pallas_call x5 -> x6, Pallas kernels: 5.02 us -> 5.66 us  [the longest x2 2.48 us: shards(): call(functools.partial(analysis_kernel, piece * waves), [shaped(2 * waves...]
  transfers between devices with their start and end apart: 21 -> 19, of which waited for: 15 -> 13; matrix products, arithmetic and copies ran while one was open for 0% -> 0% of each run, Pallas kernels for 7% -> 8%
where the time goes in v1:
time: 64.6 us; the launch traced here: 64.4 us
  waiting for transfers between devices  28.3 us (44%)
  starting transfers between devices  23.1 us (36%)
  Pallas kernels  12.1 us (19%)
  between operations  0.75 us (1%)
    ppermute x10, waiting for transfers between devices, swap(): return lax.ppermute(cells, 'lon', [(i, i ^ gen) for i in range(lon_count)])  20.1 us
    ppermute x10, starting transfers between devices, swap(): return lax.ppermute(cells, 'lon', [(i, i ^ gen) for i in range(lon_count)])  11.4 us
    ppermute x7, starting transfers between devices, shift(): return lax.ppermute(cells, ('lat', 'lon'), pairs)  9.64 us
    ppermute x7, waiting for transfers between devices, shift(): return lax.ppermute(cells, ('lat', 'lon'), pairs)  5.89 us
    pallas_call x1, Pallas kernels, shards(): call(functools.partial(step_kernel, lat_count), [shaped(lon_dev, lat_dev)...  2.89 us
    pallas_call x2, Pallas kernels, shards(): call(functools.partial(analysis_kernel, piece * waves), [shaped(2 * waves...  2.48 us
    pallas_call x1, Pallas kernels, shards(): call(functools.partial(table_kernel, (lon_dev, lat_dev, total_cols, total...  2.37 us
    ppermute x2, waiting for transfers between devices, shards(): lax.ppermute(moving, 'lat', [(i, i ^ 1 << b) for i in range(lat_count)])  2.3 us
  transfers between devices with their start and end apart: 19, of which 13 were waited for; matrix products, arithmetic and copies ran while one was open for 0% of the time, Pallas kernels for 8%

profile of v1, /device:TPU:0, one launch (start us, length us, event | category | flops | bytes accessed | tf_op | source)
XLA Modules:
  0.0 64.4 jit_solution(16300760792157896219)
XLA Ops:
  0.6 1.2 %shard_map.138 = (f32[6,128,128]{2,1,0:T(8,128)S(1)}, f32[22,8,128]{2,1,0:T(8,128)S(1)}, f32[6,8,128]{2,1,0:T(8,128)S(1)}, f32[6,8,128]{2,1,0:T(8,128)S(1)}) custom-call(f32[128,128]{1,0:T(8,128)} %sea.1, f32[128,128]{1,0:T(8,128)} %east.1, f32[128,128]{1,0:T(8,128)} %north.1, f32[128,128]{1,0:T(8,128)} %depth.1, s32[128,128]{1,0:T(8,128)} %mask.1, ...), custom_call_target="tpu_custom_call" | custom-call | tf_op jit(solution)/shard_map/pallas_call | solution.py:481
  1.9 0.6 collective-permute-start
  2.4 5.6 %collective-permute-start.1 = (f32[6,8,128]{2,1,0:T(8,128)S(1)}, f32[6,8,128]{2,1,0:T(8,128)S(1)}, u32[]{:S(2)}, u32[]{:S(2)}) collective-permute-start(f32[6,8,128]{2,1,0:T(8,128)S(1)} %get-tuple-element.32), channel_id=1, source_target_pairs={{0,15},{1,2},{2,1},{3,4},{4,3},{5,6},{6,5},{7,8},{8,7},{9,10},{10,... | collective-permute-start | bytes 73736 | tf_op jit(solution)/shard_map/ppermute | solution.py:508
  8.1 1.0 %collective-permute-start.4 = (f32[6,8,128]{2,1,0:T(8,128)S(1)}, f32[6,8,128]{2,1,0:T(8,128)S(1)}, u32[]{:S(2)}, u32[]{:S(2)}) collective-permute-start(f32[6,8,128]{2,1,0:T(8,128)S(1)} %get-tuple-element.33), channel_id=1, source_target_pairs={{0,31},{1,18},{2,17},{3,20},{4,19},{5,22},{6,21},{7,24},{8,23},{9,... | collective-permute-start | bytes 73736 | tf_op jit(solution)/shard_map/ppermute | solution.py:508
  9.0 0.0 collective-permute-start.3
  9.0 0.6 collective-permute-start.2
  9.6 0.0 collective-permute-done.near
  9.6 2.4 %shard_map.139 = (bf16[1024,256]{1,0:T(8,128)(2,1)S(1)}, bf16[256,1024]{1,0:T(8,128)(2,1)S(1)}, bf16[256,128]{1,0:T(8,128)(2,1)S(1)}, f32[4,144,256]{2,1,0:T(8,1...) custom-call(f32[1,8]{1,0:T(1,128)} %bitcast.4, ...), custom_call_target="tpu_custom_call" | custom-call | tf_op jit(solution)/shard_map/pallas_call | solution.py:525
  12.0 0.0 collective-permute-done.1.away
  12.0 2.9 %collective-permute-done.4.rest_2_ = f32[6,8,128]{2,1,0:T(8,128)S(1)} collective-permute-done((f32[6,8,128]{2,1,0:T(8,128)S(1)}, f32[6,8,128]{2,1,0:T(8,128)S(1)}, u32[]{:S(2)}, u32[]{:S(2)}) %collective-permute-start.4) | collective-permute-done | bytes 24608 | tf_op jit(solution)/shard_map/ppermute | solution.py:508
  14.9 0.0 collective-permute-done.3.rest_1_
  14.9 0.0 collective-permute-done.2.rest_0_
  14.9 2.9 %shard_map.140 = (f32[128,128]{1,0:T(8,128)}, f32[128,128]{1,0:T(8,128)}, f32[128,128]{1,0:T(8,128)}, f32[128,128]{1,0:T(8,128)S(1)}, f32[8,128]{1,0:T(8,128)S(1)}, /*index=5*/bf16[16,1024,128]{2,1,0:T(8,128)(2,1)S(1)}) custom-call(f32[6,128,128]{2,1,0:T(8,128)S(1)} %get-tuple-element.30.own, f32[22,8,128]{2,1,0:T(8,128)S(1)} %collective-permute-done.near, ...), custom_call_target="tpu_custom_call" | custom-call | tf_op jit(solution)/shard_map/pallas_call | solution.py:562
  17.8 0.3 shard_map.141
  18.1 0.1 collective-permute-start.5
  18.2 1.5 %collective-permute-done.5 = f32[520,128]{1,0:T(8,128)S(1)} collective-permute-done((f32[520,128]{1,0:T(8,128)S(1)}, f32[520,128]{1,0:T(8,128)S(1)}, u32[]{:S(2)}, u32[]{:S(2)}) %collective-permute-start.5) | collective-permute-done | bytes 266272 | tf_op jit(solution)/shard_map/ppermute | solution.py:558
  19.8 0.1 collective-permute-start.6
  19.9 1.7 %collective-permute-start.10 = (bf16[256,128]{1,0:T(8,128)(2,1)S(1)}, bf16[256,128]{1,0:T(8,128)(2,1)S(1)}, u32[]{:S(2)}, u32[]{:S(2)}) collective-permute-start(bf16[256,128]{1,0:T(8,128)(2,1)S(1)} %get-tuple-element.45.pair), channel_id=1, source_target_pairs={{0,3},{1,2},{2,1},{3,0},{4,7},{5,6},{6,5},{7,4},{8,11},{9,10},{10,... | collective-permute-start | bytes 196616 | tf_op jit(solution)/shard_map/ppermute | solution.py:558
  21.6 5.2 %collective-permute-done.10.far = bf16[256,128]{1,0:T(8,128)(2,1)S(1)} collective-permute-done((bf16[256,128]{1,0:T(8,128)(2,1)S(1)}, bf16[256,128]{1,0:T(8,128)(2,1)S(1)}, u32[]{:S(2)}, u32[]{:S(2)}) %collective-permute-start.10) | collective-permute-done | bytes 65568 | tf_op jit(solution)/shard_map/ppermute | solution.py:558
  26.8 0.6 shard_map.142
  27.4 0.1 collective-permute-start.11
  27.5 1.3 %collective-permute-start.8 = (f32[8,128]{1,0:T(8,128)S(1)}, f32[8,128]{1,0:T(8,128)S(1)}, u32[]{:S(2)}, u32[]{:S(2)}) collective-permute-start(f32[8,128]{1,0:T(8,128)S(1)} %slice_add_fusion.11), channel_id=1, source_target_pairs={{0,19},{1,18},{2,17},{3,16},{4,23},{5,22},{6,21},{7,20},{8,27},{9,... | collective-permute-start | bytes 12296 | tf_op jit(solution)/shard_map/ppermute | solution.py:508
  28.8 0.6 collective-permute-start.7
  29.5 0.0 collective-permute-done.6
  29.5 2.0 %collective-permute-done.8 = f32[8,128]{1,0:T(8,128)S(1)} collective-permute-done((f32[8,128]{1,0:T(8,128)S(1)}, f32[8,128]{1,0:T(8,128)S(1)}, u32[]{:S(2)}, u32[]{:S(2)}) %collective-permute-start.8) | collective-permute-done | bytes 4128 | tf_op jit(solution)/shard_map/ppermute | solution.py:508
  31.5 0.9 %collective-permute-done.7 = f32[8,128]{1,0:T(8,128)S(1)} collective-permute-done((f32[8,128]{1,0:T(8,128)S(1)}, f32[8,128]{1,0:T(8,128)S(1)}, u32[]{:S(2)}, u32[]{:S(2)}) %collective-permute-start.7) | collective-permute-done | bytes 4128 | tf_op jit(solution)/shard_map/ppermute | solution.py:508
  32.5 1.7 %collective-permute-start.9 = (f32[136,128]{1,0:T(8,128)S(1)}, f32[136,128]{1,0:T(8,128)S(1)}, u32[]{:S(2)}, u32[]{:S(2)}) collective-permute-start(f32[136,128]{1,0:T(8,128)S(1)} %pad_maximum_fusion.2), channel_id=1, source_target_pairs={{0,9},{1,8},{2,11},{3,10},{4,13},{5,12},{6,15},{7,14},{8,1},{9,0},... | collective-permute-start | bytes 208904 | tf_op jit(solution)/shard_map/ppermute | solution.py:558
  34.2 0.0 collective-permute-done.11
  34.2 3.5 %collective-permute-done.9 = f32[136,128]{1,0:T(8,128)S(1)} collective-permute-done((f32[136,128]{1,0:T(8,128)S(1)}, f32[136,128]{1,0:T(8,128)S(1)}, u32[]{:S(2)}, u32[]{:S(2)}) %collective-permute-start.9) | collective-permute-done | bytes 69664 | tf_op jit(solution)/shard_map/ppermute | solution.py:558
  37.7 1.5 %collective-permute-start.12 = (f32[136,128]{1,0:T(8,128)S(1)}, f32[136,128]{1,0:T(8,128)S(1)}, u32[]{:S(2)}, u32[]{:S(2)}) collective-permute-start(f32[136,128]{1,0:T(8,128)S(1)} %pad_maximum_fusion.3), channel_id=1, source_target_pairs={{0,5},{1,4},{2,7},{3,6},{4,1},{5,0},{6,3},{7,2},{8,13},{9,12},{10,... | collective-permute-start | bytes 208904 | tf_op jit(solution)/shard_map/ppermute | solution.py:558
  39.2 2.3 %collective-permute-done.12.recv = f32[136,128]{1,0:T(8,128)S(1)} collective-permute-done((f32[136,128]{1,0:T(8,128)S(1)}, f32[136,128]{1,0:T(8,128)S(1)}, u32[]{:S(2)}, u32[]{:S(2)}) %collective-permute-start.12) | collective-permute-done | bytes 69664 | tf_op jit(solution)/shard_map/ppermute | solution.py:558
  41.5 1.2 %shard_map.144 = (f32[32,1024]{1,0:T(8,128)S(1)}, bf16[32,1024]{1,0:T(8,128)(2,1)S(1)}) custom-call(f32[64,128]{1,0:T(8,128)S(1)} %get-tuple-element.61.keep, f32[136,128]{1,0:T(8,128)S(1)} %collective-permute-done.12.recv, f32[64,128]{1,0:T(8,128)S(1)} %get-tuple-element.62.wet_keep, f32[8,128]{1,0:T(8,128)S(1)} %slice_add_fusion.8.wet_sum, ...), custom_call_target="tpu_custom_call" | custom-call | tf_op jit(solution)/shard_map/pallas_call | solution.py:617
  42.8 0.3 collective-permute-start.14
  43.1 1.2 %shard_map.143 = (f32[32,1024]{1,0:T(8,128)S(1)}, bf16[32,1024]{1,0:T(8,128)(2,1)S(1)}) custom-call(f32[64,128]{1,0:T(8,128)S(1)} %get-tuple-element.61.keep, f32[136,128]{1,0:T(8,128)S(1)} %collective-permute-done.12.recv, f32[64,128]{1,0:T(8,128)S(1)} %get-tuple-element.62.wet_keep, f32[8,128]{1,0:T(8,128)S(1)} %slice_add_fusion.8.wet_sum, ...), custom_call_target="tpu_custom_call" | custom-call | tf_op jit(solution)/shard_map/pallas_call | solution.py:617
  44.3 1.8 %collective-permute-start.13 = (bf16[32,1024]{1,0:T(8,128)(2,1)S(1)}, bf16[32,1024]{1,0:T(8,128)(2,1)S(1)}, u32[]{:S(2)}, u32[]{:S(2)}) collective-permute-start(bf16[32,1024]{1,0:T(8,128)(2,1)S(1)} %get-tuple-element.51), channel_id=1, source_target_pairs={{0,16},{16,0},{1,17},{17,1},{2,18},{18,2},{3,19},{19,3},{4,20},{20... | collective-permute-start | bytes 196616 | tf_op jit(solution)/shard_map/ppermute | solution.py:623
  46.1 1.5 %collective-permute-done.14.recv = bf16[32,1024]{1,0:T(8,128)(2,1)S(1)} collective-permute-done((bf16[32,1024]{1,0:T(8,128)(2,1)S(1)}, bf16[32,1024]{1,0:T(8,128)(2,1)S(1)}, u32[]{:S(2)}, u32[]{:S(2)}) %collective-permute-start.14) | collective-permute-done | bytes 65568 | tf_op jit(solution)/shard_map/ppermute | solution.py:623
  47.5 0.7 %shard_map.145.rest_0_ = f32[32,128]{1,0:T(8,128)S(1)} custom-call(f32[32,1024]{1,0:T(8,128)S(1)} %get-tuple-element.54.own, bf16[32,1024]{1,0:T(8,128)(2,1)S(1)} %collective-permute-done.14.recv, f32[1,1024]{1,0:T(1,128)S(1)} %get-tuple-element.52.love, bf16[16,1024,128]{2,1,0:T(8,128)(2,1)S(1)} %get-tuple-element.53.table), custom_call_target="tpu_custom_call" | custom-call | tf_op jit(solution)/shard_map/pallas_call | solution.py:632
  48.2 0.8 %collective-permute-done.13.recv = bf16[32,1024]{1,0:T(8,128)(2,1)S(1)} collective-permute-done((bf16[32,1024]{1,0:T(8,128)(2,1)S(1)}, bf16[32,1024]{1,0:T(8,128)(2,1)S(1)}, u32[]{:S(2)}, u32[]{:S(2)}) %collective-permute-start.13) | collective-permute-done | bytes 65568 | tf_op jit(solution)/shard_map/ppermute | solution.py:623
  49.0 0.7 %shard_map.146 = bf16[64,128]{1,0:T(8,128)(2,1)S(1)} custom-call(f32[32,1024]{1,0:T(8,128)S(1)} %get-tuple-element.50.own, bf16[32,1024]{1,0:T(8,128)(2,1)S(1)} %collective-permute-done.13.recv, f32[1,1024]{1,0:T(1,128)S(1)} %get-tuple-element.52.love, bf16[16,1024,128]{2,1,0:T(8,128)(2,1)S(1)} %get-tuple-element.49.table, f32[32,128]{1,0:T(8,128)S(1)} %shard_map.145.rest_0_), custom_call_target="tpu_custom_call" | custom-call | tf_op jit(solution)/shard_map/pallas_call | solution.py:632
  49.7 0.5 collective-permute-start.15
  50.2 2.7 %collective-permute-done.15 = bf16[64,128]{1,0:T(8,128)(2,1)S(1)} collective-permute-done((bf16[64,128]{1,0:T(8,128)(2,1)S(1)}, bf16[64,128]{1,0:T(8,128)(2,1)S(1)}, u32[]{:S(2)}, u32[]{:S(2)}) %collective-permute-start.15) | collective-permute-done | bytes 16416 | tf_op jit(solution)/shard_map/ppermute | solution.py:558
  52.9 2.8 %collective-permute-start.16 = (bf16[128,128]{1,0:T(8,128)(2,1)S(1)}, bf16[128,128]{1,0:T(8,128)(2,1)S(1)}, u32[]{:S(2)}, u32[]{:S(2)}) collective-permute-start(bf16[128,128]{1,0:T(8,128)(2,1)S(1)} %pad_maximum_fusion.5), channel_id=1, source_target_pairs={{0,9},{1,8},{2,11},{3,10},{4,13},{5,12},{6,15},{7,14},{8,1},{9,0},... | collective-permute-start | bytes 98312 | tf_op jit(solution)/shard_map/ppermute | solution.py:558
  55.7 1.6 %collective-permute-done.16 = bf16[128,128]{1,0:T(8,128)(2,1)S(1)} collective-permute-done((bf16[128,128]{1,0:T(8,128)(2,1)S(1)}, bf16[128,128]{1,0:T(8,128)(2,1)S(1)}, u32[]{:S(2)}, u32[]{:S(2)}) %collective-permute-start.16) | collective-permute-done | bytes 32800 | tf_op jit(solution)/shard_map/ppermute | solution.py:558
  57.3 2.6 %collective-permute-start.17 = (bf16[256,128]{1,0:T(8,128)(2,1)S(1)}, bf16[256,128]{1,0:T(8,128)(2,1)S(1)}, u32[]{:S(2)}, u32[]{:S(2)}) collective-permute-start(bf16[256,128]{1,0:T(8,128)(2,1)S(1)} %pad_maximum_fusion.4), channel_id=1, source_target_pairs={{0,3},{1,2},{2,1},{3,0},{4,7},{5,6},{6,5},{7,4},{8,11},{9,10},{10,... | collective-permute-start | bytes 196616 | tf_op jit(solution)/shard_map/ppermute | solution.py:558
  59.9 2.2 %collective-permute-done.17 = bf16[256,128]{1,0:T(8,128)(2,1)S(1)} collective-permute-done((bf16[256,128]{1,0:T(8,128)(2,1)S(1)}, bf16[256,128]{1,0:T(8,128)(2,1)S(1)}, u32[]{:S(2)}, u32[]{:S(2)}) %collective-permute-start.17) | collective-permute-done | bytes 65568 | tf_op jit(solution)/shard_map/ppermute | solution.py:558
  62.1 0.3 collective-permute-start.18
  62.5 1.1 %collective-permute-done.18.far = bf16[512,128]{1,0:T(8,128)(2,1)S(1)} collective-permute-done((bf16[512,128]{1,0:T(8,128)(2,1)S(1)}, bf16[512,128]{1,0:T(8,128)(2,1)S(1)}, u32[]{:S(2)}, u32[]{:S(2)}) %collective-permute-start.18) | collective-permute-done | bytes 131104 | tf_op jit(solution)/shard_map/ppermute | solution.py:558
  63.5 0.9 %shard_map.147 = f32[128,128]{1,0:T(8,128)} custom-call(bf16[256,1024]{1,0:T(8,128)(2,1)S(1)} %get-tuple-element.39.inverse, bf16[512,128]{1,0:T(8,128)(2,1)S(1)} %pad_maximum_fusion.1.near, bf16[512,128]{1,0:T(8,128)(2,1)S(1)} %collective-permute-done.18.far), custom_call_target="tpu_custom_call" | custom-call | tf_op jit(solution)/shard_map/pallas_call | solution.py:642
  (14 shorter events, 0.1 us)
Async XLA Ops:
  1.9 7.7 %collective-permute-start = (f32[22,8,128]{2,1,0:T(8,128)S(1)}, f32[22,8,128]{2,1,0:T(8,128)S(1)}, u32[]{:S(2)}, u32[]{:S(2)}) collective-permute-start(f32[22,8,128]{2,1,0:T(8,128)S(1)} %get-tuple-element.31), channel_id=1, source_target_pairs={{0,1},{1,0},{2,3},{3,2},{4,5},{5,4},{6,7},{7,6},{8,9},{9,8},{10,11... | collective-permute-start | bytes 270344 | tf_op jit(solution)/shard_map/ppermute | solution.py:508
  2.4 9.5 %collective-permute-start.1 = (f32[6,8,128]{2,1,0:T(8,128)S(1)}, f32[6,8,128]{2,1,0:T(8,128)S(1)}, u32[]{:S(2)}, u32[]{:S(2)}) collective-permute-start(f32[6,8,128]{2,1,0:T(8,128)S(1)} %get-tuple-element.32), channel_id=1, source_target_pairs={{0,15},{1,2},{2,1},{3,4},{4,3},{5,6},{6,5},{7,8},{8,7},{9,10},{10,... | collective-permute-start | bytes 73736 | tf_op jit(solution)/shard_map/ppermute | solution.py:508
  8.1 6.8 %collective-permute-start.4 = (f32[6,8,128]{2,1,0:T(8,128)S(1)}, f32[6,8,128]{2,1,0:T(8,128)S(1)}, u32[]{:S(2)}, u32[]{:S(2)}) collective-permute-start(f32[6,8,128]{2,1,0:T(8,128)S(1)} %get-tuple-element.33), channel_id=1, source_target_pairs={{0,31},{1,18},{2,17},{3,20},{4,19},{5,22},{6,21},{7,24},{8,23},{9,... | collective-permute-start | bytes 73736 | tf_op jit(solution)/shard_map/ppermute | solution.py:508
  9.0 5.9 %collective-permute-start.3 = (f32[6,8,128]{2,1,0:T(8,128)S(1)}, f32[6,8,128]{2,1,0:T(8,128)S(1)}, u32[]{:S(2)}, u32[]{:S(2)}) collective-permute-start(f32[6,8,128]{2,1,0:T(8,128)S(1)} %get-tuple-element.33), channel_id=1, source_target_pairs={{0,17},{1,16},{2,19},{3,18},{4,21},{5,20},{6,23},{7,22},{8,25},{9,... | collective-permute-start | bytes 73736 | tf_op jit(solution)/shard_map/ppermute | solution.py:508
  9.0 5.9 %collective-permute-start.2 = (f32[6,8,128]{2,1,0:T(8,128)S(1)}, f32[6,8,128]{2,1,0:T(8,128)S(1)}, u32[]{:S(2)}, u32[]{:S(2)}) collective-permute-start(f32[6,8,128]{2,1,0:T(8,128)S(1)} %get-tuple-element.33), channel_id=1, source_target_pairs={{0,16},{1,17},{2,18},{3,19},{4,20},{5,21},{6,22},{7,23},{8,24},{9,... | collective-permute-start | bytes 73736 | tf_op jit(solution)/shard_map/ppermute | solution.py:508
  18.1 1.6 %collective-permute-start.5 = (f32[520,128]{1,0:T(8,128)S(1)}, f32[520,128]{1,0:T(8,128)S(1)}, u32[]{:S(2)}, u32[]{:S(2)}) collective-permute-start(f32[520,128]{1,0:T(8,128)S(1)} %get-tuple-element.44), channel_id=1, source_target_pairs={{0,1},{1,0},{2,3},{3,2},{4,5},{5,4},{6,7},{7,6},{8,9},{9,8},{10,11... | collective-permute-start | bytes 798728 | tf_op jit(solution)/shard_map/ppermute | solution.py:558
  19.8 9.7 %collective-permute-start.6 = (f32[264,128]{1,0:T(8,128)S(1)}, f32[264,128]{1,0:T(8,128)S(1)}, u32[]{:S(2)}, u32[]{:S(2)}) collective-permute-start(f32[264,128]{1,0:T(8,128)S(1)} %pad_maximum_fusion), channel_id=1, source_target_pairs={{0,3},{1,2},{2,1},{3,0},{4,7},{5,6},{6,5},{7,4},{8,11},{9,10},{10,... | collective-permute-start | bytes 405512 | tf_op jit(solution)/shard_map/ppermute | solution.py:558
  19.9 7.0 %collective-permute-start.10 = (bf16[256,128]{1,0:T(8,128)(2,1)S(1)}, bf16[256,128]{1,0:T(8,128)(2,1)S(1)}, u32[]{:S(2)}, u32[]{:S(2)}) collective-permute-start(bf16[256,128]{1,0:T(8,128)(2,1)S(1)} %get-tuple-element.45.pair), channel_id=1, source_target_pairs={{0,3},{1,2},{2,1},{3,0},{4,7},{5,6},{6,5},{7,4},{8,11},{9,10},{10,... | collective-permute-start | bytes 196616 | tf_op jit(solution)/shard_map/ppermute | solution.py:558
  27.4 6.7 %collective-permute-start.11 = (f32[128,128]{1,0:T(8,128)S(1)}, f32[128,128]{1,0:T(8,128)S(1)}, u32[]{:S(2)}, u32[]{:S(2)}) collective-permute-start(f32[128,128]{1,0:T(8,128)S(1)} %get-tuple-element.47), channel_id=1, source_target_pairs={{0,9},{1,8},{2,11},{3,10},{4,13},{5,12},{6,15},{7,14},{8,1},{9,0},... | collective-permute-start | bytes 196616 | tf_op jit(solution)/shard_map/ppermute | solution.py:558
  27.5 4.0 %collective-permute-start.8 = (f32[8,128]{1,0:T(8,128)S(1)}, f32[8,128]{1,0:T(8,128)S(1)}, u32[]{:S(2)}, u32[]{:S(2)}) collective-permute-start(f32[8,128]{1,0:T(8,128)S(1)} %slice_add_fusion.11), channel_id=1, source_target_pairs={{0,19},{1,18},{2,17},{3,16},{4,23},{5,22},{6,21},{7,20},{8,27},{9,... | collective-permute-start | bytes 12296 | tf_op jit(solution)/shard_map/ppermute | solution.py:508
  28.8 3.6 %collective-permute-start.7 = (f32[8,128]{1,0:T(8,128)S(1)}, f32[8,128]{1,0:T(8,128)S(1)}, u32[]{:S(2)}, u32[]{:S(2)}) collective-permute-start(f32[8,128]{1,0:T(8,128)S(1)} %slice_add_fusion.11), channel_id=1, source_target_pairs={{0,16},{1,17},{2,18},{3,19},{4,20},{5,21},{6,22},{7,23},{8,24},{9,... | collective-permute-start | bytes 12296 | tf_op jit(solution)/shard_map/ppermute | solution.py:508
  32.5 5.3 %collective-permute-start.9 = (f32[136,128]{1,0:T(8,128)S(1)}, f32[136,128]{1,0:T(8,128)S(1)}, u32[]{:S(2)}, u32[]{:S(2)}) collective-permute-start(f32[136,128]{1,0:T(8,128)S(1)} %pad_maximum_fusion.2), channel_id=1, source_target_pairs={{0,9},{1,8},{2,11},{3,10},{4,13},{5,12},{6,15},{7,14},{8,1},{9,0},... | collective-permute-start | bytes 208904 | tf_op jit(solution)/shard_map/ppermute | solution.py:558
  37.7 3.8 %collective-permute-start.12 = (f32[136,128]{1,0:T(8,128)S(1)}, f32[136,128]{1,0:T(8,128)S(1)}, u32[]{:S(2)}, u32[]{:S(2)}) collective-permute-start(f32[136,128]{1,0:T(8,128)S(1)} %pad_maximum_fusion.3), channel_id=1, source_target_pairs={{0,5},{1,4},{2,7},{3,6},{4,1},{5,0},{6,3},{7,2},{8,13},{9,12},{10,... | collective-permute-start | bytes 208904 | tf_op jit(solution)/shard_map/ppermute | solution.py:558
  42.8 4.8 %collective-permute-start.14 = (bf16[32,1024]{1,0:T(8,128)(2,1)S(1)}, bf16[32,1024]{1,0:T(8,128)(2,1)S(1)}, u32[]{:S(2)}, u32[]{:S(2)}) collective-permute-start(bf16[32,1024]{1,0:T(8,128)(2,1)S(1)} %get-tuple-element.55), channel_id=1, source_target_pairs={{0,16},{16,0},{1,17},{17,1},{2,18},{18,2},{3,19},{19,3},{4,20},{20... | collective-permute-start | bytes 196616 | tf_op jit(solution)/shard_map/ppermute | solution.py:623
  44.3 4.7 %collective-permute-start.13 = (bf16[32,1024]{1,0:T(8,128)(2,1)S(1)}, bf16[32,1024]{1,0:T(8,128)(2,1)S(1)}, u32[]{:S(2)}, u32[]{:S(2)}) collective-permute-start(bf16[32,1024]{1,0:T(8,128)(2,1)S(1)} %get-tuple-element.51), channel_id=1, source_target_pairs={{0,16},{16,0},{1,17},{17,1},{2,18},{18,2},{3,19},{19,3},{4,20},{20... | collective-permute-start | bytes 196616 | tf_op jit(solution)/shard_map/ppermute | solution.py:623
  49.7 3.2 %collective-permute-start.15 = (bf16[64,128]{1,0:T(8,128)(2,1)S(1)}, bf16[64,128]{1,0:T(8,128)(2,1)S(1)}, u32[]{:S(2)}, u32[]{:S(2)}) collective-permute-start(bf16[64,128]{1,0:T(8,128)(2,1)S(1)} %shard_map.146), channel_id=1, source_target_pairs={{0,5},{1,4},{2,7},{3,6},{4,1},{5,0},{6,3},{7,2},{8,13},{9,12},{10,... | collective-permute-start | bytes 49160 | tf_op jit(solution)/shard_map/ppermute | solution.py:558
  52.9 4.4 %collective-permute-start.16 = (bf16[128,128]{1,0:T(8,128)(2,1)S(1)}, bf16[128,128]{1,0:T(8,128)(2,1)S(1)}, u32[]{:S(2)}, u32[]{:S(2)}) collective-permute-start(bf16[128,128]{1,0:T(8,128)(2,1)S(1)} %pad_maximum_fusion.5), channel_id=1, source_target_pairs={{0,9},{1,8},{2,11},{3,10},{4,13},{5,12},{6,15},{7,14},{8,1},{9,0},... | collective-permute-start | bytes 98312 | tf_op jit(solution)/shard_map/ppermute | solution.py:558
  57.3 4.8 %collective-permute-start.17 = (bf16[256,128]{1,0:T(8,128)(2,1)S(1)}, bf16[256,128]{1,0:T(8,128)(2,1)S(1)}, u32[]{:S(2)}, u32[]{:S(2)}) collective-permute-start(bf16[256,128]{1,0:T(8,128)(2,1)S(1)} %pad_maximum_fusion.4), channel_id=1, source_target_pairs={{0,3},{1,2},{2,1},{3,0},{4,7},{5,6},{6,5},{7,4},{8,11},{9,10},{10,... | collective-permute-start | bytes 196616 | tf_op jit(solution)/shard_map/ppermute | solution.py:558
  62.1 1.4 %collective-permute-start.18 = (bf16[512,128]{1,0:T(8,128)(2,1)S(1)}, bf16[512,128]{1,0:T(8,128)(2,1)S(1)}, u32[]{:S(2)}, u32[]{:S(2)}) collective-permute-start(bf16[512,128]{1,0:T(8,128)(2,1)S(1)} %pad_maximum_fusion.1.near), channel_id=1, source_target_pairs={{0,1},{1,0},{2,3},{3,2},{4,5},{5,4},{6,7},{7,6},{8,9},{9,8},{10,11... | collective-permute-start | bytes 393224 | tf_op jit(solution)/shard_map/ppermute | solution.py:558

commit v2 on v1

--- a/solution.py
+++ b/solution.py
@@ -41,7 +41,7 @@
     return jax.ShapeDtypeStruct(dims, dtype)
 
 
-def fetch(source, first, target, sems):
+def fetch_kernel(first, source, target, turned, sems):
     pieces = sems.shape[0]
     span = target.shape[0] // pieces
     copies = []
@@ -49,7 +49,12 @@
         taken = source.at[pl.ds(first + piece * span, span)]
         placed = target.at[pl.ds(piece * span, span)]
         copies.append(pltpu.make_async_copy(taken, placed, sems.at[piece]))
-    return copies
+    for copy in copies:
+        copy.start()
+    for piece, copy in enumerate(copies):
+        copy.wait()
+        for wave in range(piece * span, (piece + 1) * span):
+            turned[wave] = target[wave].T
 
 
 def pack_kernel(sea, east, north, depth, mask, loading, own, near, away, *rest):
@@ -97,13 +102,24 @@
     return owner
 
 
+def join_kernel(near, away, *rest):
+    sources, targets = rest[: len(rest) // 2], rest[len(rest) // 2 :]
+    lat_dev = near.shape[2]
+    lane = lax.broadcasted_iota(jnp.int32, (MARGIN, lat_dev), 1)
+    edge = jnp.logical_or(lane < MARGIN, lane >= lat_dev - MARGIN)
+    for index in range(6):
+        corner = jnp.where(edge, near[index], pltpu.roll(away[index], lat_dev // 2, axis=1))
+        for source, target in zip(sources, targets):
+            target[index] = source[index]
+            target[6 + index] = corner
+
+
 def table_kernel(
     sizes,
     amp_in,
     phase_in,
     love_in,
     counts_in,
-    legendre,
     own,
     near,
     forward,
@@ -113,12 +129,10 @@
     latitude_out,
     love_out,
     counts_out,
-    table,
     amp,
     phase,
     outer,
     sems,
-    table_sems,
 ):
     lon_dev, lat_dev, total_cols, total_rows, wave_dev, gens = sizes
     pairs = ((amp_in, amp), (phase_in, phase), (love_in, love_out), (counts_in, counts_out))
@@ -126,8 +140,7 @@
         pltpu.make_async_copy(source, target, sems.at[place])
         for place, (source, target) in enumerate(pairs)
     ]
-    large = fetch(legendre, 0, table, table_sems)
-    for copy in copies + large:
+    for copy in copies:
         copy.start()
     lon_index = lax.axis_index("lon")
     lat_index = lax.axis_index("lat")
@@ -221,8 +234,6 @@
         along = cos_two * semi_real[at] - sin_two * semi_imag[at]
         across = cos_one * diurnal_real[at] - sin_one * diurnal_imag[at]
         forcing[k] = along * semi[0:1] + across * diurnal[0:1]
-    for copy in large:
-        copy.wait()
 
 
 def mask_kernel(sizes, pair, far, keep, send):
@@ -262,26 +273,19 @@
 
 
 def step_kernel(count, own, near, away, *rest):
-    strips = rest[: 3 if count == 2 else 6]
+    facing = rest[: 1 if count == 2 else 2]
     (
         forcing,
         latitude,
-        legendre,
         height_out,
         east_out,
         north_out,
         wet_height,
         wet_sum,
-        table,
         state,
         static,
-        table_sems,
-    ) = rest[len(strips) :]
-    copies = fetch(legendre, table.shape[0], table, table_sems)
-    for copy in copies:
-        copy.start()
-    above = strips[:3]
-    below = strips[-3:]
+    ) = rest[len(facing) :]
+    above, below = facing[0], facing[-1]
     lon_dev, lat_dev = own.shape[1:]
     wide = lon_dev + 2 * MARGIN
     lanes = 2 * lat_dev
@@ -290,24 +294,30 @@
     has_top = lat_index < count - 1
     has_bottom = lat_index > 0
     middle = jnp.zeros((lat_dev - 2 * MARGIN, lon_dev), f32)
-    lane = lax.broadcasted_iota(jnp.int32, (MARGIN, lon_dev), 1)
-    use_near = (lane < MARGIN) != odd
+    lane = lax.broadcasted_iota(jnp.int32, (MARGIN, lat_dev), 1)
+    at_top = jnp.logical_and(lane < MARGIN, has_top)
+    at_bottom = jnp.logical_and(lane >= lat_dev - MARGIN, has_bottom)
 
     fields = []
     for index in range(6):
         cells = own[index]
-        north_rows = jnp.where(has_top, above[0][index], 0.0)
-        south_rows = jnp.where(has_bottom, below[0][index], 0.0)
+        north_rows = jnp.where(has_top, above[index], 0.0)
+        south_rows = jnp.where(has_bottom, below[index], 0.0)
         side = jnp.concatenate([north_rows, middle, south_rows], axis=0).T
-        north_rows = jnp.where(use_near, above[1][index], above[2][index])
-        south_rows = jnp.where(use_near, below[1][index], below[2][index])
-        north_rows = jnp.where(has_top, north_rows, 0.0)
-        south_rows = jnp.where(has_bottom, south_rows, 0.0)
-        corner = jnp.concatenate([north_rows, middle, south_rows], axis=0).T
+        corners = []
+        for turn in (0, lat_dev // 2):
+            north_part, south_part = above[6 + index], below[6 + index]
+            if turn:
+                north_part = pltpu.roll(north_part, turn, axis=1)
+                south_part = pltpu.roll(south_part, turn, axis=1)
+            part = jnp.where(at_bottom, south_part, 0.0)
+            corners.append(jnp.where(at_top, north_part, part))
+        corner_east = jnp.where(odd, corners[1], corners[0])
+        corner_west = jnp.where(odd, corners[0], corners[1])
         from_east = jnp.where(odd, away[index], near[index])
         from_west = jnp.where(odd, near[index], away[index])
         left = jnp.concatenate([cells, from_east, from_west], axis=0)
-        right = jnp.concatenate([side, corner[:MARGIN], corner[lon_dev - MARGIN :]], axis=0)
+        right = jnp.concatenate([side, corner_east, corner_west], axis=0)
         fields.append(jnp.concatenate([left, right], axis=1))
     for index in range(3):
         state[index] = fields[index]
@@ -347,8 +357,6 @@
     wet_height[...] = product
     level = jnp.sum(jnp.sum(product, axis=0, keepdims=True), axis=1, keepdims=True)
     wet_sum[...] = jnp.broadcast_to(level, wet_sum.shape)
-    for copy in copies:
-        copy.wait()
 
 
 def fourier_kernel(wet_height, wet_sum, forward, keep, send):
@@ -399,12 +407,9 @@
                 ],
                 axis=1,
             )
-            term = lax.dot_general(
-                left,
-                pair(table, group * GROUP + step),
-                (((1,), (1,)), ((), ())),
-                preferred_element_type=f32,
-            )
+            wave = group * GROUP + step
+            right = jnp.concatenate([table[wave], table[wave + 1]], axis=0)
+            term = jnp.dot(left, right, preferred_element_type=f32)
             result = term if result is None else result + term
         for target in (out, *sent):
             target[group * lines : (group + 1) * lines] = result.astype(target.dtype)
@@ -507,22 +512,14 @@
                     pairs.append((a * lon_count + b, target * lon_count + move(b)))
         return lax.ppermute(cells, ("lat", "lon"), pairs)
 
-    moves = (stay, nearby, beyond)
     away = shift(away, 0, beyond)
-    sources = [(None, strips[0])] if lat_count == 2 else [(-1, strips[1]), (1, strips[0])]
-    strips = []
-    for lat_step, source in sources:
-        for move in moves:
-            strips.append(shift(source, lat_step, move))
     near = shift(near, 0, nearby)
 
     chunk = 2 * wave_dev
     lines = chunk * lon_count
     half = lines // 2
     wide = lon_dev + 2 * MARGIN
-    table = stay_put(legendre)
-    table_shape = pltpu.VMEM((wave_dev // 2, *legendre.shape[1:]), bf16)
-    forward, inverse, wet_pair, forcing, latitude, love, counts, table_0 = call(
+    forward, inverse, wet_pair, forcing, latitude, love, counts = call(
         functools.partial(
             table_kernel, (lon_dev, lat_dev, total_cols, total_rows, wave_dev, tuple(gens))
         ),
@@ -534,14 +531,12 @@
             shaped(3, 8, 2 * lat_dev),
             shaped(1, degrees),
             shaped(*wet_counts.shape, dtype=jnp.int32),
-            table_shape,
         ],
-        in_specs=[hbm] * 5 + [vmem] * 2,
+        in_specs=[hbm] * 4 + [vmem] * 2,
         scratch=[
             pltpu.VMEM((1, len(frequencies)), f32),
             pltpu.VMEM((1, len(frequencies)), f32),
             pltpu.VMEM((2, lon_count, lon_dev), f32),
-            pltpu.SemaphoreType.DMA((4,)),
             pltpu.SemaphoreType.DMA((4,)),
         ],
     )(
@@ -549,7 +544,6 @@
         stay_put(tide_phase[None]),
         stay_put(love_factor[None]),
         stay_put(wet_counts),
-        table,
         own,
         near,
     )
@@ -559,16 +553,17 @@
 
     wet_far = swap(wet_pair, gens[1])
 
-    height, east_new, north_new, wet_height, wet_sum, table_1 = call(
+    strips = call(join_kernel, [shaped(12, MARGIN, LANES)] * len(strips))(near, away, *strips)
+    if lat_count == 2:
+        facing = [shift(strips[0], None, stay)]
+    else:
+        facing = [shift(strips[1], -1, stay), shift(strips[0], 1, stay)]
+    height, east_new, north_new, wet_height, wet_sum = call(
         functools.partial(step_kernel, lat_count),
-        [shaped(lon_dev, lat_dev)] * 4 + [shaped(8, lat_dev), table_shape],
-        in_specs=[vmem] * (5 + len(strips)) + [hbm],
-        scratch=[
-            pltpu.VMEM((3, wide, 2 * lat_dev), f32),
-            pltpu.VMEM((3, wide, 2 * lat_dev), f32),
-            pltpu.SemaphoreType.DMA((4,)),
-        ],
-    )(own, near, away, *strips, forcing, latitude, table)
+        [shaped(lon_dev, lat_dev)] * 4 + [shaped(8, lat_dev)],
+        in_specs=[vmem] * (5 + len(facing)),
+        scratch=[pltpu.VMEM((3, wide, 2 * lat_dev), f32)] * 2,
+    )(own, near, away, *facing, forcing, latitude)
 
     keep, send = call(
         fourier_kernel, [shaped(half, lat_dev), shaped(half + 8, lat_dev)]
@@ -587,7 +582,7 @@
     recv = swap(send, gens[1])
     arrived = recv[part:]
     if joined:
-        arrived = arrived + shift(level, None, stay)
+        arrived = arrived + shift(level, None, nearby)
         arrived = arrived + shift(level, None, lambda b: b ^ gens[1])
     level = level + arrived
     for place, gen in enumerate(gens[2:]):
@@ -609,16 +604,28 @@
                 level, "lat", [(i, i ^ (1 << b)) for i in range(lat_count)]
             )
 
-    tables = (table_0, table_1)
-    parts = len(tables)
+    parts = 2
     waves = wave_dev // parts
+    tables = []
+    for piece in range(parts):
+        tables.append(
+            call(
+                functools.partial(fetch_kernel, piece * waves),
+                [
+                    pltpu.VMEM((waves, degrees, lat_dev), bf16),
+                    pltpu.VMEM((waves, lat_dev, degrees), bf16),
+                ],
+                in_specs=[hbm],
+                scratch=[pltpu.SemaphoreType.DMA((4,))],
+            )(stay_put(legendre))
+        )
     sums = []
     for piece in range(parts):
         mine, moving = call(
             functools.partial(analysis_kernel, piece * waves),
             [shaped(2 * waves, degrees), shaped(2 * waves, degrees, dtype=bf16)],
             in_specs=[vmem] * 6,
-        )(keep, recv, wet_keep, level, counts, tables[piece])
+        )(keep, recv, wet_keep, level, counts, tables[piece][1])
         for b in range(lat_bits):
             other = lax.ppermute(moving, "lat", [(i, i ^ (1 << b)) for i in range(lat_count)])
             if b < lat_bits - 1:
@@ -633,7 +640,7 @@
                 functools.partial(synthesis_kernel, (piece * waves, wave_dev)),
                 shaped(2 * waves * (piece + 1), lat_dev, dtype=bf16 if last else f32),
                 in_specs=[vmem] * (4 + len(spectra)),
-            )(*sums[piece], love, tables[piece], *spectra),
+            )(*sums[piece], love, tables[piece][0], *spectra),
         )
     near = spectra[0]
     for gen in gens[:0:-1]:

time: 64.6 us -> 65.9 us (1.020)
  Pallas kernels: 12.1 us -> 15.3 us
  starting transfers between devices: 23.1 us -> 20.5 us
  waiting for transfers between devices: 28.3 us -> 29.1 us
    pallas_call x0 -> x3, Pallas kernels: none -> 5.19 us  [the longest x2 5.12 us: shards(): call(functools.partial(fetch_kernel, piece * waves), [pltpu.VMEM((waves,...]
    ppermute x10, starting transfers between devices: 11.4 us -> 8.78 us  [swap(): return lax.ppermute(cells, 'lon', [(i, i ^ gen) for i in range(lon_count)])]
    ppermute x10, waiting for transfers between devices: 20.1 us -> 21.9 us  [swap(): return lax.ppermute(cells, 'lon', [(i, i ^ gen) for i in range(lon_count)])]
    pallas_call x2, Pallas kernels: 2.48 us -> 1.49 us  [shards(): call(functools.partial(analysis_kernel, piece * waves), [shaped(2 * waves...]
    ppermute x7 -> x5, waiting for transfers between devices: 5.89 us -> 4.99 us  [shift(): return lax.ppermute(cells, ('lat', 'lon'), pairs)]
    ppermute x7 -> x5, starting transfers between devices: 9.64 us -> 9.65 us  [shift(): return lax.ppermute(cells, ('lat', 'lon'), pairs)]
  transfers between devices with their start and end apart: 19 -> 17, of which waited for: 13 -> 12; matrix products, arithmetic and copies ran while one was open for 0% -> 0% of each run, Pallas kernels for 8% -> 14%
where the time goes in v2:
time: 65.9 us; the launch traced here: 65.7 us
  waiting for transfers between devices  29.1 us (44%)
  starting transfers between devices  20.5 us (31%)
  Pallas kernels  15.3 us (23%)
  between operations  0.76 us (1%)
    ppermute x10, waiting for transfers between devices, swap(): return lax.ppermute(cells, 'lon', [(i, i ^ gen) for i in range(lon_count)])  21.9 us
    ppermute x5, starting transfers between devices, shift(): return lax.ppermute(cells, ('lat', 'lon'), pairs)  9.65 us
    ppermute x10, starting transfers between devices, swap(): return lax.ppermute(cells, 'lon', [(i, i ^ gen) for i in range(lon_count)])  8.78 us
    pallas_call x2, Pallas kernels, shards(): call(functools.partial(fetch_kernel, piece * waves), [pltpu.VMEM((waves,...  5.12 us
    ppermute x5, waiting for transfers between devices, shift(): return lax.ppermute(cells, ('lat', 'lon'), pairs)  4.99 us
    pallas_call x1, Pallas kernels, shards(): call(functools.partial(step_kernel, lat_count), [shaped(lon_dev, lat_dev)...  2.35 us
    ppermute x2, waiting for transfers between devices, shards(): lax.ppermute(moving, 'lat', [(i, i ^ 1 << b) for i in range(lat_count)])  2.22 us
    ppermute x2, starting transfers between devices, shards(): lax.ppermute(moving, 'lat', [(i, i ^ 1 << b) for i in range(lat_count)])  2.04 us
  transfers between devices with their start and end apart: 17, of which 12 were waited for; matrix products, arithmetic and copies ran while one was open for 0% of the time, Pallas kernels for 14%

profile of v2, /device:TPU:0, one launch (start us, length us, event | category | flops | bytes accessed | tf_op | source)
XLA Modules:
  0.0 65.7 jit_solution(17775010996007587437)
XLA Ops:
  0.6 1.2 %shard_map.138 = (f32[6,128,128]{2,1,0:T(8,128)S(1)}, f32[22,8,128]{2,1,0:T(8,128)S(1)}, f32[6,8,128]{2,1,0:T(8,128)S(1)}, f32[6,8,128]{2,1,0:T(8,128)S(1)}) custom-call(f32[128,128]{1,0:T(8,128)} %sea.1, f32[128,128]{1,0:T(8,128)} %east.1, f32[128,128]{1,0:T(8,128)} %north.1, f32[128,128]{1,0:T(8,128)} %depth.1, s32[128,128]{1,0:T(8,128)} %mask.1, ...), custom_call_target="tpu_custom_call" | custom-call | tf_op jit(solution)/shard_map/pallas_call | solution.py:486
  1.9 0.6 collective-permute-start
  2.4 5.6 %collective-permute-start.1 = (f32[6,8,128]{2,1,0:T(8,128)S(1)}, f32[6,8,128]{2,1,0:T(8,128)S(1)}, u32[]{:S(2)}, u32[]{:S(2)}) collective-permute-start(f32[6,8,128]{2,1,0:T(8,128)S(1)} %get-tuple-element.34), channel_id=1, source_target_pairs={{0,15},{1,2},{2,1},{3,4},{4,3},{5,6},{6,5},{7,8},{8,7},{9,10},{10,... | collective-permute-start | bytes 73736 | tf_op jit(solution)/shard_map/ppermute | solution.py:513
  8.1 1.5 %collective-permute-done.1.away = f32[6,8,128]{2,1,0:T(8,128)S(1)} collective-permute-done((f32[6,8,128]{2,1,0:T(8,128)S(1)}, f32[6,8,128]{2,1,0:T(8,128)S(1)}, u32[]{:S(2)}, u32[]{:S(2)}) %collective-permute-start.1) | collective-permute-done | bytes 24608 | tf_op jit(solution)/shard_map/ppermute | solution.py:513
  9.6 0.0 collective-permute-done.near
  9.6 0.1 shard_map.139
  9.7 1.5 %collective-permute-start.2 = (f32[12,8,128]{2,1,0:T(8,128)S(1)}, f32[12,8,128]{2,1,0:T(8,128)S(1)}, u32[]{:S(2)}, u32[]{:S(2)}) collective-permute-start(f32[12,8,128]{2,1,0:T(8,128)S(1)} %shard_map.139), channel_id=1, source_target_pairs={{0,16},{1,17},{2,18},{3,19},{4,20},{5,21},{6,22},{7,23},{8,24},{9,... | collective-permute-start | bytes 147464 | tf_op jit(solution)/shard_map/ppermute | solution.py:513
  11.2 1.8 %shard_map.140 = (bf16[1024,256]{1,0:T(8,128)(2,1)S(1)}, bf16[256,1024]{1,0:T(8,128)(2,1)S(1)}, bf16[256,128]{1,0:T(8,128)(2,1)S(1)}, f32[4,144,256]{2,1,0:T(8,1...) custom-call(f32[1,8]{1,0:T(1,128)} %bitcast.4, f32[1,8]{1,0:T(1,128)} %bitcast.5, ...), custom_call_target="tpu_custom_call" | custom-call | tf_op jit(solution)/shard_map/pallas_call | solution.py:522
  13.0 0.7 %collective-permute-done.2.rest_0_ = f32[12,8,128]{2,1,0:T(8,128)S(1)} collective-permute-done((f32[12,8,128]{2,1,0:T(8,128)S(1)}, f32[12,8,128]{2,1,0:T(8,128)S(1)}, u32[]{:S(2)}, u32[]{:S(2)}) %collective-permute-start.2) | collective-permute-done | bytes 49184 | tf_op jit(solution)/shard_map/ppermute | solution.py:513
  13.7 2.4 %shard_map.141 = (f32[128,128]{1,0:T(8,128)}, f32[128,128]{1,0:T(8,128)}, f32[128,128]{1,0:T(8,128)}, f32[128,128]{1,0:T(8,128)S(1)}, f32[8,128]{1,0:T(8,128)S(1)}) custom-call(f32[6,128,128]{2,1,0:T(8,128)S(1)} %get-tuple-element.32.own, f32[22,8,128]{2,1,0:T(8,128)S(1)} %collective-permute-done.near, f32[6,8,128]{2,1,0:T(8,128)S(1)} %collective-permute-done.1.away, ...), custom_call_target="tpu_custom_call" | custom-call | tf_op jit(solution)/shard_map/pallas_call | solution.py:561
  16.1 0.3 shard_map.142
  16.4 0.1 collective-permute-start.3
  16.5 1.5 %collective-permute-done.3 = f32[520,128]{1,0:T(8,128)S(1)} collective-permute-done((f32[520,128]{1,0:T(8,128)S(1)}, f32[520,128]{1,0:T(8,128)S(1)}, u32[]{:S(2)}, u32[]{:S(2)}) %collective-permute-start.3) | collective-permute-done | bytes 266272 | tf_op jit(solution)/shard_map/ppermute | solution.py:552
  18.1 0.1 collective-permute-start.4
  18.1 1.7 %collective-permute-start.8 = (bf16[256,128]{1,0:T(8,128)(2,1)S(1)}, bf16[256,128]{1,0:T(8,128)(2,1)S(1)}, u32[]{:S(2)}, u32[]{:S(2)}) collective-permute-start(bf16[256,128]{1,0:T(8,128)(2,1)S(1)} %get-tuple-element.47.pair), channel_id=1, source_target_pairs={{0,3},{1,2},{2,1},{3,0},{4,7},{5,6},{6,5},{7,4},{8,11},{9,10},{10,... | collective-permute-start | bytes 196616 | tf_op jit(solution)/shard_map/ppermute | solution.py:552
  19.9 5.2 %collective-permute-done.8.far = bf16[256,128]{1,0:T(8,128)(2,1)S(1)} collective-permute-done((bf16[256,128]{1,0:T(8,128)(2,1)S(1)}, bf16[256,128]{1,0:T(8,128)(2,1)S(1)}, u32[]{:S(2)}, u32[]{:S(2)}) %collective-permute-start.8) | collective-permute-done | bytes 65568 | tf_op jit(solution)/shard_map/ppermute | solution.py:552
  25.1 0.6 shard_map.143
  25.7 0.5 collective-permute-start.9
  26.2 1.6 %collective-permute-start.6 = (f32[8,128]{1,0:T(8,128)S(1)}, f32[8,128]{1,0:T(8,128)S(1)}, u32[]{:S(2)}, u32[]{:S(2)}) collective-permute-start(f32[8,128]{1,0:T(8,128)S(1)} %slice_add_fusion.11), channel_id=1, source_target_pairs={{0,19},{1,18},{2,17},{3,16},{4,23},{5,22},{6,21},{7,20},{8,27},{9,... | collective-permute-start | bytes 12296 | tf_op jit(solution)/shard_map/ppermute | solution.py:513
  27.9 0.3 collective-permute-start.5
  28.1 0.0 collective-permute-done.4
  28.2 2.0 %collective-permute-done.6 = f32[8,128]{1,0:T(8,128)S(1)} collective-permute-done((f32[8,128]{1,0:T(8,128)S(1)}, f32[8,128]{1,0:T(8,128)S(1)}, u32[]{:S(2)}, u32[]{:S(2)}) %collective-permute-start.6) | collective-permute-done | bytes 4128 | tf_op jit(solution)/shard_map/ppermute | solution.py:513
  30.1 0.8 %collective-permute-done.5 = f32[8,128]{1,0:T(8,128)S(1)} collective-permute-done((f32[8,128]{1,0:T(8,128)S(1)}, f32[8,128]{1,0:T(8,128)S(1)}, u32[]{:S(2)}, u32[]{:S(2)}) %collective-permute-start.5) | collective-permute-done | bytes 4128 | tf_op jit(solution)/shard_map/ppermute | solution.py:513
  30.9 1.6 %collective-permute-start.7 = (f32[136,128]{1,0:T(8,128)S(1)}, f32[136,128]{1,0:T(8,128)S(1)}, u32[]{:S(2)}, u32[]{:S(2)}) collective-permute-start(f32[136,128]{1,0:T(8,128)S(1)} %pad_maximum_fusion.2), channel_id=1, source_target_pairs={{0,9},{1,8},{2,11},{3,10},{4,13},{5,12},{6,15},{7,14},{8,1},{9,0},... | collective-permute-start | bytes 208904 | tf_op jit(solution)/shard_map/ppermute | solution.py:552
  32.5 0.0 collective-permute-done.9
  32.5 3.2 %collective-permute-done.7 = f32[136,128]{1,0:T(8,128)S(1)} collective-permute-done((f32[136,128]{1,0:T(8,128)S(1)}, f32[136,128]{1,0:T(8,128)S(1)}, u32[]{:S(2)}, u32[]{:S(2)}) %collective-permute-start.7) | collective-permute-done | bytes 69664 | tf_op jit(solution)/shard_map/ppermute | solution.py:552
  35.7 3.0 %collective-permute-start.10 = (f32[136,128]{1,0:T(8,128)S(1)}, f32[136,128]{1,0:T(8,128)S(1)}, u32[]{:S(2)}, u32[]{:S(2)}) collective-permute-start(f32[136,128]{1,0:T(8,128)S(1)} %pad_maximum_fusion.3), channel_id=1, source_target_pairs={{0,5},{1,4},{2,7},{3,6},{4,1},{5,0},{6,3},{7,2},{8,13},{9,12},{10,... | collective-permute-start | bytes 208904 | tf_op jit(solution)/shard_map/ppermute | solution.py:552
  38.7 2.6 %shard_map.146 = (bf16[16,1024,128]{2,1,0:T(8,128)(2,1)S(1)}, bf16[16,128,1024]{2,1,0:T(8,128)(2,1)S(1)}) custom-call(bf16[32,1024,128]{2,1,0:T(8,128)(2,1)} %source.3), custom_call_target="tpu_custom_call" | custom-call | tf_op jit(solution)/shard_map/pallas_call | solution.py:612
  41.3 0.0 collective-permute-done.10.recv
  41.3 0.7 %shard_map.147 = (f32[32,1024]{1,0:T(8,128)S(1)}, bf16[32,1024]{1,0:T(8,128)(2,1)S(1)}) custom-call(f32[64,128]{1,0:T(8,128)S(1)} %get-tuple-element.65.keep, f32[136,128]{1,0:T(8,128)S(1)} %collective-permute-done.10.recv, f32[64,128]{1,0:T(8,128)S(1)} %get-tuple-element.66.wet_keep, f32[8,128]{1,0:T(8,128)S(1)} %slice_add_fusion.8.wet_sum, ...), custom_call_target="tpu_custom_call" | custom-call | tf_op jit(solution)/shard_map/pallas_call | solution.py:624
  42.0 0.6 collective-permute-start.12
  42.7 2.6 %shard_map.144 = (bf16[16,1024,128]{2,1,0:T(8,128)(2,1)S(1)}, bf16[16,128,1024]{2,1,0:T(8,128)(2,1)S(1)}) custom-call(bf16[32,1024,128]{2,1,0:T(8,128)(2,1)} %source.3), custom_call_target="tpu_custom_call" | custom-call | tf_op jit(solution)/shard_map/pallas_call | solution.py:612
  45.2 0.7 %shard_map.145 = (f32[32,1024]{1,0:T(8,128)S(1)}, bf16[32,1024]{1,0:T(8,128)(2,1)S(1)}) custom-call(f32[64,128]{1,0:T(8,128)S(1)} %get-tuple-element.65.keep, f32[136,128]{1,0:T(8,128)S(1)} %collective-permute-done.10.recv, f32[64,128]{1,0:T(8,128)S(1)} %get-tuple-element.66.wet_keep, f32[8,128]{1,0:T(8,128)S(1)} %slice_add_fusion.8.wet_sum, ...), custom_call_target="tpu_custom_call" | custom-call | tf_op jit(solution)/shard_map/pallas_call | solution.py:624
  46.0 1.4 %collective-permute-start.11 = (bf16[32,1024]{1,0:T(8,128)(2,1)S(1)}, bf16[32,1024]{1,0:T(8,128)(2,1)S(1)}, u32[]{:S(2)}, u32[]{:S(2)}) collective-permute-start(bf16[32,1024]{1,0:T(8,128)(2,1)S(1)} %get-tuple-element.53), channel_id=1, source_target_pairs={{0,16},{16,0},{1,17},{17,1},{2,18},{18,2},{3,19},{19,3},{4,20},{20... | collective-permute-start | bytes 196616 | tf_op jit(solution)/shard_map/ppermute | solution.py:630
  47.4 0.0 collective-permute-done.12.recv
  47.4 0.7 %shard_map.148.rest_0_ = f32[32,128]{1,0:T(8,128)S(1)} custom-call(f32[32,1024]{1,0:T(8,128)S(1)} %get-tuple-element.57.own, bf16[32,1024]{1,0:T(8,128)(2,1)S(1)} %collective-permute-done.12.recv, f32[1,1024]{1,0:T(1,128)S(1)} %get-tuple-element.54.love, bf16[16,1024,128]{2,1,0:T(8,128)(2,1)S(1)} %get-tuple-element.59.table), custom_call_target="tpu_custom_call" | custom-call | tf_op jit(solution)/shard_map/pallas_call | solution.py:639
  48.0 2.2 %collective-permute-done.11.recv = bf16[32,1024]{1,0:T(8,128)(2,1)S(1)} collective-permute-done((bf16[32,1024]{1,0:T(8,128)(2,1)S(1)}, bf16[32,1024]{1,0:T(8,128)(2,1)S(1)}, u32[]{:S(2)}, u32[]{:S(2)}) %collective-permute-start.11) | collective-permute-done | bytes 65568 | tf_op jit(solution)/shard_map/ppermute | solution.py:630
  50.3 0.7 %shard_map.149 = bf16[64,128]{1,0:T(8,128)(2,1)S(1)} custom-call(f32[32,1024]{1,0:T(8,128)S(1)} %get-tuple-element.52.own, bf16[32,1024]{1,0:T(8,128)(2,1)S(1)} %collective-permute-done.11.recv, f32[1,1024]{1,0:T(1,128)S(1)} %get-tuple-element.54.love, bf16[16,1024,128]{2,1,0:T(8,128)(2,1)S(1)} %get-tuple-element.55.table, f32[32,128]{1,0:T(8,128)S(1)} %shard_map.148.rest_0_), custom_call_target="tpu_custom_call" | custom-call | tf_op jit(solution)/shard_map/pallas_call | solution.py:639
  50.9 0.0 collective-permute-start.13
  50.9 3.2 %collective-permute-done.13 = bf16[64,128]{1,0:T(8,128)(2,1)S(1)} collective-permute-done((bf16[64,128]{1,0:T(8,128)(2,1)S(1)}, bf16[64,128]{1,0:T(8,128)(2,1)S(1)}, u32[]{:S(2)}, u32[]{:S(2)}) %collective-permute-start.13) | collective-permute-done | bytes 16416 | tf_op jit(solution)/shard_map/ppermute | solution.py:552
  54.2 1.4 %collective-permute-start.14 = (bf16[128,128]{1,0:T(8,128)(2,1)S(1)}, bf16[128,128]{1,0:T(8,128)(2,1)S(1)}, u32[]{:S(2)}, u32[]{:S(2)}) collective-permute-start(bf16[128,128]{1,0:T(8,128)(2,1)S(1)} %pad_maximum_fusion.5), channel_id=1, source_target_pairs={{0,9},{1,8},{2,11},{3,10},{4,13},{5,12},{6,15},{7,14},{8,1},{9,0},... | collective-permute-start | bytes 98312 | tf_op jit(solution)/shard_map/ppermute | solution.py:552
  55.6 3.7 %collective-permute-done.14 = bf16[128,128]{1,0:T(8,128)(2,1)S(1)} collective-permute-done((bf16[128,128]{1,0:T(8,128)(2,1)S(1)}, bf16[128,128]{1,0:T(8,128)(2,1)S(1)}, u32[]{:S(2)}, u32[]{:S(2)}) %collective-permute-start.14) | collective-permute-done | bytes 32800 | tf_op jit(solution)/shard_map/ppermute | solution.py:552
  59.3 0.3 collective-permute-start.15
  59.6 3.8 %collective-permute-done.15 = bf16[256,128]{1,0:T(8,128)(2,1)S(1)} collective-permute-done((bf16[256,128]{1,0:T(8,128)(2,1)S(1)}, bf16[256,128]{1,0:T(8,128)(2,1)S(1)}, u32[]{:S(2)}, u32[]{:S(2)}) %collective-permute-start.15) | collective-permute-done | bytes 65568 | tf_op jit(solution)/shard_map/ppermute | solution.py:552
  63.4 0.2 collective-permute-start.16
  63.6 1.2 %collective-permute-done.16.far = bf16[512,128]{1,0:T(8,128)(2,1)S(1)} collective-permute-done((bf16[512,128]{1,0:T(8,128)(2,1)S(1)}, bf16[512,128]{1,0:T(8,128)(2,1)S(1)}, u32[]{:S(2)}, u32[]{:S(2)}) %collective-permute-start.16) | collective-permute-done | bytes 131104 | tf_op jit(solution)/shard_map/ppermute | solution.py:552
  64.8 0.9 %shard_map.150 = f32[128,128]{1,0:T(8,128)} custom-call(bf16[256,1024]{1,0:T(8,128)(2,1)S(1)} %get-tuple-element.41.inverse, bf16[512,128]{1,0:T(8,128)(2,1)S(1)} %pad_maximum_fusion.1.near, bf16[512,128]{1,0:T(8,128)(2,1)S(1)} %collective-permute-done.16.far), custom_call_target="tpu_custom_call" | custom-call | tf_op jit(solution)/shard_map/pallas_call | solution.py:649
  (14 shorter events, 0.1 us)
Async XLA Ops:
  1.9 7.7 %collective-permute-start = (f32[22,8,128]{2,1,0:T(8,128)S(1)}, f32[22,8,128]{2,1,0:T(8,128)S(1)}, u32[]{:S(2)}, u32[]{:S(2)}) collective-permute-start(f32[22,8,128]{2,1,0:T(8,128)S(1)} %get-tuple-element.33), channel_id=1, source_target_pairs={{0,1},{1,0},{2,3},{3,2},{4,5},{5,4},{6,7},{7,6},{8,9},{9,8},{10,11... | collective-permute-start | bytes 270344 | tf_op jit(solution)/shard_map/ppermute | solution.py:513
  2.4 7.1 %collective-permute-start.1 = (f32[6,8,128]{2,1,0:T(8,128)S(1)}, f32[6,8,128]{2,1,0:T(8,128)S(1)}, u32[]{:S(2)}, u32[]{:S(2)}) collective-permute-start(f32[6,8,128]{2,1,0:T(8,128)S(1)} %get-tuple-element.34), channel_id=1, source_target_pairs={{0,15},{1,2},{2,1},{3,4},{4,3},{5,6},{6,5},{7,8},{8,7},{9,10},{10,... | collective-permute-start | bytes 73736 | tf_op jit(solution)/shard_map/ppermute | solution.py:513
  9.7 4.1 %collective-permute-start.2 = (f32[12,8,128]{2,1,0:T(8,128)S(1)}, f32[12,8,128]{2,1,0:T(8,128)S(1)}, u32[]{:S(2)}, u32[]{:S(2)}) collective-permute-start(f32[12,8,128]{2,1,0:T(8,128)S(1)} %shard_map.139), channel_id=1, source_target_pairs={{0,16},{1,17},{2,18},{3,19},{4,20},{5,21},{6,22},{7,23},{8,24},{9,... | collective-permute-start | bytes 147464 | tf_op jit(solution)/shard_map/ppermute | solution.py:513
  16.4 1.6 %collective-permute-start.3 = (f32[520,128]{1,0:T(8,128)S(1)}, f32[520,128]{1,0:T(8,128)S(1)}, u32[]{:S(2)}, u32[]{:S(2)}) collective-permute-start(f32[520,128]{1,0:T(8,128)S(1)} %get-tuple-element.46), channel_id=1, source_target_pairs={{0,1},{1,0},{2,3},{3,2},{4,5},{5,4},{6,7},{7,6},{8,9},{9,8},{10,11... | collective-permute-start | bytes 798728 | tf_op jit(solution)/shard_map/ppermute | solution.py:552
  18.1 10.1 %collective-permute-start.4 = (f32[264,128]{1,0:T(8,128)S(1)}, f32[264,128]{1,0:T(8,128)S(1)}, u32[]{:S(2)}, u32[]{:S(2)}) collective-permute-start(f32[264,128]{1,0:T(8,128)S(1)} %pad_maximum_fusion), channel_id=1, source_target_pairs={{0,3},{1,2},{2,1},{3,0},{4,7},{5,6},{6,5},{7,4},{8,11},{9,10},{10,... | collective-permute-start | bytes 405512 | tf_op jit(solution)/shard_map/ppermute | solution.py:552
  18.1 7.0 %collective-permute-start.8 = (bf16[256,128]{1,0:T(8,128)(2,1)S(1)}, bf16[256,128]{1,0:T(8,128)(2,1)S(1)}, u32[]{:S(2)}, u32[]{:S(2)}) collective-permute-start(bf16[256,128]{1,0:T(8,128)(2,1)S(1)} %get-tuple-element.47.pair), channel_id=1, source_target_pairs={{0,3},{1,2},{2,1},{3,0},{4,7},{5,6},{6,5},{7,4},{8,11},{9,10},{10,... | collective-permute-start | bytes 196616 | tf_op jit(solution)/shard_map/ppermute | solution.py:552
  25.7 6.7 %collective-permute-start.9 = (f32[128,128]{1,0:T(8,128)S(1)}, f32[128,128]{1,0:T(8,128)S(1)}, u32[]{:S(2)}, u32[]{:S(2)}) collective-permute-start(f32[128,128]{1,0:T(8,128)S(1)} %get-tuple-element.49), channel_id=1, source_target_pairs={{0,9},{1,8},{2,11},{3,10},{4,13},{5,12},{6,15},{7,14},{8,1},{9,0},... | collective-permute-start | bytes 196616 | tf_op jit(solution)/shard_map/ppermute | solution.py:552
  26.2 3.9 %collective-permute-start.6 = (f32[8,128]{1,0:T(8,128)S(1)}, f32[8,128]{1,0:T(8,128)S(1)}, u32[]{:S(2)}, u32[]{:S(2)}) collective-permute-start(f32[8,128]{1,0:T(8,128)S(1)} %slice_add_fusion.11), channel_id=1, source_target_pairs={{0,19},{1,18},{2,17},{3,16},{4,23},{5,22},{6,21},{7,20},{8,27},{9,... | collective-permute-start | bytes 12296 | tf_op jit(solution)/shard_map/ppermute | solution.py:513
  27.9 3.0 %collective-permute-start.5 = (f32[8,128]{1,0:T(8,128)S(1)}, f32[8,128]{1,0:T(8,128)S(1)}, u32[]{:S(2)}, u32[]{:S(2)}) collective-permute-start(f32[8,128]{1,0:T(8,128)S(1)} %slice_add_fusion.11), channel_id=1, source_target_pairs={{0,17},{1,16},{2,19},{3,18},{4,21},{5,20},{6,23},{7,22},{8,25},{9,... | collective-permute-start | bytes 12296 | tf_op jit(solution)/shard_map/ppermute | solution.py:513
  30.9 4.8 %collective-permute-start.7 = (f32[136,128]{1,0:T(8,128)S(1)}, f32[136,128]{1,0:T(8,128)S(1)}, u32[]{:S(2)}, u32[]{:S(2)}) collective-permute-start(f32[136,128]{1,0:T(8,128)S(1)} %pad_maximum_fusion.2), channel_id=1, source_target_pairs={{0,9},{1,8},{2,11},{3,10},{4,13},{5,12},{6,15},{7,14},{8,1},{9,0},... | collective-permute-start | bytes 208904 | tf_op jit(solution)/shard_map/ppermute | solution.py:552
  35.7 5.5 %collective-permute-start.10 = (f32[136,128]{1,0:T(8,128)S(1)}, f32[136,128]{1,0:T(8,128)S(1)}, u32[]{:S(2)}, u32[]{:S(2)}) collective-permute-start(f32[136,128]{1,0:T(8,128)S(1)} %pad_maximum_fusion.3), channel_id=1, source_target_pairs={{0,5},{1,4},{2,7},{3,6},{4,1},{5,0},{6,3},{7,2},{8,13},{9,12},{10,... | collective-permute-start | bytes 208904 | tf_op jit(solution)/shard_map/ppermute | solution.py:552
  42.0 5.4 %collective-permute-start.12 = (bf16[32,1024]{1,0:T(8,128)(2,1)S(1)}, bf16[32,1024]{1,0:T(8,128)(2,1)S(1)}, u32[]{:S(2)}, u32[]{:S(2)}) collective-permute-start(bf16[32,1024]{1,0:T(8,128)(2,1)S(1)} %get-tuple-element.58), channel_id=1, source_target_pairs={{0,16},{16,0},{1,17},{17,1},{2,18},{18,2},{3,19},{19,3},{4,20},{20... | collective-permute-start | bytes 196616 | tf_op jit(solution)/shard_map/ppermute | solution.py:630
  46.0 4.3 %collective-permute-start.11 = (bf16[32,1024]{1,0:T(8,128)(2,1)S(1)}, bf16[32,1024]{1,0:T(8,128)(2,1)S(1)}, u32[]{:S(2)}, u32[]{:S(2)}) collective-permute-start(bf16[32,1024]{1,0:T(8,128)(2,1)S(1)} %get-tuple-element.53), channel_id=1, source_target_pairs={{0,16},{16,0},{1,17},{17,1},{2,18},{18,2},{3,19},{19,3},{4,20},{20... | collective-permute-start | bytes 196616 | tf_op jit(solution)/shard_map/ppermute | solution.py:630
  50.9 3.2 %collective-permute-start.13 = (bf16[64,128]{1,0:T(8,128)(2,1)S(1)}, bf16[64,128]{1,0:T(8,128)(2,1)S(1)}, u32[]{:S(2)}, u32[]{:S(2)}) collective-permute-start(bf16[64,128]{1,0:T(8,128)(2,1)S(1)} %shard_map.149), channel_id=1, source_target_pairs={{0,5},{1,4},{2,7},{3,6},{4,1},{5,0},{6,3},{7,2},{8,13},{9,12},{10,... | collective-permute-start | bytes 49160 | tf_op jit(solution)/shard_map/ppermute | solution.py:552
  54.2 5.1 %collective-permute-start.14 = (bf16[128,128]{1,0:T(8,128)(2,1)S(1)}, bf16[128,128]{1,0:T(8,128)(2,1)S(1)}, u32[]{:S(2)}, u32[]{:S(2)}) collective-permute-start(bf16[128,128]{1,0:T(8,128)(2,1)S(1)} %pad_maximum_fusion.5), channel_id=1, source_target_pairs={{0,9},{1,8},{2,11},{3,10},{4,13},{5,12},{6,15},{7,14},{8,1},{9,0},... | collective-permute-start | bytes 98312 | tf_op jit(solution)/shard_map/ppermute | solution.py:552
  59.3 4.1 %collective-permute-start.15 = (bf16[256,128]{1,0:T(8,128)(2,1)S(1)}, bf16[256,128]{1,0:T(8,128)(2,1)S(1)}, u32[]{:S(2)}, u32[]{:S(2)}) collective-permute-start(bf16[256,128]{1,0:T(8,128)(2,1)S(1)} %pad_maximum_fusion.4), channel_id=1, source_target_pairs={{0,3},{1,2},{2,1},{3,0},{4,7},{5,6},{6,5},{7,4},{8,11},{9,10},{10,... | collective-permute-start | bytes 196616 | tf_op jit(solution)/shard_map/ppermute | solution.py:552
  63.4 1.4 %collective-permute-start.16 = (bf16[512,128]{1,0:T(8,128)(2,1)S(1)}, bf16[512,128]{1,0:T(8,128)(2,1)S(1)}, u32[]{:S(2)}, u32[]{:S(2)}) collective-permute-start(bf16[512,128]{1,0:T(8,128)(2,1)S(1)} %pad_maximum_fusion.1.near), channel_id=1, source_target_pairs={{0,1},{1,0},{2,3},{3,2},{4,5},{5,4},{6,7},{7,6},{8,9},{9,8},{10,11... | collective-permute-start | bytes 393224 | tf_op jit(solution)/shard_map/ppermute | solution.py:552

commit v3 on v2

--- a/solution.py
+++ b/solution.py
@@ -57,7 +57,30 @@
             turned[wave] = target[wave].T
 
 
-def pack_kernel(sea, east, north, depth, mask, loading, own, near, away, *rest):
+def strip_kernel(sea, east, north, depth, mask, loading, near, away, wet, sems):
+    odd = lax.axis_index("lon") & 1
+    rows = sea.shape[0]
+    copies = [pltpu.make_async_copy(mask, wet, sems.at[0, 4])]
+    for side, target in enumerate((near, away)):
+        start = (1 - odd if side == 0 else odd) * (rows - MARGIN)
+        span = pl.ds(pl.multiple_of(start, MARGIN), MARGIN)
+        for index, source in ((0, sea), (1, east), (2, north), (3, depth), (5, loading)):
+            copies.append(
+                pltpu.make_async_copy(source.at[span], target.at[index], sems.at[side, index])
+            )
+    for copy in copies:
+        copy.start()
+    for copy in copies:
+        copy.wait()
+    for index in range(rows // MARGIN):
+        near[6 + index] = wet[index * MARGIN : (index + 1) * MARGIN].astype(f32)
+    first = near[6]
+    last = near[5 + rows // MARGIN]
+    near[4] = jnp.where(odd > 0, first, last)
+    away[4] = jnp.where(odd > 0, last, first)
+
+
+def pack_kernel(sea, east, north, depth, mask, loading, own, *rest):
     strips = rest[:-3]
     wet, sems, wet_sem = rest[-3:]
     copies = [pltpu.make_async_copy(mask, wet, wet_sem)]
@@ -65,22 +88,13 @@
         copies.append(pltpu.make_async_copy(ref, own.at[index], sems.at[index]))
     for copy in copies:
         copy.start()
-    odd = (lax.axis_index("lon") & 1) > 0
     lat_index = lax.axis_index("lat")
-    rows, lat_dev = sea.shape
+    lat_dev = sea.shape[1]
     for copy in copies:
         copy.wait()
-    filled = wet[...].astype(f32)
-    own[4] = filled
-    for index in range(rows // MARGIN):
-        near[6 + index] = filled[index * MARGIN : (index + 1) * MARGIN]
+    own[4] = wet[...].astype(f32)
     for index in range(6):
-        cells = own[index]
-        first = cells[:MARGIN]
-        last = cells[rows - MARGIN :]
-        near[index] = jnp.where(odd, first, last)
-        away[index] = jnp.where(odd, last, first)
-        turned = cells.T
+        turned = own[index].T
         top = turned[lat_dev - MARGIN :]
         bottom = turned[:MARGIN]
         if len(strips) == 1:
@@ -102,9 +116,15 @@
     return owner
 
 
-def join_kernel(near, away, *rest):
-    sources, targets = rest[: len(rest) // 2], rest[len(rest) // 2 :]
-    lat_dev = near.shape[2]
+def join_kernel(own, near, away, *rest):
+    count = len(rest) // 2
+    sources, targets, wet_pair = rest[:count], rest[count:-1], rest[-1]
+    lon_dev, lat_dev = own.shape[1:]
+    wet_pair[:lon_dev] = own[4].astype(bf16)
+    for index in range(0, lon_dev // MARGIN, 2):
+        both = jnp.concatenate([near[6 + index], near[7 + index]], axis=0)
+        at = lon_dev + index * MARGIN
+        wet_pair[at : at + 2 * MARGIN] = both.astype(bf16)
     lane = lax.broadcasted_iota(jnp.int32, (MARGIN, lat_dev), 1)
     edge = jnp.logical_or(lane < MARGIN, lane >= lat_dev - MARGIN)
     for index in range(6):
@@ -120,11 +140,8 @@
     phase_in,
     love_in,
     counts_in,
-    own,
-    near,
     forward,
     inverse,
-    wet_pair,
     forcing,
     latitude_out,
     love_out,
@@ -182,12 +199,6 @@
         return 0
 
     lax.fori_loop(0, chunks // block, fill, 0)
-    wet_pair[:lon_dev] = own[4].astype(bf16)
-    for index in range(0, lon_dev // MARGIN, 2):
-        both = jnp.concatenate([near[6 + index], near[7 + index]], axis=0)
-        at = lon_dev + index * MARGIN
-        wet_pair[at : at + 2 * MARGIN] = both.astype(bf16)
-
     wide = lon_dev + 2 * MARGIN
     lane = lax.broadcasted_iota(jnp.int32, (8, 2 * lat_dev), 1)
     row = jnp.where(lane < lat_dev + lat_dev // 2, lane, lane - 2 * lat_dev) + lat_index * lat_dev
@@ -272,23 +283,49 @@
     send[...] = result[half:]
 
 
+def along(f):
+    return pltpu.roll(f, f.shape[0] - 1, axis=0) - pltpu.roll(f, 1, axis=0)
+
+
+def across(f):
+    return pltpu.roll(f, f.shape[1] - 1, axis=1) - pltpu.roll(f, 1, axis=1)
+
+
+def rise(state, static, rows):
+    cosine, secant, _ = rows
+    depth = static[0]
+    divergence = (along(depth * state[1]) + across(depth * state[2] * cosine)) * 0.5 * secant
+    state[0] = state[0] - courant * divergence * static[1]
+
+
+def veer(state, static, forcing, rows):
+    _, secant, coriolis = rows
+    east = state[1]
+    north = state[2]
+    wet = static[1]
+    pressure = state[0] - forcing - static[2]
+    slope_east = along(pressure) * 0.5 * secant
+    slope_north = across(pressure) * 0.5
+    return (
+        wet * ((1.0 - friction) * east + courant * (coriolis * north - slope_east)),
+        wet * ((1.0 - friction) * north - courant * (coriolis * east + slope_north)),
+    )
+
+
 def step_kernel(count, own, near, away, *rest):
     facing = rest[: 1 if count == 2 else 2]
     (
         forcing,
         latitude,
-        height_out,
-        east_out,
-        north_out,
-        wet_height,
+        forward,
+        keep,
+        send,
         wet_sum,
         state,
         static,
     ) = rest[len(facing) :]
     above, below = facing[0], facing[-1]
     lon_dev, lat_dev = own.shape[1:]
-    wide = lon_dev + 2 * MARGIN
-    lanes = 2 * lat_dev
     lat_index = lax.axis_index("lat")
     odd = (lax.axis_index("lon") & 1) > 0
     has_top = lat_index < count - 1
@@ -323,57 +360,41 @@
         state[index] = fields[index]
         static[index] = fields[3 + index]
 
-    def along(f):
-        return pltpu.roll(f, wide - 1, axis=0) - pltpu.roll(f, 1, axis=0)
-
-    def across(f):
-        return pltpu.roll(f, lanes - 1, axis=1) - pltpu.roll(f, 1, axis=1)
-
-    cosine = latitude[0][0:1]
-    secant = latitude[1][0:1]
-    coriolis = latitude[2][0:1]
+    rows = tuple(latitude[index][0:1] for index in range(3))
 
     def substep(k, _):
-        east = state[1]
-        north = state[2]
-        depth = static[0]
-        wet = static[1]
-        divergence = (along(depth * east) + across(depth * north * cosine)) * 0.5 * secant
-        height = state[0] - courant * divergence * wet
-        state[0] = height
-        pressure = height - forcing[k] - static[2]
-        slope_east = along(pressure) * 0.5 * secant
-        slope_north = across(pressure) * 0.5
-        state[1] = wet * ((1.0 - friction) * east + courant * (coriolis * north - slope_east))
-        state[2] = wet * ((1.0 - friction) * north - courant * (coriolis * east + slope_north))
+        rise(state, static, rows)
+        state[1], state[2] = veer(state, static, forcing[k], rows)
         return 0
 
-    lax.fori_loop(0, SUBSTEPS, substep, 0)
-    core = state[0, :lon_dev, :lat_dev]
-    height_out[...] = core
-    east_out[...] = state[1, :lon_dev, :lat_dev]
-    north_out[...] = state[2, :lon_dev, :lat_dev]
-    product = core * own[4]
-    wet_height[...] = product
+    lax.fori_loop(0, SUBSTEPS - 1, substep, 0)
+    rise(state, static, rows)
+    product = state[0, :lon_dev, :lat_dev] * own[4]
     level = jnp.sum(jnp.sum(product, axis=0, keepdims=True), axis=1, keepdims=True)
-    wet_sum[...] = jnp.broadcast_to(level, wet_sum.shape)
-
-
-def fourier_kernel(wet_height, wet_sum, forward, keep, send):
-    high, low = split_bf16(wet_height[...])
-    top = jnp.concatenate([high, low], axis=1)
+    level = jnp.broadcast_to(level, wet_sum.shape)
+    wet_sum[...] = level
+    high, low = split_bf16(product)
+    upper = jnp.concatenate([high, low], axis=1)
     under = jnp.concatenate([high, jnp.zeros_like(low)], axis=1)
-    weights = jnp.concatenate([top, under], axis=0)
+    weights = jnp.concatenate([upper, under], axis=0)
     half = keep.shape[0]
-    cols = wet_height.shape[1]
 
     def transform(span):
         both = jnp.dot(forward[span], weights, preferred_element_type=f32)
-        return both[:, :cols] + both[:, cols:]
+        return both[:, :lat_dev] + both[:, lat_dev:]
 
     send[:half] = transform(slice(half, 2 * half))
-    send[half:] = wet_sum[...]
+    send[half:] = level
     keep[...] = transform(slice(0, half))
+
+
+def finish_kernel(state, static, forcing, latitude, height_out, east_out, north_out):
+    lon_dev, lat_dev = height_out.shape
+    rows = tuple(latitude[index][0:1] for index in range(3))
+    east, north = veer(state, static, forcing[SUBSTEPS - 1], rows)
+    height_out[...] = state[0, :lon_dev, :lat_dev]
+    east_out[...] = east[:lon_dev, :lat_dev]
+    north_out[...] = north[:lon_dev, :lat_dev]
 
 
 GROUP = 8
@@ -383,7 +404,13 @@
     return jnp.concatenate([legendre[wave], legendre[wave + 1]], axis=1)
 
 
-def analysis_kernel(first, keep, recv, wet_keep, wet_sum, wet_counts, table, out, *sent):
+def locate(table, second, wave):
+    held = table.shape[0]
+    return (table, wave) if wave < held else (second, wave - held)
+
+
+def analysis_kernel(sizes, keep, recv, wet_keep, wet_sum, wet_counts, table, second, *outs):
+    first, waves = sizes
     lat_dev = keep.shape[1]
     rows = keep.shape[0]
     counts = wet_counts[...].astype(f32)
@@ -391,7 +418,7 @@
     mean = wet_sum[0:1, 0:1] / total
     lines = 2 * GROUP
     line = lax.broadcasted_iota(jnp.int32, (lines, lat_dev), 0) & (GROUP - 1)
-    for group in range(table.shape[0] // GROUP):
+    for group in range(waves // GROUP):
         values = []
         for begin in (first + group * GROUP, rows // 2 + first + group * GROUP):
             span = slice(begin, begin + GROUP)
@@ -407,16 +434,16 @@
                 ],
                 axis=1,
             )
-            wave = group * GROUP + step
-            right = jnp.concatenate([table[wave], table[wave + 1]], axis=0)
+            source, wave = locate(table, second, first + group * GROUP + step)
+            right = jnp.concatenate([source[wave], source[wave + 1]], axis=0)
             term = jnp.dot(left, right, preferred_element_type=f32)
             result = term if result is None else result + term
-        for target in (out, *sent):
+        for target in outs:
             target[group * lines : (group + 1) * lines] = result.astype(target.dtype)
 
 
-def synthesis_kernel(sizes, own, recv, love, table, *rest):
-    first, wave_dev = sizes
+def synthesis_kernel(sizes, own, recv, love, table, second, *rest):
+    first, waves, wave_dev = sizes
     out = rest[-1]
     lead = rest[:-1]
     lat_dev = out.shape[1]
@@ -424,13 +451,14 @@
     line = lax.broadcasted_iota(jnp.int32, (lines, lat_dev), 0) & (GROUP - 1)
     base = lax.axis_index("lon") * wave_dev + first
     real, imag = [], []
-    for group in range(table.shape[0] // GROUP):
+    for group in range(waves // GROUP):
         span = slice(group * lines, (group + 1) * lines)
         total = own[span].astype(f32) + recv[span].astype(f32)
         scaled = (love[...] * total).astype(bf16)
         result = None
         for step in range(0, GROUP, 2):
-            both = jnp.dot(scaled, pair(table, group * GROUP + step), preferred_element_type=f32)
+            source, wave = locate(table, second, first + group * GROUP + step)
+            both = jnp.dot(scaled, pair(source, wave), preferred_element_type=f32)
             left, right = both[:, :lat_dev], both[:, lat_dev:]
             result = left if result is None else jnp.where(line == step, left, result)
             result = jnp.where(line == step + 1, right, result)
@@ -444,11 +472,15 @@
     out[...] = jnp.concatenate(real + imag, axis=0).astype(out.dtype)
 
 
-def inverse_kernel(inverse, near, far, out):
+def inverse_near_kernel(inverse, near, out):
+    half = near.shape[0]
+    out[...] = jnp.dot(inverse[:, :half], near[...], preferred_element_type=f32)
+
+
+def inverse_far_kernel(inverse, started, far, out):
     lon_dev = out.shape[0]
-    half = near.shape[0]
-    both = jnp.dot(inverse[:, :half], near[...], preferred_element_type=f32)
-    both += jnp.dot(inverse[:, half:], far[...], preferred_element_type=f32)
+    half = far.shape[0]
+    both = started[...] + jnp.dot(inverse[:, half:], far[...], preferred_element_type=f32)
     out[...] = both[:lon_dev] + both[lon_dev:]
 
 
@@ -483,16 +515,28 @@
     def stay_put(cells):
         return pltpu.with_memory_space_constraint(cells, pltpu.HBM)
 
-    own, near, away, *strips = call(
+    fields = tuple(
+        map(stay_put, (sea_level, east_velocity, north_velocity, depth, land_mask, loading_prev))
+    )
+    near, away = call(
+        strip_kernel,
+        [shaped(6 + lon_dev // MARGIN, MARGIN, LANES), strip],
+        in_specs=[hbm] * 6,
+        scratch=[
+            pltpu.VMEM((lon_dev, lat_dev), jnp.int32),
+            pltpu.SemaphoreType.DMA((2, 6)),
+        ],
+    )(*fields)
+    own, *strips = call(
         pack_kernel,
-        [shaped(6, lon_dev, lat_dev), shaped(6 + lon_dev // MARGIN, MARGIN, LANES), strip] + [strip] * (1 if lat_count == 2 else 2),
+        [shaped(6, lon_dev, lat_dev)] + [strip] * (1 if lat_count == 2 else 2),
         in_specs=[hbm] * 6,
         scratch=[
             pltpu.VMEM((lon_dev, lat_dev), jnp.int32),
             pltpu.SemaphoreType.DMA((6,)),
             pltpu.SemaphoreType.DMA,
         ],
-    )(*map(stay_put, (sea_level, east_velocity, north_velocity, depth, land_mask, loading_prev)))
+    )(*fields)
 
     def stay(b):
         return b
@@ -515,24 +559,32 @@
     away = shift(away, 0, beyond)
     near = shift(near, 0, nearby)
 
+    *strips, wet_pair = call(
+        join_kernel,
+        [shaped(12, MARGIN, LANES)] * len(strips)
+        + [shaped(2 * lon_dev, lat_dev, dtype=bf16)],
+    )(own, near, away, *strips)
+    if lat_count == 2:
+        facing = [shift(strips[0], None, stay)]
+    else:
+        facing = [shift(strips[1], -1, stay), shift(strips[0], 1, stay)]
     chunk = 2 * wave_dev
     lines = chunk * lon_count
     half = lines // 2
     wide = lon_dev + 2 * MARGIN
-    forward, inverse, wet_pair, forcing, latitude, love, counts = call(
+    forward, inverse, forcing, latitude, love, counts = call(
         functools.partial(
             table_kernel, (lon_dev, lat_dev, total_cols, total_rows, wave_dev, tuple(gens))
         ),
         [
             shaped(lines, 2 * lon_dev, dtype=bf16),
             shaped(2 * lon_dev, lines, dtype=bf16),
-            shaped(2 * lon_dev, lat_dev, dtype=bf16),
             shaped(SUBSTEPS, wide, 2 * lat_dev),
             shaped(3, 8, 2 * lat_dev),
             shaped(1, degrees),
             shaped(*wet_counts.shape, dtype=jnp.int32),
         ],
-        in_specs=[hbm] * 4 + [vmem] * 2,
+        in_specs=[hbm] * 4,
         scratch=[
             pltpu.VMEM((1, len(frequencies)), f32),
             pltpu.VMEM((1, len(frequencies)), f32),
@@ -544,8 +596,6 @@
         stay_put(tide_phase[None]),
         stay_put(love_factor[None]),
         stay_put(wet_counts),
-        own,
-        near,
     )
 
     def swap(cells, gen):
@@ -553,21 +603,13 @@
 
     wet_far = swap(wet_pair, gens[1])
 
-    strips = call(join_kernel, [shaped(12, MARGIN, LANES)] * len(strips))(near, away, *strips)
-    if lat_count == 2:
-        facing = [shift(strips[0], None, stay)]
-    else:
-        facing = [shift(strips[1], -1, stay), shift(strips[0], 1, stay)]
-    height, east_new, north_new, wet_height, wet_sum = call(
+    keep, send, wet_sum, state, static = call(
         functools.partial(step_kernel, lat_count),
-        [shaped(lon_dev, lat_dev)] * 4 + [shaped(8, lat_dev)],
-        in_specs=[vmem] * (5 + len(facing)),
-        scratch=[pltpu.VMEM((3, wide, 2 * lat_dev), f32)] * 2,
-    )(own, near, away, *facing, forcing, latitude)
-
-    keep, send = call(
-        fourier_kernel, [shaped(half, lat_dev), shaped(half + 8, lat_dev)]
-    )(wet_height, wet_sum, forward)
+        [shaped(half, lat_dev), shaped(half + 8, lat_dev), shaped(8, lat_dev)]
+        + [pltpu.VMEM((3, wide, 2 * lat_dev), f32)] * 2,
+        in_specs=[vmem] * (6 + len(facing)),
+    )(own, near, away, *facing, forcing, latitude, forward)
+
     recv = swap(send, gens[0])
     wet_keep, wet_send = call(
         functools.partial(mask_kernel, (lon_dev, total_cols, wave_dev, tuple(gens))),
@@ -619,13 +661,16 @@
                 scratch=[pltpu.SemaphoreType.DMA((4,))],
             )(stay_put(legendre))
         )
+    turned = [table[1] for table in tables]
+    tables = [table[0] for table in tables]
+    pieces = ((0, wave_dev - wave_dev // 4), (wave_dev - wave_dev // 4, wave_dev // 4))
     sums = []
-    for piece in range(parts):
+    for first, waves in pieces:
         mine, moving = call(
-            functools.partial(analysis_kernel, piece * waves),
+            functools.partial(analysis_kernel, (first, waves)),
             [shaped(2 * waves, degrees), shaped(2 * waves, degrees, dtype=bf16)],
-            in_specs=[vmem] * 6,
-        )(keep, recv, wet_keep, level, counts, tables[piece][1])
+            in_specs=[vmem] * 7,
+        )(keep, recv, wet_keep, level, counts, *turned)
         for b in range(lat_bits):
             other = lax.ppermute(moving, "lat", [(i, i ^ (1 << b)) for i in range(lat_count)])
             if b < lat_bits - 1:
@@ -633,20 +678,24 @@
                 moving = mine.astype(bf16)
         sums.append((mine, other))
     spectra = ()
-    for piece in range(parts):
-        last = piece == parts - 1
+    for piece, (first, waves) in enumerate(pieces):
+        last = piece == len(pieces) - 1
         spectra = (
             call(
-                functools.partial(synthesis_kernel, (piece * waves, wave_dev)),
-                shaped(2 * waves * (piece + 1), lat_dev, dtype=bf16 if last else f32),
-                in_specs=[vmem] * (4 + len(spectra)),
-            )(*sums[piece], love, tables[piece][0], *spectra),
+                functools.partial(synthesis_kernel, (first, waves, wave_dev)),
+                shaped(2 * (first + waves), lat_dev, dtype=bf16 if last else f32),
+                in_specs=[vmem] * (5 + len(spectra)),
+            )(*sums[piece], love, *tables, *spectra),
         )
     near = spectra[0]
     for gen in gens[:0:-1]:
         near = jnp.concatenate([near, swap(near, gen)], axis=0)
     far = swap(near, gens[0])
-    loading_new = call(inverse_kernel, shaped(lon_dev, lat_dev))(inverse, near, far)
+    started = call(inverse_near_kernel, shaped(2 * lon_dev, lat_dev))(inverse, near)
+    loading_new = call(inverse_far_kernel, shaped(lon_dev, lat_dev))(inverse, started, far)
+    height, east_new, north_new = call(finish_kernel, [shaped(lon_dev, lat_dev)] * 3)(
+        state, static, forcing, latitude
+    )
     return (height, east_new, north_new, loading_new)
 
 

time: 65.9 us -> 65 us (0.986)
  waiting for transfers between devices: 29.1 us -> 28 us
  Pallas kernels: 15.3 us -> 16.2 us
  starting transfers between devices: 20.5 us -> 19.7 us
    ppermute x5, waiting for transfers between devices: 4.99 us -> 3.76 us  [shift(): return lax.ppermute(cells, ('lat', 'lon'), pairs)]
    pallas_call x9 -> x11, Pallas kernels: 7.69 us -> 8.63 us  [the longest x1 1.7 us: shards(): call(functools.partial(step_kernel, lat_count), [shaped(half, lat_dev), s...]
    ppermute x10, starting transfers between devices: 8.78 us -> 8 us  [swap(): return lax.ppermute(cells, 'lon', [(i, i ^ gen) for i in range(lon_count)])]
  transfers between devices with their start and end apart: 17 -> 17, of which waited for: 12 -> 12; matrix products, arithmetic and copies ran while one was open for 0% -> 0% of each run, Pallas kernels for 14% -> 17%
where the time goes in v3:
time: 65 us; the launch traced here: 64.8 us
  waiting for transfers between devices  28 us (43%)
  starting transfers between devices  19.7 us (30%)
  Pallas kernels  16.2 us (25%)
  between operations  0.78 us (1%)
    ppermute x10, waiting for transfers between devices, swap(): return lax.ppermute(cells, 'lon', [(i, i ^ gen) for i in range(lon_count)])  21.5 us
    ppermute x5, starting transfers between devices, shift(): return lax.ppermute(cells, ('lat', 'lon'), pairs)  9.65 us
    ppermute x10, starting transfers between devices, swap(): return lax.ppermute(cells, 'lon', [(i, i ^ gen) for i in range(lon_count)])  8 us
    pallas_call x2, Pallas kernels, shards(): call(functools.partial(fetch_kernel, piece * waves), [pltpu.VMEM((waves,...  5.12 us
    ppermute x5, waiting for transfers between devices, shift(): return lax.ppermute(cells, ('lat', 'lon'), pairs)  3.76 us
    ppermute x2, waiting for transfers between devices, shards(): lax.ppermute(moving, 'lat', [(i, i ^ 1 << b) for i in range(lat_count)])  2.68 us
    ppermute x2, starting transfers between devices, shards(): lax.ppermute(moving, 'lat', [(i, i ^ 1 << b) for i in range(lat_count)])  2.04 us
    pallas_call x1, Pallas kernels, shards(): call(functools.partial(table_kernel, (lon_dev, lat_dev, total_cols, total...  1.81 us
  transfers between devices with their start and end apart: 17, of which 12 were waited for; matrix products, arithmetic and copies ran while one was open for 0% of the time, Pallas kernels for 17%

profile of v3, /device:TPU:0, one launch (start us, length us, event | category | flops | bytes accessed | tf_op | source)
XLA Modules:
  0.0 64.8 jit_solution(11357100638133150395)
XLA Ops:
  0.6 1.0 %shard_map.139 = (f32[22,8,128]{2,1,0:T(8,128)S(1)}, f32[6,8,128]{2,1,0:T(8,128)S(1)}) custom-call(f32[128,128]{1,0:T(8,128)} %sea.3, f32[128,128]{1,0:T(8,128)} %east.3, f32[128,128]{1,0:T(8,128)} %north.3, f32[128,128]{1,0:T(8,128)} %depth.3, s32[128,128]{1,0:T(8,128)} %mask.3, f32[128,128]{1,0:T(8,128)} %loading.3), custom_call_target="tpu_custom_call" | custom-call | tf_op jit(solution)/shard_map/pallas_call | solution.py:521
  1.6 0.6 collective-permute-start
  2.2 5.6 %collective-permute-start.1 = (f32[6,8,128]{2,1,0:T(8,128)S(1)}, f32[6,8,128]{2,1,0:T(8,128)S(1)}, u32[]{:S(2)}, u32[]{:S(2)}) collective-permute-start(f32[6,8,128]{2,1,0:T(8,128)S(1)} %get-tuple-element.36), channel_id=1, source_target_pairs={{0,15},{1,2},{2,1},{3,4},{4,3},{5,6},{6,5},{7,8},{8,7},{9,10},{10,... | collective-permute-start | bytes 73736 | tf_op jit(solution)/shard_map/ppermute | solution.py:557
  7.8 1.2 %shard_map.138 = (f32[6,128,128]{2,1,0:T(8,128)S(1)}, f32[6,8,128]{2,1,0:T(8,128)S(1)}) custom-call(f32[128,128]{1,0:T(8,128)} %sea.3, f32[128,128]{1,0:T(8,128)} %east.3, f32[128,128]{1,0:T(8,128)} %north.3, f32[128,128]{1,0:T(8,128)} %depth.3, s32[128,128]{1,0:T(8,128)} %mask.3, f32[128,128]{1,0:T(8,128)} %loading.3), custom_call_target="tpu_custom_call" | custom-call | tf_op jit(solution)/shard_map/pallas_call | solution.py:530
  9.0 0.3 collective-permute-done.1.away
  9.3 0.0 collective-permute-done.near
  9.3 0.1 shard_map.140
  9.4 1.5 %collective-permute-start.2 = (f32[12,8,128]{2,1,0:T(8,128)S(1)}, f32[12,8,128]{2,1,0:T(8,128)S(1)}, u32[]{:S(2)}, u32[]{:S(2)}) collective-permute-start(f32[12,8,128]{2,1,0:T(8,128)S(1)} %get-tuple-element.38), channel_id=1, source_target_pairs={{0,16},{1,17},{2,18},{3,19},{4,20},{5,21},{6,22},{7,23},{8,24},{9,... | collective-permute-start | bytes 147464 | tf_op jit(solution)/shard_map/ppermute | solution.py:557
  10.9 1.8 %shard_map.141 = (bf16[1024,256]{1,0:T(8,128)(2,1)S(1)}, bf16[256,1024]{1,0:T(8,128)(2,1)S(1)}, f32[4,144,256]{2,1,0:T(8,128)S(1)}, f32[3,8,256]{2,1,0:T(8,128)S...) custom-call(f32[1,8]{1,0:T(1,128)} %bitcast.4, f32[1,8]{1,0:T(1,128)} %bitcast.5, f32[1,1024]{1,0:T(1,128)} %bitcast.3, ...), custom_call_target="tpu_custom_call" | custom-call | tf_op jit(solution)/shard_map/pallas_call | solution.py:575
  12.7 0.7 %collective-permute-done.2.rest_0_ = f32[12,8,128]{2,1,0:T(8,128)S(1)} collective-permute-done((f32[12,8,128]{2,1,0:T(8,128)S(1)}, f32[12,8,128]{2,1,0:T(8,128)S(1)}, u32[]{:S(2)}, u32[]{:S(2)}) %collective-permute-start.2) | collective-permute-done | bytes 49184 | tf_op jit(solution)/shard_map/ppermute | solution.py:557
  13.5 1.7 %shard_map.142 = (f32[512,128]{1,0:T(8,128)S(1)}, f32[520,128]{1,0:T(8,128)S(1)}, f32[8,128]{1,0:T(8,128)S(1)}, f32[3,144,256]{2,1,0:T(8,128)S(1)}, f32[3,144,256]{2,1,0:T(8,128)S(1)}) custom-call(f32[6,128,128]{2,1,0:T(8,128)S(1)} %get-tuple-element.34.own, f32[22,8,128]{2,1,0:T(8,128)S(1)} %collective-permute-done.near, ...), custom_call_target="tpu_custom_call" | custom-call | tf_op jit(solution)/shard_map/pallas_call | solution.py:606
  15.2 0.1 collective-permute-start.3
  15.3 1.5 %collective-permute-done.3 = f32[520,128]{1,0:T(8,128)S(1)} collective-permute-done((f32[520,128]{1,0:T(8,128)S(1)}, f32[520,128]{1,0:T(8,128)S(1)}, u32[]{:S(2)}, u32[]{:S(2)}) %collective-permute-start.3) | collective-permute-done | bytes 266272 | tf_op jit(solution)/shard_map/ppermute | solution.py:602
  16.9 0.1 collective-permute-start.4
  17.0 1.7 %collective-permute-start.8 = (bf16[256,128]{1,0:T(8,128)(2,1)S(1)}, bf16[256,128]{1,0:T(8,128)(2,1)S(1)}, u32[]{:S(2)}, u32[]{:S(2)}) collective-permute-start(bf16[256,128]{1,0:T(8,128)(2,1)S(1)} %get-tuple-element.51.pair), channel_id=1, source_target_pairs={{0,3},{1,2},{2,1},{3,0},{4,7},{5,6},{6,5},{7,4},{8,11},{9,10},{10,... | collective-permute-start | bytes 196616 | tf_op jit(solution)/shard_map/ppermute | solution.py:602
  18.7 5.2 %collective-permute-done.8.far = bf16[256,128]{1,0:T(8,128)(2,1)S(1)} collective-permute-done((bf16[256,128]{1,0:T(8,128)(2,1)S(1)}, bf16[256,128]{1,0:T(8,128)(2,1)S(1)}, u32[]{:S(2)}, u32[]{:S(2)}) %collective-permute-start.8) | collective-permute-done | bytes 65568 | tf_op jit(solution)/shard_map/ppermute | solution.py:602
  23.9 0.6 shard_map.144
  24.5 0.5 collective-permute-start.9
  25.0 1.7 %collective-permute-start.6 = (f32[8,128]{1,0:T(8,128)S(1)}, f32[8,128]{1,0:T(8,128)S(1)}, u32[]{:S(2)}, u32[]{:S(2)}) collective-permute-start(f32[8,128]{1,0:T(8,128)S(1)} %slice_add_fusion.11), channel_id=1, source_target_pairs={{0,19},{1,18},{2,17},{3,16},{4,23},{5,22},{6,21},{7,20},{8,27},{9,... | collective-permute-start | bytes 12296 | tf_op jit(solution)/shard_map/ppermute | solution.py:557
  26.7 0.3 collective-permute-start.5
  27.0 0.0 collective-permute-done.4
  27.0 2.0 %collective-permute-done.6 = f32[8,128]{1,0:T(8,128)S(1)} collective-permute-done((f32[8,128]{1,0:T(8,128)S(1)}, f32[8,128]{1,0:T(8,128)S(1)}, u32[]{:S(2)}, u32[]{:S(2)}) %collective-permute-start.6) | collective-permute-done | bytes 4128 | tf_op jit(solution)/shard_map/ppermute | solution.py:557
  28.9 0.8 %collective-permute-done.5 = f32[8,128]{1,0:T(8,128)S(1)} collective-permute-done((f32[8,128]{1,0:T(8,128)S(1)}, f32[8,128]{1,0:T(8,128)S(1)}, u32[]{:S(2)}, u32[]{:S(2)}) %collective-permute-start.5) | collective-permute-done | bytes 4128 | tf_op jit(solution)/shard_map/ppermute | solution.py:557
  29.7 1.6 %collective-permute-start.7 = (f32[136,128]{1,0:T(8,128)S(1)}, f32[136,128]{1,0:T(8,128)S(1)}, u32[]{:S(2)}, u32[]{:S(2)}) collective-permute-start(f32[136,128]{1,0:T(8,128)S(1)} %pad_maximum_fusion.2), channel_id=1, source_target_pairs={{0,9},{1,8},{2,11},{3,10},{4,13},{5,12},{6,15},{7,14},{8,1},{9,0},... | collective-permute-start | bytes 208904 | tf_op jit(solution)/shard_map/ppermute | solution.py:602
  31.3 0.0 collective-permute-done.9
  31.3 3.2 %collective-permute-done.7 = f32[136,128]{1,0:T(8,128)S(1)} collective-permute-done((f32[136,128]{1,0:T(8,128)S(1)}, f32[136,128]{1,0:T(8,128)S(1)}, u32[]{:S(2)}, u32[]{:S(2)}) %collective-permute-start.7) | collective-permute-done | bytes 69664 | tf_op jit(solution)/shard_map/ppermute | solution.py:602
  34.5 3.0 %collective-permute-start.10 = (f32[136,128]{1,0:T(8,128)S(1)}, f32[136,128]{1,0:T(8,128)S(1)}, u32[]{:S(2)}, u32[]{:S(2)}) collective-permute-start(f32[136,128]{1,0:T(8,128)S(1)} %pad_maximum_fusion.3), channel_id=1, source_target_pairs={{0,5},{1,4},{2,7},{3,6},{4,1},{5,0},{6,3},{7,2},{8,13},{9,12},{10,... | collective-permute-start | bytes 208904 | tf_op jit(solution)/shard_map/ppermute | solution.py:602
  37.5 2.6 %shard_map.145 = (bf16[16,1024,128]{2,1,0:T(8,128)(2,1)S(1)}, bf16[16,128,1024]{2,1,0:T(8,128)(2,1)S(1)}) custom-call(bf16[32,1024,128]{2,1,0:T(8,128)(2,1)} %source.3), custom_call_target="tpu_custom_call" | custom-call | tf_op jit(solution)/shard_map/pallas_call | solution.py:654
  40.1 2.6 %shard_map.146 = (bf16[16,1024,128]{2,1,0:T(8,128)(2,1)S(1)}, bf16[16,128,1024]{2,1,0:T(8,128)(2,1)S(1)}) custom-call(bf16[32,1024,128]{2,1,0:T(8,128)(2,1)} %source.3), custom_call_target="tpu_custom_call" | custom-call | tf_op jit(solution)/shard_map/pallas_call | solution.py:654
  42.6 0.0 collective-permute-done.10.recv
  42.7 1.0 %shard_map.148 = (f32[48,1024]{1,0:T(8,128)S(1)}, bf16[48,1024]{1,0:T(8,128)(2,1)S(1)}) custom-call(f32[64,128]{1,0:T(8,128)S(1)} %get-tuple-element.69.keep, f32[136,128]{1,0:T(8,128)S(1)} %collective-permute-done.10.recv, f32[64,128]{1,0:T(8,128)S(1)} %get-tuple-element.70.wet_keep, f32[8,128]{1,0:T(8,128)S(1)} %slice_add_fusion.8.wet_sum, ...), custom_call_target="tpu_custom_call" | custom-call | tf_op jit(solution)/shard_map/pallas_call | solution.py:669
  43.7 0.6 collective-permute-start.12
  44.3 0.5 shard_map.147
  44.8 1.4 %collective-permute-start.11 = (bf16[16,1024]{1,0:T(8,128)(2,1)S(1)}, bf16[16,1024]{1,0:T(8,128)(2,1)S(1)}, u32[]{:S(2)}, u32[]{:S(2)}) collective-permute-start(bf16[16,1024]{1,0:T(8,128)(2,1)S(1)} %get-tuple-element.58), channel_id=1, source_target_pairs={{0,16},{16,0},{1,17},{17,1},{2,18},{18,2},{3,19},{19,3},{4,20},{20... | collective-permute-start | bytes 98312 | tf_op jit(solution)/shard_map/ppermute | solution.py:675
  46.2 2.7 %collective-permute-done.12.recv = bf16[48,1024]{1,0:T(8,128)(2,1)S(1)} collective-permute-done((bf16[48,1024]{1,0:T(8,128)(2,1)S(1)}, bf16[48,1024]{1,0:T(8,128)(2,1)S(1)}, u32[]{:S(2)}, u32[]{:S(2)}) %collective-permute-start.12) | collective-permute-done | bytes 98336 | tf_op jit(solution)/shard_map/ppermute | solution.py:675
  48.9 0.9 %shard_map.149.rest_0_ = f32[48,128]{1,0:T(8,128)S(1)} custom-call(f32[48,1024]{1,0:T(8,128)S(1)} %get-tuple-element.62.own, bf16[48,1024]{1,0:T(8,128)(2,1)S(1)} %collective-permute-done.12.recv, f32[1,1024]{1,0:T(1,128)S(1)} %get-tuple-element.59.love, bf16[16,1024,128]{2,1,0:T(8,128)(2,1)S(1)} %get-tuple-element.60.table, ...), custom_call_target="tpu_custom_call" | custom-call | tf_op jit(solution)/shard_map/pallas_call | solution.py:684
  49.8 0.0 collective-permute-done.11.recv
  49.8 0.4 shard_map.150
  50.2 0.0 collective-permute-start.13
  50.2 3.2 %collective-permute-done.13 = bf16[64,128]{1,0:T(8,128)(2,1)S(1)} collective-permute-done((bf16[64,128]{1,0:T(8,128)(2,1)S(1)}, bf16[64,128]{1,0:T(8,128)(2,1)S(1)}, u32[]{:S(2)}, u32[]{:S(2)}) %collective-permute-start.13) | collective-permute-done | bytes 16416 | tf_op jit(solution)/shard_map/ppermute | solution.py:602
  53.4 1.0 %collective-permute-start.14 = (bf16[128,128]{1,0:T(8,128)(2,1)S(1)}, bf16[128,128]{1,0:T(8,128)(2,1)S(1)}, u32[]{:S(2)}, u32[]{:S(2)}) collective-permute-start(bf16[128,128]{1,0:T(8,128)(2,1)S(1)} %pad_maximum_fusion.5), channel_id=1, source_target_pairs={{0,9},{1,8},{2,11},{3,10},{4,13},{5,12},{6,15},{7,14},{8,1},{9,0},... | collective-permute-start | bytes 98312 | tf_op jit(solution)/shard_map/ppermute | solution.py:602
  54.3 4.0 %collective-permute-done.14 = bf16[128,128]{1,0:T(8,128)(2,1)S(1)} collective-permute-done((bf16[128,128]{1,0:T(8,128)(2,1)S(1)}, bf16[128,128]{1,0:T(8,128)(2,1)S(1)}, u32[]{:S(2)}, u32[]{:S(2)}) %collective-permute-start.14) | collective-permute-done | bytes 32800 | tf_op jit(solution)/shard_map/ppermute | solution.py:602
  58.4 0.0 collective-permute-start.15
  58.4 4.1 %collective-permute-done.15 = bf16[256,128]{1,0:T(8,128)(2,1)S(1)} collective-permute-done((bf16[256,128]{1,0:T(8,128)(2,1)S(1)}, bf16[256,128]{1,0:T(8,128)(2,1)S(1)}, u32[]{:S(2)}, u32[]{:S(2)}) %collective-permute-start.15) | collective-permute-done | bytes 65568 | tf_op jit(solution)/shard_map/ppermute | solution.py:602
  62.5 0.2 collective-permute-start.16
  62.7 0.8 %shard_map.143 = (f32[128,128]{1,0:T(8,128)}, f32[128,128]{1,0:T(8,128)}, f32[128,128]{1,0:T(8,128)}) custom-call(f32[3,144,256]{2,1,0:T(8,128)S(1)} %get-tuple-element.42.state, f32[3,144,256]{2,1,0:T(8,128)S(1)} %get-tuple-element.43.static, f32[4,144,256]{2,1,0:T(8,128)S(1)} %get-tuple-element.39.rest_1_.forcing, ...), custom_call_target="tpu_custom_call" | custom-call | tf_op jit(solution)/shard_map/pallas_call | solution.py:696
  63.5 0.2 shard_map.151.started
  63.7 0.2 collective-permute-done.16.far
  63.9 0.8 %shard_map.152 = f32[128,128]{1,0:T(8,128)} custom-call(bf16[256,1024]{1,0:T(8,128)(2,1)S(1)} %get-tuple-element.47.inverse, f32[256,128]{1,0:T(8,128)S(1)} %shard_map.151.started, bf16[512,128]{1,0:T(8,128)(2,1)S(1)} %collective-permute-done.16.far), custom_call_target="tpu_custom_call" | custom-call | tf_op jit(solution)/shard_map/pallas_call | solution.py:695
  (14 shorter events, 0.1 us)
Async XLA Ops:
  1.6 7.7 %collective-permute-start = (f32[22,8,128]{2,1,0:T(8,128)S(1)}, f32[22,8,128]{2,1,0:T(8,128)S(1)}, u32[]{:S(2)}, u32[]{:S(2)}) collective-permute-start(f32[22,8,128]{2,1,0:T(8,128)S(1)} %get-tuple-element.35), channel_id=1, source_target_pairs={{0,1},{1,0},{2,3},{3,2},{4,5},{5,4},{6,7},{7,6},{8,9},{9,8},{10,11... | collective-permute-start | bytes 270344 | tf_op jit(solution)/shard_map/ppermute | solution.py:557
  2.2 7.1 %collective-permute-start.1 = (f32[6,8,128]{2,1,0:T(8,128)S(1)}, f32[6,8,128]{2,1,0:T(8,128)S(1)}, u32[]{:S(2)}, u32[]{:S(2)}) collective-permute-start(f32[6,8,128]{2,1,0:T(8,128)S(1)} %get-tuple-element.36), channel_id=1, source_target_pairs={{0,15},{1,2},{2,1},{3,4},{4,3},{5,6},{6,5},{7,8},{8,7},{9,10},{10,... | collective-permute-start | bytes 73736 | tf_op jit(solution)/shard_map/ppermute | solution.py:557
  9.4 4.1 %collective-permute-start.2 = (f32[12,8,128]{2,1,0:T(8,128)S(1)}, f32[12,8,128]{2,1,0:T(8,128)S(1)}, u32[]{:S(2)}, u32[]{:S(2)}) collective-permute-start(f32[12,8,128]{2,1,0:T(8,128)S(1)} %get-tuple-element.38), channel_id=1, source_target_pairs={{0,16},{1,17},{2,18},{3,19},{4,20},{5,21},{6,22},{7,23},{8,24},{9,... | collective-permute-start | bytes 147464 | tf_op jit(solution)/shard_map/ppermute | solution.py:557
  15.2 1.6 %collective-permute-start.3 = (f32[520,128]{1,0:T(8,128)S(1)}, f32[520,128]{1,0:T(8,128)S(1)}, u32[]{:S(2)}, u32[]{:S(2)}) collective-permute-start(f32[520,128]{1,0:T(8,128)S(1)} %get-tuple-element.49), channel_id=1, source_target_pairs={{0,1},{1,0},{2,3},{3,2},{4,5},{5,4},{6,7},{7,6},{8,9},{9,8},{10,11... | collective-permute-start | bytes 798728 | tf_op jit(solution)/shard_map/ppermute | solution.py:602
  16.9 10.1 %collective-permute-start.4 = (f32[264,128]{1,0:T(8,128)S(1)}, f32[264,128]{1,0:T(8,128)S(1)}, u32[]{:S(2)}, u32[]{:S(2)}) collective-permute-start(f32[264,128]{1,0:T(8,128)S(1)} %pad_maximum_fusion), channel_id=1, source_target_pairs={{0,3},{1,2},{2,1},{3,0},{4,7},{5,6},{6,5},{7,4},{8,11},{9,10},{10,... | collective-permute-start | bytes 405512 | tf_op jit(solution)/shard_map/ppermute | solution.py:602
  17.0 7.0 %collective-permute-start.8 = (bf16[256,128]{1,0:T(8,128)(2,1)S(1)}, bf16[256,128]{1,0:T(8,128)(2,1)S(1)}, u32[]{:S(2)}, u32[]{:S(2)}) collective-permute-start(bf16[256,128]{1,0:T(8,128)(2,1)S(1)} %get-tuple-element.51.pair), channel_id=1, source_target_pairs={{0,3},{1,2},{2,1},{3,0},{4,7},{5,6},{6,5},{7,4},{8,11},{9,10},{10,... | collective-permute-start | bytes 196616 | tf_op jit(solution)/shard_map/ppermute | solution.py:602
  24.5 6.7 %collective-permute-start.9 = (f32[128,128]{1,0:T(8,128)S(1)}, f32[128,128]{1,0:T(8,128)S(1)}, u32[]{:S(2)}, u32[]{:S(2)}) collective-permute-start(f32[128,128]{1,0:T(8,128)S(1)} %get-tuple-element.53), channel_id=1, source_target_pairs={{0,9},{1,8},{2,11},{3,10},{4,13},{5,12},{6,15},{7,14},{8,1},{9,0},... | collective-permute-start | bytes 196616 | tf_op jit(solution)/shard_map/ppermute | solution.py:602
  25.0 3.9 %collective-permute-start.6 = (f32[8,128]{1,0:T(8,128)S(1)}, f32[8,128]{1,0:T(8,128)S(1)}, u32[]{:S(2)}, u32[]{:S(2)}) collective-permute-start(f32[8,128]{1,0:T(8,128)S(1)} %slice_add_fusion.11), channel_id=1, source_target_pairs={{0,19},{1,18},{2,17},{3,16},{4,23},{5,22},{6,21},{7,20},{8,27},{9,... | collective-permute-start | bytes 12296 | tf_op jit(solution)/shard_map/ppermute | solution.py:557
  26.7 3.0 %collective-permute-start.5 = (f32[8,128]{1,0:T(8,128)S(1)}, f32[8,128]{1,0:T(8,128)S(1)}, u32[]{:S(2)}, u32[]{:S(2)}) collective-permute-start(f32[8,128]{1,0:T(8,128)S(1)} %slice_add_fusion.11), channel_id=1, source_target_pairs={{0,17},{1,16},{2,19},{3,18},{4,21},{5,20},{6,23},{7,22},{8,25},{9,... | collective-permute-start | bytes 12296 | tf_op jit(solution)/shard_map/ppermute | solution.py:557
  29.7 4.8 %collective-permute-start.7 = (f32[136,128]{1,0:T(8,128)S(1)}, f32[136,128]{1,0:T(8,128)S(1)}, u32[]{:S(2)}, u32[]{:S(2)}) collective-permute-start(f32[136,128]{1,0:T(8,128)S(1)} %pad_maximum_fusion.2), channel_id=1, source_target_pairs={{0,9},{1,8},{2,11},{3,10},{4,13},{5,12},{6,15},{7,14},{8,1},{9,0},... | collective-permute-start | bytes 208904 | tf_op jit(solution)/shard_map/ppermute | solution.py:602
  34.5 8.1 %collective-permute-start.10 = (f32[136,128]{1,0:T(8,128)S(1)}, f32[136,128]{1,0:T(8,128)S(1)}, u32[]{:S(2)}, u32[]{:S(2)}) collective-permute-start(f32[136,128]{1,0:T(8,128)S(1)} %pad_maximum_fusion.3), channel_id=1, source_target_pairs={{0,5},{1,4},{2,7},{3,6},{4,1},{5,0},{6,3},{7,2},{8,13},{9,12},{10,... | collective-permute-start | bytes 208904 | tf_op jit(solution)/shard_map/ppermute | solution.py:602
  43.7 5.2 %collective-permute-start.12 = (bf16[48,1024]{1,0:T(8,128)(2,1)S(1)}, bf16[48,1024]{1,0:T(8,128)(2,1)S(1)}, u32[]{:S(2)}, u32[]{:S(2)}) collective-permute-start(bf16[48,1024]{1,0:T(8,128)(2,1)S(1)} %get-tuple-element.63), channel_id=1, source_target_pairs={{0,16},{16,0},{1,17},{17,1},{2,18},{18,2},{3,19},{19,3},{4,20},{20... | collective-permute-start | bytes 294920 | tf_op jit(solution)/shard_map/ppermute | solution.py:675
  44.8 5.0 %collective-permute-start.11 = (bf16[16,1024]{1,0:T(8,128)(2,1)S(1)}, bf16[16,1024]{1,0:T(8,128)(2,1)S(1)}, u32[]{:S(2)}, u32[]{:S(2)}) collective-permute-start(bf16[16,1024]{1,0:T(8,128)(2,1)S(1)} %get-tuple-element.58), channel_id=1, source_target_pairs={{0,16},{16,0},{1,17},{17,1},{2,18},{18,2},{3,19},{19,3},{4,20},{20... | collective-permute-start | bytes 98312 | tf_op jit(solution)/shard_map/ppermute | solution.py:675
  50.2 3.2 %collective-permute-start.13 = (bf16[64,128]{1,0:T(8,128)(2,1)S(1)}, bf16[64,128]{1,0:T(8,128)(2,1)S(1)}, u32[]{:S(2)}, u32[]{:S(2)}) collective-permute-start(bf16[64,128]{1,0:T(8,128)(2,1)S(1)} %shard_map.150), channel_id=1, source_target_pairs={{0,5},{1,4},{2,7},{3,6},{4,1},{5,0},{6,3},{7,2},{8,13},{9,12},{10,... | collective-permute-start | bytes 49160 | tf_op jit(solution)/shard_map/ppermute | solution.py:602
  53.4 5.0 %collective-permute-start.14 = (bf16[128,128]{1,0:T(8,128)(2,1)S(1)}, bf16[128,128]{1,0:T(8,128)(2,1)S(1)}, u32[]{:S(2)}, u32[]{:S(2)}) collective-permute-start(bf16[128,128]{1,0:T(8,128)(2,1)S(1)} %pad_maximum_fusion.5), channel_id=1, source_target_pairs={{0,9},{1,8},{2,11},{3,10},{4,13},{5,12},{6,15},{7,14},{8,1},{9,0},... | collective-permute-start | bytes 98312 | tf_op jit(solution)/shard_map/ppermute | solution.py:602
  58.4 4.1 %collective-permute-start.15 = (bf16[256,128]{1,0:T(8,128)(2,1)S(1)}, bf16[256,128]{1,0:T(8,128)(2,1)S(1)}, u32[]{:S(2)}, u32[]{:S(2)}) collective-permute-start(bf16[256,128]{1,0:T(8,128)(2,1)S(1)} %pad_maximum_fusion.4), channel_id=1, source_target_pairs={{0,3},{1,2},{2,1},{3,0},{4,7},{5,6},{6,5},{7,4},{8,11},{9,10},{10,... | collective-permute-start | bytes 196616 | tf_op jit(solution)/shard_map/ppermute | solution.py:602
  62.5 1.4 %collective-permute-start.16 = (bf16[512,128]{1,0:T(8,128)(2,1)S(1)}, bf16[512,128]{1,0:T(8,128)(2,1)S(1)}, u32[]{:S(2)}, u32[]{:S(2)}) collective-permute-start(bf16[512,128]{1,0:T(8,128)(2,1)S(1)} %pad_maximum_fusion.1.near), channel_id=1, source_target_pairs={{0,1},{1,0},{2,3},{3,2},{4,5},{5,4},{6,7},{7,6},{8,9},{9,8},{10,11... | collective-permute-start | bytes 393224 | tf_op jit(solution)/shard_map/ppermute | solution.py:602

commit v4 on v3

--- a/solution.py
+++ b/solution.py
@@ -362,12 +362,13 @@
 
     rows = tuple(latitude[index][0:1] for index in range(3))
 
-    def substep(k, _):
+    def substep(k):
         rise(state, static, rows)
         state[1], state[2] = veer(state, static, forcing[k], rows)
         return 0
 
-    lax.fori_loop(0, SUBSTEPS - 1, substep, 0)
+    for k in range(SUBSTEPS - 1):
+        substep(k)
     rise(state, static, rows)
     product = state[0, :lon_dev, :lat_dev] * own[4]
     level = jnp.sum(jnp.sum(product, axis=0, keepdims=True), axis=1, keepdims=True)

time: 65 us -> 64.6 us (level)
  no operation moved by 1% of the time
where the time goes in v4:
time: 64.6 us; the launch traced here: 64.3 us
  waiting for transfers between devices  28 us (43%)
  starting transfers between devices  19.7 us (30%)
  Pallas kernels  15.7 us (24%)
  between operations  0.78 us (1%)
    ppermute x10, waiting for transfers between devices, swap(): return lax.ppermute(cells, 'lon', [(i, i ^ gen) for i in range(lon_count)])  21.5 us
    ppermute x5, starting transfers between devices, shift(): return lax.ppermute(cells, ('lat', 'lon'), pairs)  9.65 us
    ppermute x10, starting transfers between devices, swap(): return lax.ppermute(cells, 'lon', [(i, i ^ gen) for i in range(lon_count)])  8.02 us
    pallas_call x2, Pallas kernels, shards(): call(functools.partial(fetch_kernel, piece * waves), [pltpu.VMEM((waves,...  5.12 us
    ppermute x5, waiting for transfers between devices, shift(): return lax.ppermute(cells, ('lat', 'lon'), pairs)  3.75 us
    ppermute x2, waiting for transfers between devices, shards(): lax.ppermute(moving, 'lat', [(i, i ^ 1 << b) for i in range(lat_count)])  2.68 us
    ppermute x2, starting transfers between devices, shards(): lax.ppermute(moving, 'lat', [(i, i ^ 1 << b) for i in range(lat_count)])  2.04 us
    pallas_call x1, Pallas kernels, shards(): call(functools.partial(table_kernel, (lon_dev, lat_dev, total_cols, total...  1.81 us
  transfers between devices with their start and end apart: 17, of which 12 were waited for; matrix products, arithmetic and copies ran while one was open for 0% of the time, Pallas kernels for 17%

profile of v4, /device:TPU:0, one launch (start us, length us, event | category | flops | bytes accessed | tf_op | source)
XLA Modules:
  0.0 64.3 jit_solution(5573417817520083342)
XLA Ops:
  0.6 1.0 %shard_map.139 = (f32[22,8,128]{2,1,0:T(8,128)S(1)}, f32[6,8,128]{2,1,0:T(8,128)S(1)}) custom-call(f32[128,128]{1,0:T(8,128)} %sea.3, f32[128,128]{1,0:T(8,128)} %east.3, f32[128,128]{1,0:T(8,128)} %north.3, f32[128,128]{1,0:T(8,128)} %depth.3, s32[128,128]{1,0:T(8,128)} %mask.3, f32[128,128]{1,0:T(8,128)} %loading.3), custom_call_target="tpu_custom_call" | custom-call | tf_op jit(solution)/shard_map/pallas_call | solution.py:522
  1.6 0.6 collective-permute-start
  2.2 5.6 %collective-permute-start.1 = (f32[6,8,128]{2,1,0:T(8,128)S(1)}, f32[6,8,128]{2,1,0:T(8,128)S(1)}, u32[]{:S(2)}, u32[]{:S(2)}) collective-permute-start(f32[6,8,128]{2,1,0:T(8,128)S(1)} %get-tuple-element.36), channel_id=1, source_target_pairs={{0,15},{1,2},{2,1},{3,4},{4,3},{5,6},{6,5},{7,8},{8,7},{9,10},{10,... | collective-permute-start | bytes 73736 | tf_op jit(solution)/shard_map/ppermute | solution.py:558
  7.8 1.2 %shard_map.138 = (f32[6,128,128]{2,1,0:T(8,128)S(1)}, f32[6,8,128]{2,1,0:T(8,128)S(1)}) custom-call(f32[128,128]{1,0:T(8,128)} %sea.3, f32[128,128]{1,0:T(8,128)} %east.3, f32[128,128]{1,0:T(8,128)} %north.3, f32[128,128]{1,0:T(8,128)} %depth.3, s32[128,128]{1,0:T(8,128)} %mask.3, f32[128,128]{1,0:T(8,128)} %loading.3), custom_call_target="tpu_custom_call" | custom-call | tf_op jit(solution)/shard_map/pallas_call | solution.py:531
  9.0 0.3 collective-permute-done.1.away
  9.3 0.0 collective-permute-done.near
  9.3 0.1 shard_map.140
  9.4 1.5 %collective-permute-start.2 = (f32[12,8,128]{2,1,0:T(8,128)S(1)}, f32[12,8,128]{2,1,0:T(8,128)S(1)}, u32[]{:S(2)}, u32[]{:S(2)}) collective-permute-start(f32[12,8,128]{2,1,0:T(8,128)S(1)} %get-tuple-element.38), channel_id=1, source_target_pairs={{0,16},{1,17},{2,18},{3,19},{4,20},{5,21},{6,22},{7,23},{8,24},{9,... | collective-permute-start | bytes 147464 | tf_op jit(solution)/shard_map/ppermute | solution.py:558
  10.9 1.8 %shard_map.141 = (bf16[1024,256]{1,0:T(8,128)(2,1)S(1)}, bf16[256,1024]{1,0:T(8,128)(2,1)S(1)}, f32[4,144,256]{2,1,0:T(8,128)S(1)}, f32[3,8,256]{2,1,0:T(8,128)S...) custom-call(f32[1,8]{1,0:T(1,128)} %bitcast.4, f32[1,8]{1,0:T(1,128)} %bitcast.5, f32[1,1024]{1,0:T(1,128)} %bitcast.3, ...), custom_call_target="tpu_custom_call" | custom-call | tf_op jit(solution)/shard_map/pallas_call | solution.py:576
  12.7 0.7 %collective-permute-done.2.rest_0_ = f32[12,8,128]{2,1,0:T(8,128)S(1)} collective-permute-done((f32[12,8,128]{2,1,0:T(8,128)S(1)}, f32[12,8,128]{2,1,0:T(8,128)S(1)}, u32[]{:S(2)}, u32[]{:S(2)}) %collective-permute-start.2) | collective-permute-done | bytes 49184 | tf_op jit(solution)/shard_map/ppermute | solution.py:558
  13.5 1.2 %shard_map.142 = (f32[512,128]{1,0:T(8,128)S(1)}, f32[520,128]{1,0:T(8,128)S(1)}, f32[8,128]{1,0:T(8,128)S(1)}, f32[3,144,256]{2,1,0:T(8,128)S(1)}, f32[3,144,256]{2,1,0:T(8,128)S(1)}) custom-call(f32[6,128,128]{2,1,0:T(8,128)S(1)} %get-tuple-element.34.own, f32[22,8,128]{2,1,0:T(8,128)S(1)} %collective-permute-done.near, ...), custom_call_target="tpu_custom_call" | custom-call | tf_op jit(solution)/shard_map/pallas_call | solution.py:607
  14.7 0.1 collective-permute-start.3
  14.8 1.5 %collective-permute-done.3 = f32[520,128]{1,0:T(8,128)S(1)} collective-permute-done((f32[520,128]{1,0:T(8,128)S(1)}, f32[520,128]{1,0:T(8,128)S(1)}, u32[]{:S(2)}, u32[]{:S(2)}) %collective-permute-start.3) | collective-permute-done | bytes 266272 | tf_op jit(solution)/shard_map/ppermute | solution.py:603
  16.4 0.1 collective-permute-start.4
  16.5 1.7 %collective-permute-start.8 = (bf16[256,128]{1,0:T(8,128)(2,1)S(1)}, bf16[256,128]{1,0:T(8,128)(2,1)S(1)}, u32[]{:S(2)}, u32[]{:S(2)}) collective-permute-start(bf16[256,128]{1,0:T(8,128)(2,1)S(1)} %get-tuple-element.51.pair), channel_id=1, source_target_pairs={{0,3},{1,2},{2,1},{3,0},{4,7},{5,6},{6,5},{7,4},{8,11},{9,10},{10,... | collective-permute-start | bytes 196616 | tf_op jit(solution)/shard_map/ppermute | solution.py:603
  18.2 5.2 %collective-permute-done.8.far = bf16[256,128]{1,0:T(8,128)(2,1)S(1)} collective-permute-done((bf16[256,128]{1,0:T(8,128)(2,1)S(1)}, bf16[256,128]{1,0:T(8,128)(2,1)S(1)}, u32[]{:S(2)}, u32[]{:S(2)}) %collective-permute-start.8) | collective-permute-done | bytes 65568 | tf_op jit(solution)/shard_map/ppermute | solution.py:603
  23.5 0.6 shard_map.144
  24.1 0.5 collective-permute-start.9
  24.6 1.6 %collective-permute-start.6 = (f32[8,128]{1,0:T(8,128)S(1)}, f32[8,128]{1,0:T(8,128)S(1)}, u32[]{:S(2)}, u32[]{:S(2)}) collective-permute-start(f32[8,128]{1,0:T(8,128)S(1)} %slice_add_fusion.11), channel_id=1, source_target_pairs={{0,19},{1,18},{2,17},{3,16},{4,23},{5,22},{6,21},{7,20},{8,27},{9,... | collective-permute-start | bytes 12296 | tf_op jit(solution)/shard_map/ppermute | solution.py:558
  26.2 0.3 collective-permute-start.5
  26.5 0.0 collective-permute-done.4
  26.5 2.0 %collective-permute-done.6 = f32[8,128]{1,0:T(8,128)S(1)} collective-permute-done((f32[8,128]{1,0:T(8,128)S(1)}, f32[8,128]{1,0:T(8,128)S(1)}, u32[]{:S(2)}, u32[]{:S(2)}) %collective-permute-start.6) | collective-permute-done | bytes 4128 | tf_op jit(solution)/shard_map/ppermute | solution.py:558
  28.5 0.7 %collective-permute-done.5 = f32[8,128]{1,0:T(8,128)S(1)} collective-permute-done((f32[8,128]{1,0:T(8,128)S(1)}, f32[8,128]{1,0:T(8,128)S(1)}, u32[]{:S(2)}, u32[]{:S(2)}) %collective-permute-start.5) | collective-permute-done | bytes 4128 | tf_op jit(solution)/shard_map/ppermute | solution.py:558
  29.2 1.6 %collective-permute-start.7 = (f32[136,128]{1,0:T(8,128)S(1)}, f32[136,128]{1,0:T(8,128)S(1)}, u32[]{:S(2)}, u32[]{:S(2)}) collective-permute-start(f32[136,128]{1,0:T(8,128)S(1)} %pad_maximum_fusion.2), channel_id=1, source_target_pairs={{0,9},{1,8},{2,11},{3,10},{4,13},{5,12},{6,15},{7,14},{8,1},{9,0},... | collective-permute-start | bytes 208904 | tf_op jit(solution)/shard_map/ppermute | solution.py:603
  30.8 0.0 collective-permute-done.9
  30.8 3.2 %collective-permute-done.7 = f32[136,128]{1,0:T(8,128)S(1)} collective-permute-done((f32[136,128]{1,0:T(8,128)S(1)}, f32[136,128]{1,0:T(8,128)S(1)}, u32[]{:S(2)}, u32[]{:S(2)}) %collective-permute-start.7) | collective-permute-done | bytes 69664 | tf_op jit(solution)/shard_map/ppermute | solution.py:603
  34.1 3.0 %collective-permute-start.10 = (f32[136,128]{1,0:T(8,128)S(1)}, f32[136,128]{1,0:T(8,128)S(1)}, u32[]{:S(2)}, u32[]{:S(2)}) collective-permute-start(f32[136,128]{1,0:T(8,128)S(1)} %pad_maximum_fusion.3), channel_id=1, source_target_pairs={{0,5},{1,4},{2,7},{3,6},{4,1},{5,0},{6,3},{7,2},{8,13},{9,12},{10,... | collective-permute-start | bytes 208904 | tf_op jit(solution)/shard_map/ppermute | solution.py:603
  37.0 2.6 %shard_map.145 = (bf16[16,1024,128]{2,1,0:T(8,128)(2,1)S(1)}, bf16[16,128,1024]{2,1,0:T(8,128)(2,1)S(1)}) custom-call(bf16[32,1024,128]{2,1,0:T(8,128)(2,1)} %source.3), custom_call_target="tpu_custom_call" | custom-call | tf_op jit(solution)/shard_map/pallas_call | solution.py:655
  39.6 2.6 %shard_map.146 = (bf16[16,1024,128]{2,1,0:T(8,128)(2,1)S(1)}, bf16[16,128,1024]{2,1,0:T(8,128)(2,1)S(1)}) custom-call(bf16[32,1024,128]{2,1,0:T(8,128)(2,1)} %source.3), custom_call_target="tpu_custom_call" | custom-call | tf_op jit(solution)/shard_map/pallas_call | solution.py:655
  42.2 0.0 collective-permute-done.10.recv
  42.2 1.0 %shard_map.148 = (f32[48,1024]{1,0:T(8,128)S(1)}, bf16[48,1024]{1,0:T(8,128)(2,1)S(1)}) custom-call(f32[64,128]{1,0:T(8,128)S(1)} %get-tuple-element.69.keep, f32[136,128]{1,0:T(8,128)S(1)} %collective-permute-done.10.recv, f32[64,128]{1,0:T(8,128)S(1)} %get-tuple-element.70.wet_keep, f32[8,128]{1,0:T(8,128)S(1)} %slice_add_fusion.8.wet_sum, ...), custom_call_target="tpu_custom_call" | custom-call | tf_op jit(solution)/shard_map/pallas_call | solution.py:670
  43.2 0.6 collective-permute-start.12
  43.9 0.5 shard_map.147
  44.3 1.4 %collective-permute-start.11 = (bf16[16,1024]{1,0:T(8,128)(2,1)S(1)}, bf16[16,1024]{1,0:T(8,128)(2,1)S(1)}, u32[]{:S(2)}, u32[]{:S(2)}) collective-permute-start(bf16[16,1024]{1,0:T(8,128)(2,1)S(1)} %get-tuple-element.58), channel_id=1, source_target_pairs={{0,16},{16,0},{1,17},{17,1},{2,18},{18,2},{3,19},{19,3},{4,20},{20... | collective-permute-start | bytes 98312 | tf_op jit(solution)/shard_map/ppermute | solution.py:676
  45.7 2.7 %collective-permute-done.12.recv = bf16[48,1024]{1,0:T(8,128)(2,1)S(1)} collective-permute-done((bf16[48,1024]{1,0:T(8,128)(2,1)S(1)}, bf16[48,1024]{1,0:T(8,128)(2,1)S(1)}, u32[]{:S(2)}, u32[]{:S(2)}) %collective-permute-start.12) | collective-permute-done | bytes 98336 | tf_op jit(solution)/shard_map/ppermute | solution.py:676
  48.4 0.9 %shard_map.149.rest_0_ = f32[48,128]{1,0:T(8,128)S(1)} custom-call(f32[48,1024]{1,0:T(8,128)S(1)} %get-tuple-element.62.own, bf16[48,1024]{1,0:T(8,128)(2,1)S(1)} %collective-permute-done.12.recv, f32[1,1024]{1,0:T(1,128)S(1)} %get-tuple-element.59.love, bf16[16,1024,128]{2,1,0:T(8,128)(2,1)S(1)} %get-tuple-element.60.table, ...), custom_call_target="tpu_custom_call" | custom-call | tf_op jit(solution)/shard_map/pallas_call | solution.py:685
  49.4 0.0 collective-permute-done.11.recv
  49.4 0.4 shard_map.150
  49.7 0.0 collective-permute-start.13
  49.8 3.2 %collective-permute-done.13 = bf16[64,128]{1,0:T(8,128)(2,1)S(1)} collective-permute-done((bf16[64,128]{1,0:T(8,128)(2,1)S(1)}, bf16[64,128]{1,0:T(8,128)(2,1)S(1)}, u32[]{:S(2)}, u32[]{:S(2)}) %collective-permute-start.13) | collective-permute-done | bytes 16416 | tf_op jit(solution)/shard_map/ppermute | solution.py:603
  52.9 0.9 %collective-permute-start.14 = (bf16[128,128]{1,0:T(8,128)(2,1)S(1)}, bf16[128,128]{1,0:T(8,128)(2,1)S(1)}, u32[]{:S(2)}, u32[]{:S(2)}) collective-permute-start(bf16[128,128]{1,0:T(8,128)(2,1)S(1)} %pad_maximum_fusion.5), channel_id=1, source_target_pairs={{0,9},{1,8},{2,11},{3,10},{4,13},{5,12},{6,15},{7,14},{8,1},{9,0},... | collective-permute-start | bytes 98312 | tf_op jit(solution)/shard_map/ppermute | solution.py:603
  53.9 4.1 %collective-permute-done.14 = bf16[128,128]{1,0:T(8,128)(2,1)S(1)} collective-permute-done((bf16[128,128]{1,0:T(8,128)(2,1)S(1)}, bf16[128,128]{1,0:T(8,128)(2,1)S(1)}, u32[]{:S(2)}, u32[]{:S(2)}) %collective-permute-start.14) | collective-permute-done | bytes 32800 | tf_op jit(solution)/shard_map/ppermute | solution.py:603
  57.9 0.0 collective-permute-start.15
  57.9 4.1 %collective-permute-done.15 = bf16[256,128]{1,0:T(8,128)(2,1)S(1)} collective-permute-done((bf16[256,128]{1,0:T(8,128)(2,1)S(1)}, bf16[256,128]{1,0:T(8,128)(2,1)S(1)}, u32[]{:S(2)}, u32[]{:S(2)}) %collective-permute-start.15) | collective-permute-done | bytes 65568 | tf_op jit(solution)/shard_map/ppermute | solution.py:603
  62.1 0.2 collective-permute-start.16
  62.2 0.8 %shard_map.143 = (f32[128,128]{1,0:T(8,128)}, f32[128,128]{1,0:T(8,128)}, f32[128,128]{1,0:T(8,128)}) custom-call(f32[3,144,256]{2,1,0:T(8,128)S(1)} %get-tuple-element.42.state, f32[3,144,256]{2,1,0:T(8,128)S(1)} %get-tuple-element.43.static, f32[4,144,256]{2,1,0:T(8,128)S(1)} %get-tuple-element.39.rest_1_.forcing, ...), custom_call_target="tpu_custom_call" | custom-call | tf_op jit(solution)/shard_map/pallas_call | solution.py:697
  63.0 0.2 shard_map.151.started
  63.2 0.2 collective-permute-done.16.far
  63.5 0.8 %shard_map.152 = f32[128,128]{1,0:T(8,128)} custom-call(bf16[256,1024]{1,0:T(8,128)(2,1)S(1)} %get-tuple-element.47.inverse, f32[256,128]{1,0:T(8,128)S(1)} %shard_map.151.started, bf16[512,128]{1,0:T(8,128)(2,1)S(1)} %collective-permute-done.16.far), custom_call_target="tpu_custom_call" | custom-call | tf_op jit(solution)/shard_map/pallas_call | solution.py:696
  (14 shorter events, 0.1 us)
Async XLA Ops:
  1.6 7.7 %collective-permute-start = (f32[22,8,128]{2,1,0:T(8,128)S(1)}, f32[22,8,128]{2,1,0:T(8,128)S(1)}, u32[]{:S(2)}, u32[]{:S(2)}) collective-permute-start(f32[22,8,128]{2,1,0:T(8,128)S(1)} %get-tuple-element.35), channel_id=1, source_target_pairs={{0,1},{1,0},{2,3},{3,2},{4,5},{5,4},{6,7},{7,6},{8,9},{9,8},{10,11... | collective-permute-start | bytes 270344 | tf_op jit(solution)/shard_map/ppermute | solution.py:558
  2.2 7.1 %collective-permute-start.1 = (f32[6,8,128]{2,1,0:T(8,128)S(1)}, f32[6,8,128]{2,1,0:T(8,128)S(1)}, u32[]{:S(2)}, u32[]{:S(2)}) collective-permute-start(f32[6,8,128]{2,1,0:T(8,128)S(1)} %get-tuple-element.36), channel_id=1, source_target_pairs={{0,15},{1,2},{2,1},{3,4},{4,3},{5,6},{6,5},{7,8},{8,7},{9,10},{10,... | collective-permute-start | bytes 73736 | tf_op jit(solution)/shard_map/ppermute | solution.py:558
  9.4 4.1 %collective-permute-start.2 = (f32[12,8,128]{2,1,0:T(8,128)S(1)}, f32[12,8,128]{2,1,0:T(8,128)S(1)}, u32[]{:S(2)}, u32[]{:S(2)}) collective-permute-start(f32[12,8,128]{2,1,0:T(8,128)S(1)} %get-tuple-element.38), channel_id=1, source_target_pairs={{0,16},{1,17},{2,18},{3,19},{4,20},{5,21},{6,22},{7,23},{8,24},{9,... | collective-permute-start | bytes 147464 | tf_op jit(solution)/shard_map/ppermute | solution.py:558
  14.7 1.6 %collective-permute-start.3 = (f32[520,128]{1,0:T(8,128)S(1)}, f32[520,128]{1,0:T(8,128)S(1)}, u32[]{:S(2)}, u32[]{:S(2)}) collective-permute-start(f32[520,128]{1,0:T(8,128)S(1)} %get-tuple-element.49), channel_id=1, source_target_pairs={{0,1},{1,0},{2,3},{3,2},{4,5},{5,4},{6,7},{7,6},{8,9},{9,8},{10,11... | collective-permute-start | bytes 798728 | tf_op jit(solution)/shard_map/ppermute | solution.py:603
  16.4 10.1 %collective-permute-start.4 = (f32[264,128]{1,0:T(8,128)S(1)}, f32[264,128]{1,0:T(8,128)S(1)}, u32[]{:S(2)}, u32[]{:S(2)}) collective-permute-start(f32[264,128]{1,0:T(8,128)S(1)} %pad_maximum_fusion), channel_id=1, source_target_pairs={{0,3},{1,2},{2,1},{3,0},{4,7},{5,6},{6,5},{7,4},{8,11},{9,10},{10,... | collective-permute-start | bytes 405512 | tf_op jit(solution)/shard_map/ppermute | solution.py:603
  16.5 7.0 %collective-permute-start.8 = (bf16[256,128]{1,0:T(8,128)(2,1)S(1)}, bf16[256,128]{1,0:T(8,128)(2,1)S(1)}, u32[]{:S(2)}, u32[]{:S(2)}) collective-permute-start(bf16[256,128]{1,0:T(8,128)(2,1)S(1)} %get-tuple-element.51.pair), channel_id=1, source_target_pairs={{0,3},{1,2},{2,1},{3,0},{4,7},{5,6},{6,5},{7,4},{8,11},{9,10},{10,... | collective-permute-start | bytes 196616 | tf_op jit(solution)/shard_map/ppermute | solution.py:603
  24.1 6.7 %collective-permute-start.9 = (f32[128,128]{1,0:T(8,128)S(1)}, f32[128,128]{1,0:T(8,128)S(1)}, u32[]{:S(2)}, u32[]{:S(2)}) collective-permute-start(f32[128,128]{1,0:T(8,128)S(1)} %get-tuple-element.53), channel_id=1, source_target_pairs={{0,9},{1,8},{2,11},{3,10},{4,13},{5,12},{6,15},{7,14},{8,1},{9,0},... | collective-permute-start | bytes 196616 | tf_op jit(solution)/shard_map/ppermute | solution.py:603
  24.6 3.9 %collective-permute-start.6 = (f32[8,128]{1,0:T(8,128)S(1)}, f32[8,128]{1,0:T(8,128)S(1)}, u32[]{:S(2)}, u32[]{:S(2)}) collective-permute-start(f32[8,128]{1,0:T(8,128)S(1)} %slice_add_fusion.11), channel_id=1, source_target_pairs={{0,19},{1,18},{2,17},{3,16},{4,23},{5,22},{6,21},{7,20},{8,27},{9,... | collective-permute-start | bytes 12296 | tf_op jit(solution)/shard_map/ppermute | solution.py:558
  26.2 3.0 %collective-permute-start.5 = (f32[8,128]{1,0:T(8,128)S(1)}, f32[8,128]{1,0:T(8,128)S(1)}, u32[]{:S(2)}, u32[]{:S(2)}) collective-permute-start(f32[8,128]{1,0:T(8,128)S(1)} %slice_add_fusion.11), channel_id=1, source_target_pairs={{0,17},{1,16},{2,19},{3,18},{4,21},{5,20},{6,23},{7,22},{8,25},{9,... | collective-permute-start | bytes 12296 | tf_op jit(solution)/shard_map/ppermute | solution.py:558
  29.2 4.8 %collective-permute-start.7 = (f32[136,128]{1,0:T(8,128)S(1)}, f32[136,128]{1,0:T(8,128)S(1)}, u32[]{:S(2)}, u32[]{:S(2)}) collective-permute-start(f32[136,128]{1,0:T(8,128)S(1)} %pad_maximum_fusion.2), channel_id=1, source_target_pairs={{0,9},{1,8},{2,11},{3,10},{4,13},{5,12},{6,15},{7,14},{8,1},{9,0},... | collective-permute-start | bytes 208904 | tf_op jit(solution)/shard_map/ppermute | solution.py:603
  34.1 8.1 %collective-permute-start.10 = (f32[136,128]{1,0:T(8,128)S(1)}, f32[136,128]{1,0:T(8,128)S(1)}, u32[]{:S(2)}, u32[]{:S(2)}) collective-permute-start(f32[136,128]{1,0:T(8,128)S(1)} %pad_maximum_fusion.3), channel_id=1, source_target_pairs={{0,5},{1,4},{2,7},{3,6},{4,1},{5,0},{6,3},{7,2},{8,13},{9,12},{10,... | collective-permute-start | bytes 208904 | tf_op jit(solution)/shard_map/ppermute | solution.py:603
  43.2 5.2 %collective-permute-start.12 = (bf16[48,1024]{1,0:T(8,128)(2,1)S(1)}, bf16[48,1024]{1,0:T(8,128)(2,1)S(1)}, u32[]{:S(2)}, u32[]{:S(2)}) collective-permute-start(bf16[48,1024]{1,0:T(8,128)(2,1)S(1)} %get-tuple-element.63), channel_id=1, source_target_pairs={{0,16},{16,0},{1,17},{17,1},{2,18},{18,2},{3,19},{19,3},{4,20},{20... | collective-permute-start | bytes 294920 | tf_op jit(solution)/shard_map/ppermute | solution.py:676
  44.3 5.0 %collective-permute-start.11 = (bf16[16,1024]{1,0:T(8,128)(2,1)S(1)}, bf16[16,1024]{1,0:T(8,128)(2,1)S(1)}, u32[]{:S(2)}, u32[]{:S(2)}) collective-permute-start(bf16[16,1024]{1,0:T(8,128)(2,1)S(1)} %get-tuple-element.58), channel_id=1, source_target_pairs={{0,16},{16,0},{1,17},{17,1},{2,18},{18,2},{3,19},{19,3},{4,20},{20... | collective-permute-start | bytes 98312 | tf_op jit(solution)/shard_map/ppermute | solution.py:676
  49.7 3.2 %collective-permute-start.13 = (bf16[64,128]{1,0:T(8,128)(2,1)S(1)}, bf16[64,128]{1,0:T(8,128)(2,1)S(1)}, u32[]{:S(2)}, u32[]{:S(2)}) collective-permute-start(bf16[64,128]{1,0:T(8,128)(2,1)S(1)} %shard_map.150), channel_id=1, source_target_pairs={{0,5},{1,4},{2,7},{3,6},{4,1},{5,0},{6,3},{7,2},{8,13},{9,12},{10,... | collective-permute-start | bytes 49160 | tf_op jit(solution)/shard_map/ppermute | solution.py:603
  52.9 5.0 %collective-permute-start.14 = (bf16[128,128]{1,0:T(8,128)(2,1)S(1)}, bf16[128,128]{1,0:T(8,128)(2,1)S(1)}, u32[]{:S(2)}, u32[]{:S(2)}) collective-permute-start(bf16[128,128]{1,0:T(8,128)(2,1)S(1)} %pad_maximum_fusion.5), channel_id=1, source_target_pairs={{0,9},{1,8},{2,11},{3,10},{4,13},{5,12},{6,15},{7,14},{8,1},{9,0},... | collective-permute-start | bytes 98312 | tf_op jit(solution)/shard_map/ppermute | solution.py:603
  57.9 4.1 %collective-permute-start.15 = (bf16[256,128]{1,0:T(8,128)(2,1)S(1)}, bf16[256,128]{1,0:T(8,128)(2,1)S(1)}, u32[]{:S(2)}, u32[]{:S(2)}) collective-permute-start(bf16[256,128]{1,0:T(8,128)(2,1)S(1)} %pad_maximum_fusion.4), channel_id=1, source_target_pairs={{0,3},{1,2},{2,1},{3,0},{4,7},{5,6},{6,5},{7,4},{8,11},{9,10},{10,... | collective-permute-start | bytes 196616 | tf_op jit(solution)/shard_map/ppermute | solution.py:603
  62.1 1.4 %collective-permute-start.16 = (bf16[512,128]{1,0:T(8,128)(2,1)S(1)}, bf16[512,128]{1,0:T(8,128)(2,1)S(1)}, u32[]{:S(2)}, u32[]{:S(2)}) collective-permute-start(bf16[512,128]{1,0:T(8,128)(2,1)S(1)} %pad_maximum_fusion.1.near), channel_id=1, source_target_pairs={{0,1},{1,0},{2,3},{3,2},{4,5},{5,4},{6,7},{7,6},{8,9},{9,8},{10,11... | collective-permute-start | bytes 393224 | tf_op jit(solution)/shard_map/ppermute | solution.py:603

commit v5 on v4

--- a/solution.py
+++ b/solution.py
@@ -318,7 +318,7 @@
         forcing,
         latitude,
         forward,
-        keep,
+        held,
         send,
         wet_sum,
         state,
@@ -378,7 +378,7 @@
     upper = jnp.concatenate([high, low], axis=1)
     under = jnp.concatenate([high, jnp.zeros_like(low)], axis=1)
     weights = jnp.concatenate([upper, under], axis=0)
-    half = keep.shape[0]
+    half = forward.shape[0] // 2
 
     def transform(span):
         both = jnp.dot(forward[span], weights, preferred_element_type=f32)
@@ -386,7 +386,13 @@
 
     send[:half] = transform(slice(half, 2 * half))
     send[half:] = level
-    keep[...] = transform(slice(0, half))
+    held[...] = weights
+
+
+def keep_kernel(forward, weights, keep):
+    half, lat_dev = keep.shape
+    both = jnp.dot(forward[:half], weights[...], preferred_element_type=f32)
+    keep[...] = both[:, :lat_dev] + both[:, lat_dev:]
 
 
 def finish_kernel(state, static, forcing, latitude, height_out, east_out, north_out):
@@ -604,14 +610,19 @@
 
     wet_far = swap(wet_pair, gens[1])
 
-    keep, send, wet_sum, state, static = call(
+    held, send, wet_sum, state, static = call(
         functools.partial(step_kernel, lat_count),
-        [shaped(half, lat_dev), shaped(half + 8, lat_dev), shaped(8, lat_dev)]
+        [
+            shaped(2 * lon_dev, 2 * lat_dev, dtype=bf16),
+            shaped(half + 8, lat_dev),
+            shaped(8, lat_dev),
+        ]
         + [pltpu.VMEM((3, wide, 2 * lat_dev), f32)] * 2,
         in_specs=[vmem] * (6 + len(facing)),
     )(own, near, away, *facing, forcing, latitude, forward)
 
     recv = swap(send, gens[0])
+    keep = call(keep_kernel, shaped(half, lat_dev))(forward, held)
     wet_keep, wet_send = call(
         functools.partial(mask_kernel, (lon_dev, total_cols, wave_dev, tuple(gens))),
         [shaped(half // 4, lat_dev)] * 2,

time: 64.6 us -> 64.5 us (level)
    pallas_call x1 -> x2, Pallas kernels: 1.24 us -> 1.41 us  [the longest x1 1.18 us: shards(): call(functools.partial(step_kernel, lat_count), [shaped(2 * lon_dev, 2 *...]
  transfers between devices with their start and end apart: 17 -> 17, of which waited for: 12 -> 12; matrix products, arithmetic and copies ran while one was open for 0% -> 0% of each run, Pallas kernels for 17% -> 18%
where the time goes in v5:
time: 64.5 us; the launch traced here: 64.3 us
  waiting for transfers between devices  27.7 us (43%)
  starting transfers between devices  19.7 us (31%)
  Pallas kernels  15.9 us (25%)
  between operations  0.79 us (1%)
    ppermute x10, waiting for transfers between devices, swap(): return lax.ppermute(cells, 'lon', [(i, i ^ gen) for i in range(lon_count)])  21.3 us
    ppermute x5, starting transfers between devices, shift(): return lax.ppermute(cells, ('lat', 'lon'), pairs)  9.65 us
    ppermute x10, starting transfers between devices, swap(): return lax.ppermute(cells, 'lon', [(i, i ^ gen) for i in range(lon_count)])  8.04 us
    pallas_call x2, Pallas kernels, shards(): call(functools.partial(fetch_kernel, piece * waves), [pltpu.VMEM((waves,...  5.12 us
    ppermute x5, waiting for transfers between devices, shift(): return lax.ppermute(cells, ('lat', 'lon'), pairs)  3.75 us
    ppermute x2, waiting for transfers between devices, shards(): lax.ppermute(moving, 'lat', [(i, i ^ 1 << b) for i in range(lat_count)])  2.68 us
    ppermute x2, starting transfers between devices, shards(): lax.ppermute(moving, 'lat', [(i, i ^ 1 << b) for i in range(lat_count)])  2.04 us
    pallas_call x1, Pallas kernels, shards(): call(functools.partial(table_kernel, (lon_dev, lat_dev, total_cols, total...  1.81 us
  transfers between devices with their start and end apart: 17, of which 12 were waited for; matrix products, arithmetic and copies ran while one was open for 0% of the time, Pallas kernels for 18%

profile of v5, /device:TPU:0, one launch (start us, length us, event | category | flops | bytes accessed | tf_op | source)
XLA Modules:
  0.0 64.3 jit_solution(8530350959105787861)
XLA Ops:
  0.6 1.0 %shard_map.139 = (f32[22,8,128]{2,1,0:T(8,128)S(1)}, f32[6,8,128]{2,1,0:T(8,128)S(1)}) custom-call(f32[128,128]{1,0:T(8,128)} %sea.3, f32[128,128]{1,0:T(8,128)} %east.3, f32[128,128]{1,0:T(8,128)} %north.3, f32[128,128]{1,0:T(8,128)} %depth.3, s32[128,128]{1,0:T(8,128)} %mask.3, f32[128,128]{1,0:T(8,128)} %loading.3), custom_call_target="tpu_custom_call" | custom-call | tf_op jit(solution)/shard_map/pallas_call | solution.py:528
  1.6 0.6 collective-permute-start
  2.2 5.6 %collective-permute-start.1 = (f32[6,8,128]{2,1,0:T(8,128)S(1)}, f32[6,8,128]{2,1,0:T(8,128)S(1)}, u32[]{:S(2)}, u32[]{:S(2)}) collective-permute-start(f32[6,8,128]{2,1,0:T(8,128)S(1)} %get-tuple-element.36), channel_id=1, source_target_pairs={{0,15},{1,2},{2,1},{3,4},{4,3},{5,6},{6,5},{7,8},{8,7},{9,10},{10,... | collective-permute-start | bytes 73736 | tf_op jit(solution)/shard_map/ppermute | solution.py:564
  7.8 1.2 %shard_map.138 = (f32[6,128,128]{2,1,0:T(8,128)S(1)}, f32[6,8,128]{2,1,0:T(8,128)S(1)}) custom-call(f32[128,128]{1,0:T(8,128)} %sea.3, f32[128,128]{1,0:T(8,128)} %east.3, f32[128,128]{1,0:T(8,128)} %north.3, f32[128,128]{1,0:T(8,128)} %depth.3, s32[128,128]{1,0:T(8,128)} %mask.3, f32[128,128]{1,0:T(8,128)} %loading.3), custom_call_target="tpu_custom_call" | custom-call | tf_op jit(solution)/shard_map/pallas_call | solution.py:537
  9.0 0.3 collective-permute-done.1.away
  9.3 0.0 collective-permute-done.near
  9.3 0.1 shard_map.140
  9.4 1.5 %collective-permute-start.2 = (f32[12,8,128]{2,1,0:T(8,128)S(1)}, f32[12,8,128]{2,1,0:T(8,128)S(1)}, u32[]{:S(2)}, u32[]{:S(2)}) collective-permute-start(f32[12,8,128]{2,1,0:T(8,128)S(1)} %get-tuple-element.38), channel_id=1, source_target_pairs={{0,16},{1,17},{2,18},{3,19},{4,20},{5,21},{6,22},{7,23},{8,24},{9,... | collective-permute-start | bytes 147464 | tf_op jit(solution)/shard_map/ppermute | solution.py:564
  10.9 1.8 %shard_map.141 = (bf16[1024,256]{1,0:T(8,128)(2,1)S(1)}, bf16[256,1024]{1,0:T(8,128)(2,1)S(1)}, f32[4,144,256]{2,1,0:T(8,128)S(1)}, f32[3,8,256]{2,1,0:T(8,128)S...) custom-call(f32[1,8]{1,0:T(1,128)} %bitcast.4, f32[1,8]{1,0:T(1,128)} %bitcast.5, f32[1,1024]{1,0:T(1,128)} %bitcast.3, ...), custom_call_target="tpu_custom_call" | custom-call | tf_op jit(solution)/shard_map/pallas_call | solution.py:582
  12.7 0.7 %collective-permute-done.2.rest_0_ = f32[12,8,128]{2,1,0:T(8,128)S(1)} collective-permute-done((f32[12,8,128]{2,1,0:T(8,128)S(1)}, f32[12,8,128]{2,1,0:T(8,128)S(1)}, u32[]{:S(2)}, u32[]{:S(2)}) %collective-permute-start.2) | collective-permute-done | bytes 49184 | tf_op jit(solution)/shard_map/ppermute | solution.py:564
  13.5 1.2 %shard_map.142 = (bf16[256,256]{1,0:T(8,128)(2,1)S(1)}, f32[520,128]{1,0:T(8,128)S(1)}, f32[8,128]{1,0:T(8,128)S(1)}, f32[3,144,256]{2,1,0:T(8,128)S(1)}, f32[3,144,256]{2,1,0:T(8,128)S(1)}) custom-call(f32[6,128,128]{2,1,0:T(8,128)S(1)} %get-tuple-element.34.own, f32[22,8,128]{2,1,0:T(8,128)S(1)} %collective-permute-done.near, ...), custom_call_target="tpu_custom_call" | custom-call | tf_op jit(solution)/shard_map/pallas_call | solution.py:613
  14.7 0.1 collective-permute-start.3
  14.8 0.2 shard_map.144
  15.0 1.3 %collective-permute-done.3 = f32[520,128]{1,0:T(8,128)S(1)} collective-permute-done((f32[520,128]{1,0:T(8,128)S(1)}, f32[520,128]{1,0:T(8,128)S(1)}, u32[]{:S(2)}, u32[]{:S(2)}) %collective-permute-start.3) | collective-permute-done | bytes 266272 | tf_op jit(solution)/shard_map/ppermute | solution.py:609
  16.4 0.1 collective-permute-start.4
  16.4 1.7 %collective-permute-start.8 = (bf16[256,128]{1,0:T(8,128)(2,1)S(1)}, bf16[256,128]{1,0:T(8,128)(2,1)S(1)}, u32[]{:S(2)}, u32[]{:S(2)}) collective-permute-start(bf16[256,128]{1,0:T(8,128)(2,1)S(1)} %get-tuple-element.51.pair), channel_id=1, source_target_pairs={{0,3},{1,2},{2,1},{3,0},{4,7},{5,6},{6,5},{7,4},{8,11},{9,10},{10,... | collective-permute-start | bytes 196616 | tf_op jit(solution)/shard_map/ppermute | solution.py:609
  18.2 5.2 %collective-permute-done.8.far = bf16[256,128]{1,0:T(8,128)(2,1)S(1)} collective-permute-done((bf16[256,128]{1,0:T(8,128)(2,1)S(1)}, bf16[256,128]{1,0:T(8,128)(2,1)S(1)}, u32[]{:S(2)}, u32[]{:S(2)}) %collective-permute-start.8) | collective-permute-done | bytes 65568 | tf_op jit(solution)/shard_map/ppermute | solution.py:609
  23.4 0.6 shard_map.145
  24.0 0.5 collective-permute-start.9
  24.5 1.6 %collective-permute-start.6 = (f32[8,128]{1,0:T(8,128)S(1)}, f32[8,128]{1,0:T(8,128)S(1)}, u32[]{:S(2)}, u32[]{:S(2)}) collective-permute-start(f32[8,128]{1,0:T(8,128)S(1)} %slice_add_fusion.11), channel_id=1, source_target_pairs={{0,19},{1,18},{2,17},{3,16},{4,23},{5,22},{6,21},{7,20},{8,27},{9,... | collective-permute-start | bytes 12296 | tf_op jit(solution)/shard_map/ppermute | solution.py:564
  26.1 0.3 collective-permute-start.5
  26.4 0.0 collective-permute-done.4
  26.5 2.0 %collective-permute-done.6 = f32[8,128]{1,0:T(8,128)S(1)} collective-permute-done((f32[8,128]{1,0:T(8,128)S(1)}, f32[8,128]{1,0:T(8,128)S(1)}, u32[]{:S(2)}, u32[]{:S(2)}) %collective-permute-start.6) | collective-permute-done | bytes 4128 | tf_op jit(solution)/shard_map/ppermute | solution.py:564
  28.4 0.7 %collective-permute-done.5 = f32[8,128]{1,0:T(8,128)S(1)} collective-permute-done((f32[8,128]{1,0:T(8,128)S(1)}, f32[8,128]{1,0:T(8,128)S(1)}, u32[]{:S(2)}, u32[]{:S(2)}) %collective-permute-start.5) | collective-permute-done | bytes 4128 | tf_op jit(solution)/shard_map/ppermute | solution.py:564
  29.2 1.6 %collective-permute-start.7 = (f32[136,128]{1,0:T(8,128)S(1)}, f32[136,128]{1,0:T(8,128)S(1)}, u32[]{:S(2)}, u32[]{:S(2)}) collective-permute-start(f32[136,128]{1,0:T(8,128)S(1)} %pad_maximum_fusion.2), channel_id=1, source_target_pairs={{0,9},{1,8},{2,11},{3,10},{4,13},{5,12},{6,15},{7,14},{8,1},{9,0},... | collective-permute-start | bytes 208904 | tf_op jit(solution)/shard_map/ppermute | solution.py:609
  30.8 0.0 collective-permute-done.9
  30.8 3.2 %collective-permute-done.7 = f32[136,128]{1,0:T(8,128)S(1)} collective-permute-done((f32[136,128]{1,0:T(8,128)S(1)}, f32[136,128]{1,0:T(8,128)S(1)}, u32[]{:S(2)}, u32[]{:S(2)}) %collective-permute-start.7) | collective-permute-done | bytes 69664 | tf_op jit(solution)/shard_map/ppermute | solution.py:609
  34.0 3.0 %collective-permute-start.10 = (f32[136,128]{1,0:T(8,128)S(1)}, f32[136,128]{1,0:T(8,128)S(1)}, u32[]{:S(2)}, u32[]{:S(2)}) collective-permute-start(f32[136,128]{1,0:T(8,128)S(1)} %pad_maximum_fusion.3), channel_id=1, source_target_pairs={{0,5},{1,4},{2,7},{3,6},{4,1},{5,0},{6,3},{7,2},{8,13},{9,12},{10,... | collective-permute-start | bytes 208904 | tf_op jit(solution)/shard_map/ppermute | solution.py:609
  37.0 2.6 %shard_map.146 = (bf16[16,1024,128]{2,1,0:T(8,128)(2,1)S(1)}, bf16[16,128,1024]{2,1,0:T(8,128)(2,1)S(1)}) custom-call(bf16[32,1024,128]{2,1,0:T(8,128)(2,1)} %source.3), custom_call_target="tpu_custom_call" | custom-call | tf_op jit(solution)/shard_map/pallas_call | solution.py:666
  39.6 2.6 %shard_map.147 = (bf16[16,1024,128]{2,1,0:T(8,128)(2,1)S(1)}, bf16[16,128,1024]{2,1,0:T(8,128)(2,1)S(1)}) custom-call(bf16[32,1024,128]{2,1,0:T(8,128)(2,1)} %source.3), custom_call_target="tpu_custom_call" | custom-call | tf_op jit(solution)/shard_map/pallas_call | solution.py:666
  42.1 0.0 collective-permute-done.10.recv
  42.1 1.0 %shard_map.149 = (f32[48,1024]{1,0:T(8,128)S(1)}, bf16[48,1024]{1,0:T(8,128)(2,1)S(1)}) custom-call(f32[64,128]{1,0:T(8,128)S(1)} %get-tuple-element.69.keep, f32[136,128]{1,0:T(8,128)S(1)} %collective-permute-done.10.recv, f32[64,128]{1,0:T(8,128)S(1)} %get-tuple-element.70.wet_keep, f32[8,128]{1,0:T(8,128)S(1)} %slice_add_fusion.8.wet_sum, ...), custom_call_target="tpu_custom_call" | custom-call | tf_op jit(solution)/shard_map/pallas_call | solution.py:681
  43.2 0.6 %collective-permute-start.12 = (bf16[48,1024]{1,0:T(8,128)(2,1)S(1)}, bf16[48,1024]{1,0:T(8,128)(2,1)S(1)}, u32[]{:S(2)}, u32[]{:S(2)}) collective-permute-start(bf16[48,1024]{1,0:T(8,128)(2,1)S(1)} %get-tuple-element.63), channel_id=1, source_target_pairs={{0,16},{16,0},{1,17},{17,1},{2,18},{18,2},{3,19},{19,3},{4,20},{20... | collective-permute-start | bytes 294920 | tf_op jit(solution)/shard_map/ppermute | solution.py:687
  43.8 0.5 shard_map.148
  44.3 1.4 %collective-permute-start.11 = (bf16[16,1024]{1,0:T(8,128)(2,1)S(1)}, bf16[16,1024]{1,0:T(8,128)(2,1)S(1)}, u32[]{:S(2)}, u32[]{:S(2)}) collective-permute-start(bf16[16,1024]{1,0:T(8,128)(2,1)S(1)} %get-tuple-element.58), channel_id=1, source_target_pairs={{0,16},{16,0},{1,17},{17,1},{2,18},{18,2},{3,19},{19,3},{4,20},{20... | collective-permute-start | bytes 98312 | tf_op jit(solution)/shard_map/ppermute | solution.py:687
  45.7 2.7 %collective-permute-done.12.recv = bf16[48,1024]{1,0:T(8,128)(2,1)S(1)} collective-permute-done((bf16[48,1024]{1,0:T(8,128)(2,1)S(1)}, bf16[48,1024]{1,0:T(8,128)(2,1)S(1)}, u32[]{:S(2)}, u32[]{:S(2)}) %collective-permute-start.12) | collective-permute-done | bytes 98336 | tf_op jit(solution)/shard_map/ppermute | solution.py:687
  48.4 0.9 %shard_map.150.rest_0_ = f32[48,128]{1,0:T(8,128)S(1)} custom-call(f32[48,1024]{1,0:T(8,128)S(1)} %get-tuple-element.62.own, bf16[48,1024]{1,0:T(8,128)(2,1)S(1)} %collective-permute-done.12.recv, f32[1,1024]{1,0:T(1,128)S(1)} %get-tuple-element.59.love, bf16[16,1024,128]{2,1,0:T(8,128)(2,1)S(1)} %get-tuple-element.60.table, ...), custom_call_target="tpu_custom_call" | custom-call | tf_op jit(solution)/shard_map/pallas_call | solution.py:696
  49.3 0.0 collective-permute-done.11.recv
  49.3 0.4 shard_map.151
  49.7 0.0 collective-permute-start.13
  49.7 3.2 %collective-permute-done.13 = bf16[64,128]{1,0:T(8,128)(2,1)S(1)} collective-permute-done((bf16[64,128]{1,0:T(8,128)(2,1)S(1)}, bf16[64,128]{1,0:T(8,128)(2,1)S(1)}, u32[]{:S(2)}, u32[]{:S(2)}) %collective-permute-start.13) | collective-permute-done | bytes 16416 | tf_op jit(solution)/shard_map/ppermute | solution.py:609
  52.9 1.0 %collective-permute-start.14 = (bf16[128,128]{1,0:T(8,128)(2,1)S(1)}, bf16[128,128]{1,0:T(8,128)(2,1)S(1)}, u32[]{:S(2)}, u32[]{:S(2)}) collective-permute-start(bf16[128,128]{1,0:T(8,128)(2,1)S(1)} %pad_maximum_fusion.5), channel_id=1, source_target_pairs={{0,9},{1,8},{2,11},{3,10},{4,13},{5,12},{6,15},{7,14},{8,1},{9,0},... | collective-permute-start | bytes 98312 | tf_op jit(solution)/shard_map/ppermute | solution.py:609
  53.8 4.1 %collective-permute-done.14 = bf16[128,128]{1,0:T(8,128)(2,1)S(1)} collective-permute-done((bf16[128,128]{1,0:T(8,128)(2,1)S(1)}, bf16[128,128]{1,0:T(8,128)(2,1)S(1)}, u32[]{:S(2)}, u32[]{:S(2)}) %collective-permute-start.14) | collective-permute-done | bytes 32800 | tf_op jit(solution)/shard_map/ppermute | solution.py:609
  57.9 0.0 collective-permute-start.15
  57.9 4.1 %collective-permute-done.15 = bf16[256,128]{1,0:T(8,128)(2,1)S(1)} collective-permute-done((bf16[256,128]{1,0:T(8,128)(2,1)S(1)}, bf16[256,128]{1,0:T(8,128)(2,1)S(1)}, u32[]{:S(2)}, u32[]{:S(2)}) %collective-permute-start.15) | collective-permute-done | bytes 65568 | tf_op jit(solution)/shard_map/ppermute | solution.py:609
  62.0 0.2 collective-permute-start.16
  62.2 0.8 %shard_map.143 = (f32[128,128]{1,0:T(8,128)}, f32[128,128]{1,0:T(8,128)}, f32[128,128]{1,0:T(8,128)}) custom-call(f32[3,144,256]{2,1,0:T(8,128)S(1)} %get-tuple-element.42.state, f32[3,144,256]{2,1,0:T(8,128)S(1)} %get-tuple-element.43.static, f32[4,144,256]{2,1,0:T(8,128)S(1)} %get-tuple-element.39.rest_1_.forcing, ...), custom_call_target="tpu_custom_call" | custom-call | tf_op jit(solution)/shard_map/pallas_call | solution.py:708
  63.0 0.2 shard_map.152.started
  63.2 0.2 collective-permute-done.16.far
  63.4 0.8 %shard_map.153 = f32[128,128]{1,0:T(8,128)} custom-call(bf16[256,1024]{1,0:T(8,128)(2,1)S(1)} %get-tuple-element.47.inverse, f32[256,128]{1,0:T(8,128)S(1)} %shard_map.152.started, bf16[512,128]{1,0:T(8,128)(2,1)S(1)} %collective-permute-done.16.far), custom_call_target="tpu_custom_call" | custom-call | tf_op jit(solution)/shard_map/pallas_call | solution.py:707
  (14 shorter events, 0.1 us)
Async XLA Ops:
  1.6 7.7 %collective-permute-start = (f32[22,8,128]{2,1,0:T(8,128)S(1)}, f32[22,8,128]{2,1,0:T(8,128)S(1)}, u32[]{:S(2)}, u32[]{:S(2)}) collective-permute-start(f32[22,8,128]{2,1,0:T(8,128)S(1)} %get-tuple-element.35), channel_id=1, source_target_pairs={{0,1},{1,0},{2,3},{3,2},{4,5},{5,4},{6,7},{7,6},{8,9},{9,8},{10,11... | collective-permute-start | bytes 270344 | tf_op jit(solution)/shard_map/ppermute | solution.py:564
  2.2 7.1 %collective-permute-start.1 = (f32[6,8,128]{2,1,0:T(8,128)S(1)}, f32[6,8,128]{2,1,0:T(8,128)S(1)}, u32[]{:S(2)}, u32[]{:S(2)}) collective-permute-start(f32[6,8,128]{2,1,0:T(8,128)S(1)} %get-tuple-element.36), channel_id=1, source_target_pairs={{0,15},{1,2},{2,1},{3,4},{4,3},{5,6},{6,5},{7,8},{8,7},{9,10},{10,... | collective-permute-start | bytes 73736 | tf_op jit(solution)/shard_map/ppermute | solution.py:564
  9.4 4.1 %collective-permute-start.2 = (f32[12,8,128]{2,1,0:T(8,128)S(1)}, f32[12,8,128]{2,1,0:T(8,128)S(1)}, u32[]{:S(2)}, u32[]{:S(2)}) collective-permute-start(f32[12,8,128]{2,1,0:T(8,128)S(1)} %get-tuple-element.38), channel_id=1, source_target_pairs={{0,16},{1,17},{2,18},{3,19},{4,20},{5,21},{6,22},{7,23},{8,24},{9,... | collective-permute-start | bytes 147464 | tf_op jit(solution)/shard_map/ppermute | solution.py:564
  14.7 1.6 %collective-permute-start.3 = (f32[520,128]{1,0:T(8,128)S(1)}, f32[520,128]{1,0:T(8,128)S(1)}, u32[]{:S(2)}, u32[]{:S(2)}) collective-permute-start(f32[520,128]{1,0:T(8,128)S(1)} %get-tuple-element.49), channel_id=1, source_target_pairs={{0,1},{1,0},{2,3},{3,2},{4,5},{5,4},{6,7},{7,6},{8,9},{9,8},{10,11... | collective-permute-start | bytes 798728 | tf_op jit(solution)/shard_map/ppermute | solution.py:609
  16.4 10.1 %collective-permute-start.4 = (f32[264,128]{1,0:T(8,128)S(1)}, f32[264,128]{1,0:T(8,128)S(1)}, u32[]{:S(2)}, u32[]{:S(2)}) collective-permute-start(f32[264,128]{1,0:T(8,128)S(1)} %pad_maximum_fusion), channel_id=1, source_target_pairs={{0,3},{1,2},{2,1},{3,0},{4,7},{5,6},{6,5},{7,4},{8,11},{9,10},{10,... | collective-permute-start | bytes 405512 | tf_op jit(solution)/shard_map/ppermute | solution.py:609
  16.4 7.0 %collective-permute-start.8 = (bf16[256,128]{1,0:T(8,128)(2,1)S(1)}, bf16[256,128]{1,0:T(8,128)(2,1)S(1)}, u32[]{:S(2)}, u32[]{:S(2)}) collective-permute-start(bf16[256,128]{1,0:T(8,128)(2,1)S(1)} %get-tuple-element.51.pair), channel_id=1, source_target_pairs={{0,3},{1,2},{2,1},{3,0},{4,7},{5,6},{6,5},{7,4},{8,11},{9,10},{10,... | collective-permute-start | bytes 196616 | tf_op jit(solution)/shard_map/ppermute | solution.py:609
  24.0 6.7 %collective-permute-start.9 = (f32[128,128]{1,0:T(8,128)S(1)}, f32[128,128]{1,0:T(8,128)S(1)}, u32[]{:S(2)}, u32[]{:S(2)}) collective-permute-start(f32[128,128]{1,0:T(8,128)S(1)} %get-tuple-element.53), channel_id=1, source_target_pairs={{0,9},{1,8},{2,11},{3,10},{4,13},{5,12},{6,15},{7,14},{8,1},{9,0},... | collective-permute-start | bytes 196616 | tf_op jit(solution)/shard_map/ppermute | solution.py:609
  24.5 3.9 %collective-permute-start.6 = (f32[8,128]{1,0:T(8,128)S(1)}, f32[8,128]{1,0:T(8,128)S(1)}, u32[]{:S(2)}, u32[]{:S(2)}) collective-permute-start(f32[8,128]{1,0:T(8,128)S(1)} %slice_add_fusion.11), channel_id=1, source_target_pairs={{0,19},{1,18},{2,17},{3,16},{4,23},{5,22},{6,21},{7,20},{8,27},{9,... | collective-permute-start | bytes 12296 | tf_op jit(solution)/shard_map/ppermute | solution.py:564
  26.1 3.0 %collective-permute-start.5 = (f32[8,128]{1,0:T(8,128)S(1)}, f32[8,128]{1,0:T(8,128)S(1)}, u32[]{:S(2)}, u32[]{:S(2)}) collective-permute-start(f32[8,128]{1,0:T(8,128)S(1)} %slice_add_fusion.11), channel_id=1, source_target_pairs={{0,17},{1,16},{2,19},{3,18},{4,21},{5,20},{6,23},{7,22},{8,25},{9,... | collective-permute-start | bytes 12296 | tf_op jit(solution)/shard_map/ppermute | solution.py:564
  29.2 4.8 %collective-permute-start.7 = (f32[136,128]{1,0:T(8,128)S(1)}, f32[136,128]{1,0:T(8,128)S(1)}, u32[]{:S(2)}, u32[]{:S(2)}) collective-permute-start(f32[136,128]{1,0:T(8,128)S(1)} %pad_maximum_fusion.2), channel_id=1, source_target_pairs={{0,9},{1,8},{2,11},{3,10},{4,13},{5,12},{6,15},{7,14},{8,1},{9,0},... | collective-permute-start | bytes 208904 | tf_op jit(solution)/shard_map/ppermute | solution.py:609
  34.0 8.1 %collective-permute-start.10 = (f32[136,128]{1,0:T(8,128)S(1)}, f32[136,128]{1,0:T(8,128)S(1)}, u32[]{:S(2)}, u32[]{:S(2)}) collective-permute-start(f32[136,128]{1,0:T(8,128)S(1)} %pad_maximum_fusion.3), channel_id=1, source_target_pairs={{0,5},{1,4},{2,7},{3,6},{4,1},{5,0},{6,3},{7,2},{8,13},{9,12},{10,... | collective-permute-start | bytes 208904 | tf_op jit(solution)/shard_map/ppermute | solution.py:609
  43.2 5.2 %collective-permute-start.12 = (bf16[48,1024]{1,0:T(8,128)(2,1)S(1)}, bf16[48,1024]{1,0:T(8,128)(2,1)S(1)}, u32[]{:S(2)}, u32[]{:S(2)}) collective-permute-start(bf16[48,1024]{1,0:T(8,128)(2,1)S(1)} %get-tuple-element.63), channel_id=1, source_target_pairs={{0,16},{16,0},{1,17},{17,1},{2,18},{18,2},{3,19},{19,3},{4,20},{20... | collective-permute-start | bytes 294920 | tf_op jit(solution)/shard_map/ppermute | solution.py:687
  44.3 5.0 %collective-permute-start.11 = (bf16[16,1024]{1,0:T(8,128)(2,1)S(1)}, bf16[16,1024]{1,0:T(8,128)(2,1)S(1)}, u32[]{:S(2)}, u32[]{:S(2)}) collective-permute-start(bf16[16,1024]{1,0:T(8,128)(2,1)S(1)} %get-tuple-element.58), channel_id=1, source_target_pairs={{0,16},{16,0},{1,17},{17,1},{2,18},{18,2},{3,19},{19,3},{4,20},{20... | collective-permute-start | bytes 98312 | tf_op jit(solution)/shard_map/ppermute | solution.py:687
  49.7 3.2 %collective-permute-start.13 = (bf16[64,128]{1,0:T(8,128)(2,1)S(1)}, bf16[64,128]{1,0:T(8,128)(2,1)S(1)}, u32[]{:S(2)}, u32[]{:S(2)}) collective-permute-start(bf16[64,128]{1,0:T(8,128)(2,1)S(1)} %shard_map.151), channel_id=1, source_target_pairs={{0,5},{1,4},{2,7},{3,6},{4,1},{5,0},{6,3},{7,2},{8,13},{9,12},{10,... | collective-permute-start | bytes 49160 | tf_op jit(solution)/shard_map/ppermute | solution.py:609
  52.9 5.0 %collective-permute-start.14 = (bf16[128,128]{1,0:T(8,128)(2,1)S(1)}, bf16[128,128]{1,0:T(8,128)(2,1)S(1)}, u32[]{:S(2)}, u32[]{:S(2)}) collective-permute-start(bf16[128,128]{1,0:T(8,128)(2,1)S(1)} %pad_maximum_fusion.5), channel_id=1, source_target_pairs={{0,9},{1,8},{2,11},{3,10},{4,13},{5,12},{6,15},{7,14},{8,1},{9,0},... | collective-permute-start | bytes 98312 | tf_op jit(solution)/shard_map/ppermute | solution.py:609
  57.9 4.1 %collective-permute-start.15 = (bf16[256,128]{1,0:T(8,128)(2,1)S(1)}, bf16[256,128]{1,0:T(8,128)(2,1)S(1)}, u32[]{:S(2)}, u32[]{:S(2)}) collective-permute-start(bf16[256,128]{1,0:T(8,128)(2,1)S(1)} %pad_maximum_fusion.4), channel_id=1, source_target_pairs={{0,3},{1,2},{2,1},{3,0},{4,7},{5,6},{6,5},{7,4},{8,11},{9,10},{10,... | collective-permute-start | bytes 196616 | tf_op jit(solution)/shard_map/ppermute | solution.py:609
  62.0 1.4 %collective-permute-start.16 = (bf16[512,128]{1,0:T(8,128)(2,1)S(1)}, bf16[512,128]{1,0:T(8,128)(2,1)S(1)}, u32[]{:S(2)}, u32[]{:S(2)}) collective-permute-start(bf16[512,128]{1,0:T(8,128)(2,1)S(1)} %pad_maximum_fusion.1.near), channel_id=1, source_target_pairs={{0,1},{1,0},{2,3},{3,2},{4,5},{5,4},{6,7},{7,6},{8,9},{9,8},{10,11... | collective-permute-start | bytes 393224 | tf_op jit(solution)/shard_map/ppermute | solution.py:609
